TPU v7x, 512 devices: a whole 4x8x8 slice. The times are simulated.
512 devices in a mesh: row: 16 (over z, core), col: 32 (over y, x).
Axes of the slice: x: 4, y: 8, z: 8, core: 2. Of those that a mesh axis runs over, the one named last changes fastest.
Arguments:
- source: bfloat16 [8192, 1024], P(('row', 'col')), may hold values from -6 to 6
- target: bfloat16 [65536, 1024], P(('col', 'row')), may hold values from -16 to 16
- source_mass: float32 [8192], P('row'), may hold values from 0.5 to 2
- target_mass: float32 [65536], P('col'), may hold values from 0.5 to 2
- tile_src: int32 [16, 32, 32], P('row', 'col'), may hold values from 0 to 3, as said below
- tile_dst: int32 [16, 32, 32], P('row', 'col'), may hold values from 0 to 15, as said below
- tile_count: int32 [16, 32], P('row', 'col'), may hold values from 16 to 32, as said below
Outputs:
- source_potential: float32 [8192], P('row')
- target_potential: float32 [65536], P('col')
- mapped: bfloat16 [8192, 1024], P(('row', 'col'))
Inputs may be any that keep to these rules, and one draw needn't show every extreme that they name: Within one grid cell the listed (tile_src, tile_dst) pairs are all different; entries at k >= tile_count are valid cluster numbers but not part of the support. Every source cluster of every grid row and every target cluster of every grid column is live in some grid cell. `tile_dst`: see tile_src. `tile_count`: some grid cell has exactly 32 live tiles in every draw; counts are uneven over cells.
All inputs are finite; a program needn't handle non-finite values.
Results may differ from a plain program's by a relative error of at most 0.0055.
Values may be sent and summed in bfloat16 or wider, within the bound.
No kernel may reach another device: no remote copies, remote signals or barrier semaphores. Data moves between devices by JAX's collectives and lax.ppermute only.
A program may use at most 64 MiB of HBM per device.

v0:
```python
import jax
import jax.numpy as jnp
from jax import lax
from jax.sharding import PartitionSpec as P

BLK = 128
ITERS = 3


EPS = 0.02
FLOOR = -1e30


def tile_costs(src_block, tgt_block, src_norms, tgt_norms, src_idx, tgt_idx, live):
    width = float(src_block.shape[1])
    capacity = src_idx.shape[0]

    def one_tile(k, acc):
        src_start = src_idx[k] * BLK
        tgt_start = tgt_idx[k] * BLK
        rows_s = lax.dynamic_slice_in_dim(src_block, src_start, BLK, 0)
        rows_t = lax.dynamic_slice_in_dim(tgt_block, tgt_start, BLK, 0)
        cross = lax.dot_general(
            rows_s, rows_t, (((1,), (1,)), ((), ())), preferred_element_type=jnp.float32
        )
        norm_s = lax.dynamic_slice_in_dim(src_norms, src_start, BLK, 0)
        norm_t = lax.dynamic_slice_in_dim(tgt_norms, tgt_start, BLK, 0)
        cost = (norm_s[:, None] + norm_t[None, :] - 2.0 * cross) / width
        return lax.dynamic_update_index_in_dim(acc, cost, k, 0)

    return lax.fori_loop(0, live, one_tile, jnp.zeros((capacity, BLK, BLK), jnp.float32))


def partial_lse(logits, own_idx, valid, nblocks):
    tile_max = jnp.where(valid[:, None], jnp.max(logits, axis=2), FLOOR)
    member = (own_idx[:, None] == jnp.arange(nblocks, dtype=jnp.int32)[None, :]) & valid[:, None]
    blk_max = jnp.max(jnp.where(member[:, :, None], tile_max[:, None, :], FLOOR), axis=0)
    shift = jnp.take(blk_max, own_idx, axis=0)
    tile_sum = jnp.where(valid[:, None], jnp.sum(jnp.exp(logits - shift[:, :, None]), axis=2), 0.0)
    blk_sum = jnp.einsum(
        "kn,ki->ni", member.astype(jnp.float32), tile_sum, precision=lax.Precision.HIGHEST
    )
    return (blk_max.reshape(-1), blk_sum.reshape(-1))


def body(source, target, source_mass, target_mass, tile_src, tile_dst, tile_count):
    src_block = lax.all_gather(source, "col", axis=0, tiled=True)
    tgt_block = lax.all_gather(target, "row", axis=0, tiled=True)
    src_idx = tile_src.reshape(-1)
    tgt_idx = tile_dst.reshape(-1)
    live = tile_count.reshape(())
    valid = jnp.arange(src_idx.shape[0], dtype=jnp.int32) < live
    nsrc = src_block.shape[0] // BLK
    ntgt = tgt_block.shape[0] // BLK
    src_norms = jnp.einsum("nd,nd->n", src_block, src_block, preferred_element_type=jnp.float32)
    tgt_norms = jnp.einsum("nd,nd->n", tgt_block, tgt_block, preferred_element_type=jnp.float32)
    log_a = jnp.log(source_mass)
    log_b = jnp.log(target_mass)
    potential_g = jnp.zeros((tgt_block.shape[0],), jnp.float32)
    potential_f = jnp.zeros((src_block.shape[0],), jnp.float32)
    costs = jnp.zeros((src_idx.shape[0], BLK, BLK), jnp.float32)
    for step in range(ITERS):
        costs = tile_costs(src_block, tgt_block, src_norms, tgt_norms, src_idx, tgt_idx, live)
        g_tiles = jnp.take(potential_g.reshape(ntgt, BLK), tgt_idx, axis=0)
        part = partial_lse((g_tiles[:, None, :] - costs) / EPS, src_idx, valid, nsrc)
        big = lax.pmax(part[0], "col")
        total = lax.psum(part[1] * jnp.exp(part[0] - big), "col")
        potential_f = EPS * log_a - EPS * (big + jnp.log(total))
        f_tiles = jnp.take(potential_f.reshape(nsrc, BLK), src_idx, axis=0)
        logits = jnp.swapaxes((f_tiles[:, :, None] - costs) / EPS, 1, 2)
        part = partial_lse(logits, tgt_idx, valid, ntgt)
        big = lax.pmax(part[0], "row")
        total = lax.psum(part[1] * jnp.exp(part[0] - big), "row")
        potential_g = EPS * log_b - EPS * (big + jnp.log(total))
    f_tiles = jnp.take(potential_f.reshape(nsrc, BLK), src_idx, axis=0)
    g_tiles = jnp.take(potential_g.reshape(ntgt, BLK), tgt_idx, axis=0)
    weights = jnp.where(
        valid[:, None, None],
        jnp.exp((f_tiles[:, :, None] + g_tiles[:, None, :] - costs) / EPS),
        0.0,
    )
    member = (
        (src_idx[:, None] == jnp.arange(nsrc, dtype=jnp.int32)[None, :]) & valid[:, None]
    ).astype(jnp.float32)
    low = weights.astype(jnp.bfloat16)
    row_mass = jnp.sum(low, axis=2, dtype=jnp.float32)
    denom = jnp.einsum("kn,ki->ni", member, row_mass, precision=lax.Precision.HIGHEST).reshape(-1)

    def add_tile(k, acc):
        rows_t = lax.dynamic_slice_in_dim(tgt_block, tgt_idx[k] * BLK, BLK, 0)
        product = jnp.dot(low[k], rows_t, preferred_element_type=jnp.float32)
        src_start = src_idx[k] * BLK
        current = lax.dynamic_slice_in_dim(acc, src_start, BLK, 0)
        return lax.dynamic_update_slice_in_dim(acc, current + product, src_start, 0)

    numer = lax.fori_loop(
        0, live, add_tile, jnp.zeros((src_block.shape[0], src_block.shape[1]), jnp.float32)
    )
    numer_all, denom_all = lax.psum((numer, denom), "col")
    share = numer.shape[0] // lax.axis_size("col")
    offset = lax.axis_index("col") * share
    numer_mine = lax.dynamic_slice_in_dim(numer_all, offset, share, 0)
    denom_mine = lax.dynamic_slice_in_dim(denom_all, offset, share, 0)
    mapped = (numer_mine / denom_mine[:, None]).astype(jnp.bfloat16)
    return (potential_f, potential_g, mapped)


def solution(mesh):
    in_specs = (
        P(("row", "col"), None),
        P(("col", "row"), None),
        P("row"),
        P("col"),
        P("row", "col", None),
        P("row", "col", None),
        P("row", "col"),
    )
    out_specs = (P("row"), P("col"), P(("row", "col"), None))
    return jax.shard_map(body, mesh=mesh, in_specs=in_specs, out_specs=out_specs, check_vma=False)
```

profile of v0, /device:TPU:1, one launch (start us, length us, event | category | flops | bytes accessed | tf_op | source)
XLA Modules:
  0.0 1189.3 jit_solution(572187132392675397)
XLA Ops:
  14.1 79.7 %all-gather.3.cloned.1.call-done = bf16[512,1024]{1,0:T(8,128)(2,1)} async-done(((bf16[16,1024]{1,0:T(8,128)(2,1)}), bf16[512,1024]{1,0:T(8,128)(2,1)}) %all-gather.3.cloned.1.call-update) | async-done | bytes 1048592 | tf_op jit(solution)/shard_map/all_gather | solution.py:47
  93.7 1.5 fusion.19
  95.2 49.1 %all-gather.5.cloned.1.call-done = bf16[2048,1024]{1,0:T(8,128)(2,1)} async-done(((bf16[128,1024]{1,0:T(8,128)(2,1)}), bf16[2048,1024]{1,0:T(8,128)(2,1)}) %all-gather.5.cloned.1.call-update) | async-done | bytes 4194320 | tf_op jit(solution)/shard_map/all_gather | solution.py:48
  144.4 3.1 fusion.12
  148.1 119.6 %while.4 = (s32[]{:T(128)}, f32[32,128,128]{2,1,0:T(8,128)S(1)}, s32[]{:T(128)}, s32[32]{0:T(128)S(1)}, f32[512]{0:T(512)S(1)}, /*index=5*/s32[32]{0:T(128)S(1)}...) while((s32[]{:T(128)}, f32[32,128,128]{2,1,0:T(8,128)S(1)}, ...), condition=%wide.region_1.0_spmd, body=%wide.region_0.0_spmd.sunk | while | flops 33619980 | bytes 593207 | solution.py:31
  151.4 1.3 fusion.71
  156.0 1.3 fusion.71
  165.1 1.3 fusion.71
  192.6 1.3 fusion.71
  224.6 1.3 fusion.71
  256.6 1.3 fusion.71
  269.2 1.3 exponential_reduce_fusion.2
  270.5 78.6 %pmax.42 = f32[512]{0:T(512)S(1)} all-reduce(f32[512]{0:T(512)S(1)} %bitcast.107), channel_id=1, replica_groups=mesh['row'=16,'col'=32] {'col'}, use_global_device_ids=true, to_apply=%region_4.6 | all-reduce | flops 512 | bytes 4096 | tf_op jit(solution)/shard_map/pmax | solution.py:66
  349.2 57.8 %psum.56 = f32[512]{0:T(512)S(1)} all-reduce(f32[512]{0:T(512)S(1)} %fusion.28), channel_id=1, replica_groups=mesh['row'=16,'col'=32] {'col'}, use_global_device_ids=true, to_apply=%region_6.9 | all-reduce | flops 512 | bytes 4096 | tf_op jit(solution)/shard_map/psum | solution.py:67
  410.0 57.6 %pmax.43 = f32[2048]{0:T(1024)S(1)} all-reduce(f32[2048]{0:T(1024)S(1)} %bitcast.111), channel_id=1, replica_groups=mesh['row'=16,'col'=32] {'row'}, use_global_device_ids=true, to_apply=%region_9.12 | all-reduce | flops 2048 | bytes 16384 | tf_op jit(solution)/shard_map/pmax | solution.py:72
  467.9 23.5 %psum.57 = f32[2048]{0:T(1024)S(1)} all-reduce(f32[2048]{0:T(1024)S(1)} %fusion.25), channel_id=1, replica_groups=mesh['row'=16,'col'=32] {'row'}, use_global_device_ids=true, to_apply=%region_11.14 | all-reduce | flops 2048 | bytes 16384 | tf_op jit(solution)/shard_map/psum | solution.py:73
  493.5 1.3 exponential_reduce_fusion.1
  494.8 57.7 %pmax.44 = f32[512]{0:T(512)S(1)} all-reduce(f32[512]{0:T(512)S(1)} %bitcast.108), channel_id=1, replica_groups=mesh['row'=16,'col'=32] {'col'}, use_global_device_ids=true, to_apply=%region_14.17 | all-reduce | flops 512 | bytes 4096 | tf_op jit(solution)/shard_map/pmax | solution.py:66
  552.7 56.3 %psum.58 = f32[512]{0:T(512)S(1)} all-reduce(f32[512]{0:T(512)S(1)} %fusion.27), channel_id=1, replica_groups=mesh['row'=16,'col'=32] {'col'}, use_global_device_ids=true, to_apply=%region_16.19 | all-reduce | flops 512 | bytes 4096 | tf_op jit(solution)/shard_map/psum | solution.py:67
  611.9 51.8 %pmax.45 = f32[2048]{0:T(1024)S(1)} all-reduce(f32[2048]{0:T(1024)S(1)} %bitcast.112), channel_id=1, replica_groups=mesh['row'=16,'col'=32] {'row'}, use_global_device_ids=true, to_apply=%region_19.22 | all-reduce | flops 2048 | bytes 16384 | tf_op jit(solution)/shard_map/pmax | solution.py:72
  663.9 24.0 %psum.59 = f32[2048]{0:T(1024)S(1)} all-reduce(f32[2048]{0:T(1024)S(1)} %fusion.24), channel_id=1, replica_groups=mesh['row'=16,'col'=32] {'row'}, use_global_device_ids=true, to_apply=%region_21.24 | all-reduce | flops 2048 | bytes 16384 | tf_op jit(solution)/shard_map/psum | solution.py:73
  690.1 1.3 exponential_reduce_fusion
  691.4 57.4 %pmax.46 = f32[512]{0:T(512)S(1)} all-reduce(f32[512]{0:T(512)S(1)} %bitcast.109), channel_id=1, replica_groups=mesh['row'=16,'col'=32] {'col'}, use_global_device_ids=true, to_apply=%region_24.27 | all-reduce | flops 512 | bytes 4096 | tf_op jit(solution)/shard_map/pmax | solution.py:66
  749.1 56.1 %psum.60 = f32[512]{0:T(512)S(1)} all-reduce(f32[512]{0:T(512)S(1)} %fusion.26), channel_id=1, replica_groups=mesh['row'=16,'col'=32] {'col'}, use_global_device_ids=true, to_apply=%region_26.29 | all-reduce | flops 512 | bytes 4096 | tf_op jit(solution)/shard_map/psum | solution.py:67
  808.2 51.8 %pmax.47 = f32[2048]{0:T(1024)S(1)} all-reduce(f32[2048]{0:T(1024)S(1)} %bitcast.113), channel_id=1, replica_groups=mesh['row'=16,'col'=32] {'row'}, use_global_device_ids=true, to_apply=%region_29.32 | all-reduce | flops 2048 | bytes 16384 | tf_op jit(solution)/shard_map/pmax | solution.py:72
  860.2 24.0 %psum.61 = f32[2048]{0:T(1024)S(1)} all-reduce(f32[2048]{0:T(1024)S(1)} %fusion.23), channel_id=1, replica_groups=mesh['row'=16,'col'=32] {'row'}, use_global_device_ids=true, to_apply=%region_31.34 | all-reduce | flops 2048 | bytes 16384 | tf_op jit(solution)/shard_map/psum | solution.py:73
  884.9 1.4 convert_reduce_fusion
  886.6 112.3 %while.5 = (s32[]{:T(128)}, f32[512,1024]{1,0:T(8,128)S(1)}, s32[]{:T(128)}, s32[32]{0:T(128)S(1)}, bf16[32,128,128]{2,1,0:T(8,128)(2,1)S(1)}, /*index=5*/s32[32...) while((s32[]{:T(128)}, f32[512,1024]{1,0:T(8,128)S(1)}, ...), condition=%wide.region_33.36_spmd, body=%wide.region_32.35_spmd.sunk | while | flops 33685516 | bytes 1343775 | solution.py:96
  999.0 1.3 copy-done
  1000.4 70.5 %psum.63 = f32[512]{0:T(512)S(1)} all-reduce(f32[512]{0:T(512)S(1)} %convolution_bitcast_fusion.3), channel_id=1, replica_groups=mesh['row'=16,'col'=32] {'col'}, use_global_device_ids=true, to_apply=%region_36.39 | all-reduce | flops 512 | bytes 4096 | tf_op jit(solution)/shard_map/psum | solution.py:99
  1071.0 110.2 %all-reduce.2.cloned.1.call-done = f32[512,1024]{1,0:T(8,128)} async-done(((f32[512,1024]{1,0:T(8,128)}), f32[512,1024]{1,0:T(8,128)}) %all-reduce.2.cloned.1.call-update) | async-done | bytes 2097168 | tf_op jit(solution)/shard_map/psum | solution.py:99
  1181.2 1.5 divide_convert_fusion
  (294 shorter events, 145.0 us)
Async XLA Ops:
  7.2 86.6 %all-gather.3.cloned.1.call-start = ((), (), s32[]{:S(2)}) async-start(), calls=%async_computation | async-start | bytes 1081344 | tf_op jit(solution)/shard_map/all_gather | solution.py:47
  7.9 136.5 %all-gather.5.cloned.1.call-start = ((), (), s32[]{:S(2)}) async-start(), calls=%async_computation.1 | async-start | bytes 4456448 | tf_op jit(solution)/shard_map/all_gather | solution.py:48
  8.6 1172.6 %all-reduce.2.cloned.1.call-start = ((), (), s32[]{:S(2)}) async-start(), calls=%async_computation.2 | async-start | bytes 4194304 | tf_op jit(solution)/shard_map/psum | solution.py:99
  147.4 0.7 copy-start.5
  147.5 0.7 copy-start.6
  267.7 139.3 %copy-start.4 = (f32[512]{0:T(512)S(1)}, f32[512]{0:T(512)}, u32[]{:S(2)}) copy-start(f32[512]{0:T(512)} %param.17) | copy-start | bytes 6148
  407.7 83.7 %copy-start.3 = (f32[2048]{0:T(1024)S(1)}, f32[2048]{0:T(1024)}, u32[]{:S(2)}) copy-start(f32[2048]{0:T(1024)} %param.18) | copy-start | bytes 24580
  805.2 3.0 copy-start.1
  884.3 2.4 copy-start.2
  999.0 1.3 copy-start
Sparse Core Ops, SparseCore 0:
  11.2 82.5 all-gather.2
  95.8 48.4 all-gather.4
  1000.4 180.7 all-reduce.1
where the time goes:
time: 1200 us; the launch traced here: 1190 us
  blocking collectives  667 us (56%)
  waiting for transfers between devices  240 us (20%)
  loops' own time  103 us (9%)
  local copies, waits for them, and re-layouts  75.2 us (6%)
  matrix products  64.8 us (5%)
  other arithmetic  23.8 us (2%)
  between operations  14.7 us (1%)
    pmax x3, blocking collectives, body(): big = lax.pmax(part[0], 'col')  194 us
    psum x3, blocking collectives, body(): total = lax.psum(part[1] * jnp.exp(part[0] - big), 'col')  170 us
    pmax x3, blocking collectives, body(): big = lax.pmax(part[0], 'row')  161 us
    psum x1, waiting for transfers between devices, body(): numer_all, denom_all = lax.psum((numer, denom), 'col')  110 us
    all_gather x1, waiting for transfers between devices, body(): src_block = lax.all_gather(source, 'col', axis=0, tiled=True)  79.7 us
    psum x3, blocking collectives, body(): total = lax.psum(part[1] * jnp.exp(part[0] - big), 'row')  71.6 us
    psum x1, blocking collectives, body(): numer_all, denom_all = lax.psum((numer, denom), 'col')  70.5 us
    another operation x1, loops' own time, tile_costs(): lax.fori_loop(0, live, one_tile, jnp.zeros((capacity, BLK, BLK), jnp.floa...  52.4 us
  transfers between devices with their start and end apart: 3, of which 3 were waited for; matrix products, arithmetic and copies ran while one was open for 1% of the time, Pallas kernels for 0%

commit v1 on v0

v1 whole, which is shorter than its diff:
```python
import math

import jax
import jax.numpy as jnp
from jax import lax
from jax.experimental import pallas as pl
from jax.experimental.pallas import tpu as pltpu
from jax.sharding import PartitionSpec as P

BLK = 128
ITERS = 3
EPS = 0.02
UNIT = EPS * math.log(2.0)
FAR = 1e30
MIB = 1 << 20


def nt_dot(a, b):
    return lax.dot_general(a, b, (((1,), (1,)), ((), ())), preferred_element_type=jnp.float32)


def lanes_of(row):
    return jnp.transpose(jnp.broadcast_to(row, (BLK, BLK)))


def finish_rows(peak, total):
    peak, total = jnp.transpose(peak), jnp.transpose(total)
    top = jnp.max(peak, axis=0, keepdims=True)
    return top + jnp.log2(jnp.sum(total * jnp.exp2(peak - top), axis=0, keepdims=True))


def put_copies(out_ref, row_at, row):
    copies = out_ref.shape[0]
    for k in range(copies):
        out_ref[k, pl.ds(row_at, 1), :] = row


def cost_kernel(sidx, tidx, live, src_ref, tgt_ref, cost_ref, part_ref, far, snorm, peak, total):
    step = pl.program_id(0)
    nsrc = src_ref.shape[0] // BLK
    per = tgt_ref.shape[0] // BLK
    width = src_ref.shape[1]
    scale = 1.0 / (width * UNIT)

    @pl.when(step == 0)
    def _():
        for i in range(far.shape[0]):
            far[i] = FAR

        def mark(k, c):
            far[sidx[k] * (far.shape[0] // nsrc) + tidx[k]] = 0.0
            return c

        lax.fori_loop(0, live[0], mark, 0)
        for s in range(nsrc):
            rows = src_ref[s * BLK : (s + 1) * BLK, :].astype(jnp.float32)
            norm = jnp.sum(rows * rows, axis=1, keepdims=True) * scale
            snorm[s * BLK : (s + 1) * BLK, :] = jnp.broadcast_to(norm, (BLK, BLK))
        peak[...] = jnp.full_like(peak, -FAR)
        total[...] = jnp.zeros_like(total)

    rows = tgt_ref[...].astype(jnp.float32)
    square = rows * rows
    high = square.astype(jnp.bfloat16)
    low = (square - high.astype(jnp.float32)).astype(jnp.bfloat16)
    ones = jnp.ones((8, width), jnp.bfloat16)
    tnorm = (nt_dot(ones, high) + nt_dot(ones, low))[0:1, :] * scale
    nall = far.shape[0] // nsrc
    for s in range(nsrc):
        at = slice(s * BLK, (s + 1) * BLK)
        cross = nt_dot(src_ref[at, :], tgt_ref[...]) * (-2.0 * scale)
        tiles = []
        for t in range(per):
            lanes = slice(t * BLK, (t + 1) * BLK)
            away = tnorm[:, lanes] + far[s * nall + step * per + t]
            tile = cross[:, lanes] + snorm[at, :] + away
            cost_ref[at, lanes] = tile
            tiles.append(tile)
        old = peak[at, :]
        new = old
        for tile in tiles:
            new = jnp.maximum(new, -tile)
        acc = total[at, :] * jnp.exp2(old - new)
        for tile in tiles:
            acc = acc + jnp.exp2(-tile - new)
        peak[at, :] = new
        total[at, :] = acc

    @pl.when(step == pl.num_programs(0) - 1)
    def _():
        for s in range(nsrc):
            at = slice(s * BLK, (s + 1) * BLK)
            put_copies(part_ref, s, finish_rows(peak[at, :], total[at, :]))


def combine(log_mass, parts_ref):
    parts = parts_ref[...]
    top = jnp.max(parts, axis=0)
    return log_mass - (top + jnp.log2(jnp.sum(jnp.exp2(parts - top[None]), axis=0)))


def target_kernel(parts_ref, mass_ref, cost_ref, pot_ref, part_ref, wide):
    pot = combine(jnp.log2(mass_ref[...]), parts_ref)
    pot_ref[...] = pot
    nsrc, ntgt = pot.shape[0], cost_ref.shape[1] // BLK
    for s in range(nsrc):
        wide[s * BLK : (s + 1) * BLK, :] = lanes_of(pot[s : s + 1, :])
    for t in range(ntgt):
        lanes = slice(t * BLK, (t + 1) * BLK)
        gap = (wide[...] - cost_ref[:, lanes]).reshape(-1, 8, BLK)
        peak = jnp.max(gap, axis=0)
        top = jnp.max(peak, axis=0, keepdims=True)
        total = jnp.sum(jnp.exp2(gap - top[None]), axis=0)
        row = top + jnp.log2(jnp.sum(total, axis=0, keepdims=True))
        put_copies(part_ref, t, row)


def source_kernel(parts_ref, mass_ref, cost_ref, part_ref):
    pot = combine(jnp.log2(mass_ref[...]), parts_ref)
    ntgt, nsrc = pot.shape[0], cost_ref.shape[0] // BLK
    for s in range(nsrc):
        at = slice(s * BLK, (s + 1) * BLK)

        def gap(t):
            return pot[t : t + 1, :] - cost_ref[at, t * BLK : (t + 1) * BLK]

        peak = gap(0)
        for t in range(1, ntgt):
            peak = jnp.maximum(peak, gap(t))
        total = jnp.exp2(gap(0) - peak)
        for t in range(1, ntgt):
            total = total + jnp.exp2(gap(t) - peak)
        put_copies(part_ref, s, finish_rows(peak, total))


def map_kernel(parts_ref, mass_ref, fpot_ref, cost_ref, tgt_ref, pot_ref, sums_ref, weight):
    pot = combine(jnp.log2(mass_ref[...]), parts_ref)
    pot_ref[...] = pot
    ntgt, nsrc = pot.shape[0], cost_ref.shape[0] // BLK
    width = tgt_ref.shape[1]
    for s in range(nsrc):
        at = slice(s * BLK, (s + 1) * BLK)
        mine = lanes_of(fpot_ref[s : s + 1, :])
        for t in range(ntgt):
            lanes = slice(t * BLK, (t + 1) * BLK)
            power = jnp.exp2(mine + pot[t : t + 1, :] - cost_ref[at, lanes])
            weight[at, lanes] = power.astype(jnp.bfloat16)
    low = weight[...]
    for d in range(0, width, 256):
        part = jnp.dot(low, tgt_ref[:, d : d + 256], preferred_element_type=jnp.float32)
        sums_ref[:, d : d + 256] = part.astype(jnp.bfloat16)
    total = jnp.dot(low, jnp.ones((low.shape[1], BLK), jnp.bfloat16), preferred_element_type=jnp.float32)
    high = total.astype(jnp.bfloat16).astype(jnp.float32)
    lane = lax.broadcasted_iota(jnp.int32, total.shape, 1)
    sums_ref[:, width:] = jnp.where(lane == 0, high, total - high).astype(jnp.bfloat16)


def divide_kernel(sums_ref, out_ref):
    width = out_ref.shape[1]
    sums = sums_ref[0].astype(jnp.float32)
    for k in range(1, sums_ref.shape[0]):
        sums = sums + sums_ref[k].astype(jnp.float32)
    total = sums[:, width : width + 1] + sums[:, width + 1 : width + 2]
    out_ref[...] = (sums[:, :width] / total).astype(out_ref.dtype)


def whole(n):
    return [pl.BlockSpec(memory_space=pltpu.VMEM)] * n


def call(kernel, shapes, scratch, args, limit, flops=0):
    return pl.pallas_call(
        kernel,
        out_shape=shapes,
        in_specs=whole(len(args)),
        out_specs=jax.tree.map(lambda _: pl.BlockSpec(memory_space=pltpu.VMEM), shapes),
        scratch_shapes=scratch,
        compiler_params=pltpu.CompilerParams(vmem_limit_bytes=limit * MIB),
    )(*args)


def shape(*dims, dtype=jnp.float32):
    return jax.ShapeDtypeStruct(dims, dtype)


def spread(x, axis):
    return lax.all_to_all(x, axis, 0, 0, tiled=True)


def body(source, target, source_mass, target_mass, tile_src, tile_dst, tile_count):
    rows, cols = lax.axis_size("row"), lax.axis_size("col")
    width = source.shape[1]
    tgt = lax.all_gather(target, "row", axis=0, tiled=True)
    src = spread(jnp.broadcast_to(source[None], (cols, *source.shape)), "col")
    src = src.reshape(-1, width)
    nsrc, ntgt = src.shape[0] // BLK, tgt.shape[0] // BLK
    amass = source_mass.reshape(nsrc, BLK)
    bmass = target_mass.reshape(ntgt, BLK)

    per = 2
    cost, part = pl.pallas_call(
        cost_kernel,
        out_shape=(shape(src.shape[0], tgt.shape[0]), shape(cols, nsrc, BLK)),
        grid_spec=pltpu.PrefetchScalarGridSpec(
            num_scalar_prefetch=3,
            grid=(ntgt // per,),
            in_specs=[
                pl.BlockSpec(src.shape, lambda t, *_: (0, 0)),
                pl.BlockSpec((per * BLK, width), lambda t, *_: (t, 0)),
            ],
            out_specs=(
                pl.BlockSpec((src.shape[0], per * BLK), lambda t, *_: (0, t)),
                pl.BlockSpec((cols, nsrc, BLK), lambda t, *_: (0, 0, 0)),
            ),
            scratch_shapes=[
                pltpu.SMEM((nsrc * ntgt,), jnp.float32),
                pltpu.VMEM((src.shape[0], BLK), jnp.float32),
                pltpu.VMEM((src.shape[0], BLK), jnp.float32),
                pltpu.VMEM((src.shape[0], BLK), jnp.float32),
            ],
        ),
        compiler_params=pltpu.CompilerParams(vmem_limit_bytes=24 * MIB),
    )(tile_src.reshape(-1), tile_dst.reshape(-1), tile_count.reshape(-1), src, tgt)

    for step in range(ITERS):
        fpot, part = call(
            target_kernel,
            (shape(nsrc, BLK), shape(rows, ntgt, BLK)),
            [pltpu.VMEM((src.shape[0], BLK), jnp.float32)],
            (spread(part, "col"), amass, cost),
            16,
        )
        parts = spread(part, "row")
        if step < ITERS - 1:
            part = call(source_kernel, shape(cols, nsrc, BLK), [], (parts, bmass, cost), 16)
    gpot, sums = call(
        map_kernel,
        (shape(ntgt, BLK), shape(src.shape[0], width + BLK, dtype=jnp.bfloat16)),
        [pltpu.VMEM(cost.shape, jnp.bfloat16)],
        (parts, bmass, fpot, cost, tgt),
        32,
    )
    share = src.shape[0] // cols
    sums = spread(sums.reshape(cols, share, width + BLK), "col")
    mapped = call(divide_kernel, shape(share, width, dtype=jnp.bfloat16), [], (sums,), 8)
    return (fpot.reshape(-1) * UNIT, gpot.reshape(-1) * UNIT, mapped)


def solution(mesh):
    in_specs = (
        P(("row", "col"), None),
        P(("col", "row"), None),
        P("row"),
        P("col"),
        P("row", "col", None),
        P("row", "col", None),
        P("row", "col"),
    )
    out_specs = (P("row"), P("col"), P(("row", "col"), None))
    return jax.shard_map(body, mesh=mesh, in_specs=in_specs, out_specs=out_specs, check_vma=False)
```

time: 1200 us -> 211 us (0.18)
  blocking collectives: 667 us -> 82.5 us
  waiting for transfers between devices: 240 us -> 71.2 us
  loops' own time: 103 us -> 0 us
  local copies, waits for them, and re-layouts: 75.2 us -> 5.38 us
  matrix products: 64.8 us -> 0 us
  other arithmetic: 23.8 us -> 1.18 us
  Pallas kernels: 0 us -> 21.1 us
  starting transfers between devices: 0.11 us -> 14.5 us
    pmax x6 -> x0, blocking collectives: 355 us -> none  [the longest x3 194 us: body(): big = lax.pmax(part[0], 'col')]
    psum x7 -> x0, blocking collectives: 312 us -> none  [the longest x3 170 us: body(): total = lax.psum(part[1] * jnp.exp(part[0] - big), 'col')]
    all_gather x2 -> x1, waiting for transfers between devices: 129 us -> 15.2 us  [body(): tgt = lax.all_gather(target, 'row', axis=0, tiled=True)]
    psum x1 -> x0, waiting for transfers between devices: 110 us -> none  [body(): numer_all, denom_all = lax.psum((numer, denom), 'col')]
    another operation x2 -> x0, loops' own time: 103 us -> none  [the longest x1 52.4 us: tile_costs(): lax.fori_loop(0, live, one_tile, jnp.zeros((capacity, BLK, BLK), jnp.floa...]
    all_to_all x0 -> x6, blocking collectives: none -> 82.5 us  [spread(): return lax.all_to_all(x, axis, 0, 0, tiled=True)]
    dynamic_slice x157 -> x0, local copies, waits for them, and re-layouts: 65.5 us -> none  [the longest x26 15.5 us: add_tile(): src_start = src_idx[k] * BLK]
    dot_general x59 -> x0, matrix products: 64.8 us -> none  [the longest x26 32.8 us: one_tile(): lax.dot_general(rows_s, rows_t, (((1,), (1,)), ((), ())), preferred_eleme...]
where the time goes in v1:
time: 211 us
  blocking collectives  82.5 us (39%)
  waiting for transfers between devices  71.2 us (34%)
  Pallas kernels  21.1 us (10%)
  between operations  14.7 us (7%)
  starting transfers between devices  14.5 us (7%)
  local copies, waits for them, and re-layouts  5.38 us (3%)
    all_to_all x6, blocking collectives, spread(): return lax.all_to_all(x, axis, 0, 0, tiled=True)  82.5 us
    all_to_all x2, waiting for transfers between devices, spread(): return lax.all_to_all(x, axis, 0, 0, tiled=True)  55.3 us
    all_gather x1, waiting for transfers between devices, body(): tgt = lax.all_gather(target, 'row', axis=0, tiled=True)  15.2 us
    all_to_all x2, starting transfers between devices, spread(): return lax.all_to_all(x, axis, 0, 0, tiled=True)  14.4 us
    pallas_call x1, Pallas kernels, body(): pl.pallas_call(cost_kernel, out_shape=(shape(src.shape[0], tgt.shape[0]),...  11.1 us
    pallas_call x7, Pallas kernels, call(): pl.pallas_call(kernel, out_shape=shapes, in_specs=whole(len(args)), out_s...  10.1 us
  transfers between devices with their start and end apart: 3, of which 3 were waited for; matrix products, arithmetic and copies ran while one was open for 1% of the time, Pallas kernels for 0%

profile of v1, /device:TPU:1, one launch (start us, length us, event | category | flops | bytes accessed | tf_op | source)
XLA Modules:
  0.0 210.6 jit_solution(16748079828356362670)
XLA Ops:
  7.2 0.0 all-gather.2.cloned.1.call-start
  7.2 0.7 all-gather.2.cloned.1.call-update
  7.9 0.0 copy-start.3
  7.9 1.9 broadcast_in_dim.2
  9.8 10.5 %all-to-all-start = ((bf16[32,16,1024]{2,1,0:T(8,128)(2,1)}), bf16[32,16,1024]{2,1,0:T(8,128)(2,1)S(1)}, u32[]{:S(2)}, u32[]{:S(2)}) async-start(bf16[32,16,1024]{2,1,0:T(8,128)(2,1)} %broadcast_in_dim.2), calls=%async_computation | async-start | bytes 2097152 | tf_op jit(solution)/shard_map/all_to_all | solution.py:187
  20.9 25.6 %all-to-all-done = bf16[32,16,1024]{2,1,0:T(8,128)(2,1)S(1)} async-done(((bf16[32,16,1024]{2,1,0:T(8,128)(2,1)}), bf16[32,16,1024]{2,1,0:T(8,128)(2,1)S(1)}, u32[]{:S(2)}, u32[]{:S(2)}) %all-to-all-start) | async-done | bytes 1048608 | tf_op jit(solution)/shard_map/all_to_all | solution.py:187
  46.5 15.2 %all-gather.2.cloned.1.call-done.tgt_ref = bf16[2048,1024]{1,0:T(8,128)(2,1)} async-done(((bf16[128,1024]{1,0:T(8,128)(2,1)}), bf16[2048,1024]{1,0:T(8,128)(2,1)}) %all-gather.2.cloned.1.call-update) | async-done | bytes 4194320 | tf_op jit(solution)/shard_map/all_gather | solution.py:193
  61.7 0.0 copy-start
  61.7 2.2 %copy-done = bf16[2048,1024]{1,0:T(8,128)(2,1)S(1)} copy-done((bf16[2048,1024]{1,0:T(8,128)(2,1)S(1)}, bf16[2048,1024]{1,0:T(8,128)(2,1)}, u32[]{:S(2)}) %copy-start) | copy-done | bytes 4194328
  63.9 0.7 copy-done.4
  64.6 0.7 copy-done.5
  65.2 11.1 %shard_map.94 = (f32[512,2048]{1,0:T(8,128)S(1)}, f32[32,4,128]{2,1,0:T(4,128)S(1)}) custom-call(s32[32]{0:T(128)S(1)} %bitcast.19, s32[32]{0:T(128)S(1)} %bitcast.20, s32[1]{0:T(128)} %bitcast.11.live, bf16[512,1024]{1,0:T(8,128)(2,1)S(1)} %bitcast.12, bf16[2048,1024]{1,0:T(8,128)(2,1)S(1)} %copy-done), custom_call_target="tpu_custom_call" | custom-call | tf_op jit(solution)/shard_map/pallas_call | solution.py:201
  76.3 17.9 %all_to_all.40.parts_ref = f32[32,4,128]{2,1,0:T(4,128)S(1)} all-to-all(f32[32,4,128]{2,1,0:T(4,128)S(1)} %get-tuple-element.11), channel_id=1, replica_groups=mesh['row'=16,'col'=32] {'col'}, dimensions={0} | all-to-all | bytes 131072 | tf_op jit(solution)/shard_map/all_to_all | solution.py:187
  94.3 0.0 copy-done.3
  94.3 1.0 shard_map.95
  95.2 14.7 %all_to_all.41.parts_ref = f32[16,16,128]{2,1,0:T(8,128)S(1)} all-to-all(f32[16,16,128]{2,1,0:T(8,128)S(1)} %get-tuple-element.13), channel_id=1, replica_groups=mesh['row'=16,'col'=32] {'row'}, dimensions={0} | all-to-all | bytes 262144 | tf_op jit(solution)/shard_map/all_to_all | solution.py:187
  110.0 0.0 copy-done.2
  110.0 1.0 shard_map.96
  110.9 12.3 %all_to_all.42.parts_ref = f32[32,4,128]{2,1,0:T(4,128)S(1)} all-to-all(f32[32,4,128]{2,1,0:T(4,128)S(1)} %shard_map.96), channel_id=1, replica_groups=mesh['row'=16,'col'=32] {'col'}, dimensions={0} | all-to-all | bytes 131072 | tf_op jit(solution)/shard_map/all_to_all | solution.py:187
  123.2 1.0 shard_map.97
  124.2 12.5 %all_to_all.43.parts_ref = f32[16,16,128]{2,1,0:T(8,128)S(1)} all-to-all(f32[16,16,128]{2,1,0:T(8,128)S(1)} %get-tuple-element.14), channel_id=1, replica_groups=mesh['row'=16,'col'=32] {'row'}, dimensions={0} | all-to-all | bytes 262144 | tf_op jit(solution)/shard_map/all_to_all | solution.py:187
  136.8 1.0 shard_map.98
  137.7 12.4 %all_to_all.44.parts_ref = f32[32,4,128]{2,1,0:T(4,128)S(1)} all-to-all(f32[32,4,128]{2,1,0:T(4,128)S(1)} %shard_map.98), channel_id=1, replica_groups=mesh['row'=16,'col'=32] {'col'}, dimensions={0} | all-to-all | bytes 131072 | tf_op jit(solution)/shard_map/all_to_all | solution.py:187
  150.1 1.0 shard_map.99
  151.1 12.5 %all_to_all.45.parts_ref = f32[16,16,128]{2,1,0:T(8,128)S(1)} all-to-all(f32[16,16,128]{2,1,0:T(8,128)S(1)} %get-tuple-element.16), channel_id=1, replica_groups=mesh['row'=16,'col'=32] {'row'}, dimensions={0} | all-to-all | bytes 262144 | tf_op jit(solution)/shard_map/all_to_all | solution.py:187
  163.7 0.0 copy-done.1
  163.7 4.4 %shard_map.100 = (f32[16,128]{1,0:T(8,128)S(1)}, bf16[512,1152]{1,0:T(8,128)(2,1)}) custom-call(f32[16,16,128]{2,1,0:T(8,128)S(1)} %all_to_all.45.parts_ref, f32[16,128]{1,0:T(8,128)S(1)} %bitcast.15, f32[4,128]{1,0:T(4,128)S(1)} %get-tuple-element.15.fpot_ref, f32[512,2048]{1,0:T(8,128)S(1)} %get-tuple-element.12.cost_ref, bf16[2048,1024]{1,0:T(8,128)(2,1)S(1)} %copy-done.1), custom_call_target="tpu_custom_call" | custom-call | tf_op jit(solution)/shard_map/pallas_call | solution.py:172
  168.1 3.9 %all-to-all-start.7 = ((bf16[32,16,1152]{2,1,0:T(8,128)(2,1)}), bf16[32,16,1152]{2,1,0:T(8,128)(2,1)S(1)}, u32[]{:S(2)}, u32[]{:S(2)}) async-start(bf16[32,16,1152]{2,1,0:T(8,128)(2,1)} %bitcast.8), calls=%async_computation.7 | async-start | bytes 2359296 | tf_op jit(solution)/shard_map/all_to_all | solution.py:187
  172.0 0.6 multiply_bitcast_fusion.1
  172.6 0.6 multiply_bitcast_fusion
  173.2 29.7 %all-to-all-done.7.sums_ref = bf16[32,16,1152]{2,1,0:T(8,128)(2,1)S(1)} async-done(((bf16[32,16,1152]{2,1,0:T(8,128)(2,1)}), bf16[32,16,1152]{2,1,0:T(8,128)(2,1)S(1)}, u32[]{:S(2)}, u32[]{:S(2)}) %all-to-all-start.7) | async-done | bytes 1179680 | tf_op jit(solution)/shard_map/all_to_all | solution.py:187
  202.9 0.8 shard_map.101
  (4 shorter events, 0.0 us)
Async XLA Ops:
  7.2 54.6 %all-gather.2.cloned.1.call-start = ((), (), s32[]{:S(2)}) async-start(), calls=%async_computation.8 | async-start | bytes 4456448 | tf_op jit(solution)/shard_map/all_gather | solution.py:193
  7.9 86.4 %copy-start.3 = (f32[512]{0:T(512)S(1)}, f32[512]{0:T(512)}, u32[]{:S(2)}) copy-start(f32[512]{0:T(512)} %param.9) | copy-start | bytes 6148
  9.8 36.7 %all-to-all-start = ((bf16[32,16,1024]{2,1,0:T(8,128)(2,1)}), bf16[32,16,1024]{2,1,0:T(8,128)(2,1)S(1)}, u32[]{:S(2)}, u32[]{:S(2)}) async-start(bf16[32,16,1024]{2,1,0:T(8,128)(2,1)} %broadcast_in_dim.2), calls=%async_computation | async-start | bytes 2097152 | tf_op jit(solution)/shard_map/all_to_all | solution.py:187
  61.7 2.2 %copy-start = (bf16[2048,1024]{1,0:T(8,128)(2,1)S(1)}, bf16[2048,1024]{1,0:T(8,128)(2,1)}, u32[]{:S(2)}) copy-start(bf16[2048,1024]{1,0:T(8,128)(2,1)} %all-gather.2.cloned.1.call-done.tgt_ref) | copy-start | bytes 12582916
  63.9 0.7 copy-start.4
  64.6 0.7 copy-start.5
  65.2 44.7 %copy-start.2 = (f32[2048]{0:T(1024)S(1)}, f32[2048]{0:T(1024)}, u32[]{:S(2)}) copy-start(f32[2048]{0:T(1024)} %param.10) | copy-start | bytes 24580
  136.8 26.9 %copy-start.1 = (bf16[2048,1024]{1,0:T(8,128)(2,1)S(1)}, bf16[2048,1024]{1,0:T(8,128)(2,1)}, u32[]{:S(2)}) copy-start(bf16[2048,1024]{1,0:T(8,128)(2,1)} %all-gather.2.cloned.1.call-done.tgt_ref) | copy-start | bytes 12582916
  168.1 34.8 %all-to-all-start.7 = ((bf16[32,16,1152]{2,1,0:T(8,128)(2,1)}), bf16[32,16,1152]{2,1,0:T(8,128)(2,1)S(1)}, u32[]{:S(2)}, u32[]{:S(2)}) async-start(bf16[32,16,1152]{2,1,0:T(8,128)(2,1)} %bitcast.8), calls=%async_computation.7 | async-start | bytes 2359296 | tf_op jit(solution)/shard_map/all_to_all | solution.py:187
Sparse Core Ops, SparseCore 0:
  10.1 51.5 all-gather.1

commit v2 on v1

v2 whole, which is shorter than its diff:
```python
import math

import jax
import jax.numpy as jnp
import numpy as np
from jax import lax
from jax.experimental import pallas as pl
from jax.experimental.pallas import tpu as pltpu
from jax.sharding import PartitionSpec as P

BLK = 128
ITERS = 3
EPS = 0.02
UNIT = EPS * math.log(2.0)
FAR = 1e30
MIB = 1 << 20
CHIPS, CORES = 8, 2
COLY, COLX = 8, 4
CHUNK = 256


def nt_dot(a, b):
    return lax.dot_general(a, b, (((1,), (1,)), ((), ())), preferred_element_type=jnp.float32)


def square_sums(rows):
    rows = rows.astype(jnp.float32)
    rows = rows * rows
    total = rows[:, :BLK]
    for d in range(BLK, rows.shape[1], BLK):
        total = total + rows[:, d : d + BLK]
    return total


def lanes_of(row):
    return jnp.transpose(jnp.broadcast_to(row, (BLK, BLK)))


def finish_rows(peak, total):
    peak, total = jnp.transpose(peak), jnp.transpose(total)
    top = jnp.max(peak, axis=0, keepdims=True)
    return top + jnp.log2(jnp.sum(total * jnp.exp2(peak - top), axis=0, keepdims=True))


def tiles_of(cost_refs):
    return [(ref, slice(d, d + BLK)) for ref in cost_refs for d in range(0, ref.shape[1], BLK)]


def source_parts(cost_refs, pot_row, part_ref):
    tiles = tiles_of(cost_refs)
    for s in range(cost_refs[0].shape[0] // BLK):
        at = slice(s * BLK, (s + 1) * BLK)

        def gap(n):
            ref, lanes = tiles[n]
            return pot_row(n) - ref[at, lanes]

        peak = gap(0)
        for n in range(1, len(tiles)):
            peak = jnp.maximum(peak, gap(n))
        total = jnp.exp2(gap(0) - peak)
        for n in range(1, len(tiles)):
            total = total + jnp.exp2(gap(n) - peak)
        row = finish_rows(peak, total)
        for k in range(part_ref.shape[0]):
            part_ref[k, s : s + 1, :] = row


def cost_kernel(first, npiece, last, *refs):
    order, sidx, tidx, live, src_ref, *refs = refs
    pieces, refs = refs[:npiece], refs[npiece:]
    if first == 0:
        cost_ref, norm_ref, far = refs
    elif last:
        norm_ref, *held, cost_ref, part_ref, far = refs
    else:
        norm_ref, cost_ref, far = refs
    nsrc = src_ref.shape[0] // BLK
    ntgt = far.shape[0] // nsrc
    scale = 1.0 / (src_ref.shape[1] * UNIT)
    for i in range(far.shape[0]):
        far[i] = FAR

    def mark(k, c):
        far[sidx[k] * ntgt + tidx[k]] = 0.0
        return c

    lax.fori_loop(0, live[0], mark, 0)
    if first == 0:
        for s in range(nsrc):
            at = slice(s * BLK, (s + 1) * BLK)
            norm = jnp.sum(square_sums(src_ref[at, :]), axis=1, keepdims=True) * scale
            norm_ref[at, :] = jnp.broadcast_to(norm, (BLK, BLK))
    slot, lane = first, 0
    for piece in pieces:
        count = piece.shape[0] // BLK
        away = []
        for t in range(count):
            sums = jnp.transpose(square_sums(piece[t * BLK : (t + 1) * BLK, :]))
            away.append(jnp.sum(sums, axis=0, keepdims=True) * scale)
        for s in range(nsrc):
            at = slice(s * BLK, (s + 1) * BLK)
            cross = nt_dot(src_ref[at, :], piece[...]) * (-2.0 * scale)
            for t in range(count):
                far_off = far[s * ntgt + order[slot + t]]
                tile = cross[:, t * BLK : (t + 1) * BLK] + norm_ref[at, :] + (away[t] + far_off)
                cost_ref[at, lane + t * BLK : lane + (t + 1) * BLK] = tile
        slot += count
        lane += count * BLK
    if last:
        source_parts([*held, cost_ref], lambda n: 0.0, part_ref)


def combine(mass_ref, parts_ref):
    parts = parts_ref[...]
    top = jnp.max(parts, axis=0)
    low = jnp.log2(jnp.sum(jnp.exp2(parts - top[None]), axis=0))
    return jnp.log2(mass_ref[...]) - (top + low)


def target_kernel(order, parts_ref, mass_ref, *refs):
    *cost_refs, pot_ref, part_ref, wide, mine = refs
    pot = combine(mass_ref, parts_ref)
    pot_ref[...] = pot
    for s in range(pot.shape[0]):
        wide[s * BLK : (s + 1) * BLK, :] = lanes_of(pot[s : s + 1, :])
    for n, (ref, lanes) in enumerate(tiles_of(cost_refs)):
        gap = (wide[...] - ref[:, lanes]).reshape(-1, 8, BLK)
        peak = jnp.max(gap, axis=0)
        top = jnp.max(peak, axis=0, keepdims=True)
        total = jnp.sum(jnp.exp2(gap - top[None]), axis=0)
        mine[pl.ds(order[n], 1), :] = top + jnp.log2(jnp.sum(total, axis=0, keepdims=True))
    part_ref[...] = jnp.broadcast_to(mine[...][None], part_ref.shape)


def source_kernel(order, parts_ref, mass_ref, *refs):
    *cost_refs, part_ref, pot_ref = refs
    pot_ref[...] = combine(mass_ref, parts_ref)
    rows = [pot_ref[pl.ds(order[n], 1), :] for n in range(pot_ref.shape[0])]
    source_parts(cost_refs, lambda n: rows[n], part_ref)


def map_kernel(npiece, order, parts_ref, mass_ref, fpot_ref, *refs):
    pieces, refs = refs[:npiece], refs[npiece:]
    *cost_refs, pot_ref, sums_ref, weight = refs
    pot_ref[...] = combine(mass_ref, parts_ref)
    nsrc = cost_refs[0].shape[0] // BLK
    width = pieces[0].shape[1]
    for s in range(nsrc):
        at = slice(s * BLK, (s + 1) * BLK)
        mine = lanes_of(fpot_ref[s : s + 1, :])
        for n, (ref, lanes) in enumerate(tiles_of(cost_refs)):
            power = jnp.exp2(mine + pot_ref[pl.ds(order[n], 1), :] - ref[at, lanes])
            weight[at, n * BLK : (n + 1) * BLK] = power.astype(jnp.bfloat16)

    share = sums_ref.shape[1] // COLY

    def put(block, lanes):
        for y in range(COLY):
            for x in range(COLX):
                k = (y * COLX + x) * share
                sums_ref[x, y * share : (y + 1) * share, lanes] = block[k : k + share, :]

    for d in range(0, width, CHUNK):
        part, lane = None, 0
        for piece in pieces:
            low = weight[:, lane : lane + piece.shape[0]]
            add = jnp.dot(low, piece[:, d : d + CHUNK], preferred_element_type=jnp.float32)
            part = add if part is None else part + add
            lane += piece.shape[0]
        put(part.astype(jnp.bfloat16), slice(d, d + CHUNK))
    ones = jnp.ones((weight.shape[1], BLK), jnp.bfloat16)
    total = jnp.dot(weight[...], ones, preferred_element_type=jnp.float32)
    put(two_pieces(total), slice(width, width + BLK))


def two_pieces(total):
    high = total.astype(jnp.bfloat16).astype(jnp.float32)
    lane = lax.broadcasted_iota(jnp.int32, total.shape, 1)
    return jnp.where(lane == 0, high, total - high).astype(jnp.bfloat16)


def add_up(sums_ref):
    sums = sums_ref[0].astype(jnp.float32)
    for k in range(1, sums_ref.shape[0]):
        sums = sums + sums_ref[k].astype(jnp.float32)
    return sums


def add_kernel(sums_ref, out_ref):
    width = out_ref.shape[1] - BLK
    sums = add_up(sums_ref)
    total = sums[:, width : width + 1] + sums[:, width + 1 : width + 2]
    out_ref[:, :width] = sums[:, :width].astype(jnp.bfloat16)
    out_ref[:, width:] = two_pieces(jnp.broadcast_to(total, (total.shape[0], BLK)))


def divide_kernel(sums_ref, out_ref):
    width = out_ref.shape[1]
    sums = add_up(sums_ref)
    total = sums[:, width : width + 1] + sums[:, width + 1 : width + 2]
    out_ref[...] = (sums[:, :width] / total).astype(out_ref.dtype)


def call(kernel, shapes, scratch, scalars, args, limit):
    vmem = pl.BlockSpec(memory_space=pltpu.VMEM)
    smem = pl.BlockSpec(memory_space=pltpu.SMEM)
    return pl.pallas_call(
        kernel,
        out_shape=shapes,
        in_specs=[smem] * len(scalars) + [vmem] * len(args),
        out_specs=jax.tree.map(lambda _: vmem, shapes),
        scratch_shapes=scratch,
        compiler_params=pltpu.CompilerParams(vmem_limit_bytes=limit * MIB),
    )(*scalars, *args)


def shape(*dims, dtype=jnp.float32):
    return jax.ShapeDtypeStruct(dims, dtype)


def spread(x, axis, groups=None):
    return lax.all_to_all(x, axis, 0, 0, tiled=True, axis_index_groups=groups)


def move(x, place):
    pairs = []
    for z in range(CHIPS):
        for c in range(CORES):
            to = place(z, c)
            pairs.append((z * CORES + c, to[0] % CHIPS * CORES + to[1]))
    return lax.ppermute(x, "row", pairs)


def ring(x):
    return move(x, lambda z, c: (z + 1 - 2 * c, c))


def partner(x):
    return move(x, lambda z, c: (z, 1 - c))


def held_order():
    table = []
    for z in range(CHIPS):
        for c in range(CORES):
            way = 2 * c - 1
            slots = [z * 2 + c, z * 2 + 1 - c]
            for k in range(1, CHIPS // 2):
                near, other = (z + way * k) % CHIPS, (z - way * k) % CHIPS
                slots += [near * 2 + c, near * 2 + 1 - c, other * 2 + 1 - c, other * 2 + c]
            across = (z + CHIPS // 2) % CHIPS
            table.append(slots + [across * 2 + c, across * 2 + 1 - c])
    table = jnp.asarray(np.array(table, np.int32))
    return lax.dynamic_index_in_dim(table, lax.axis_index("row"), 0, keepdims=False)


def gather_targets(target):
    held = jnp.concatenate([target, partner(target)])
    pieces = [held]
    for _ in range(1, CHIPS // 2):
        held = ring(held)
        pieces += [held, partner(held)]
    held = ring(held[: target.shape[0]])
    return pieces + [held, partner(held)]


def body(source, target, source_mass, target_mass, tile_src, tile_dst, tile_count):
    rows, cols = lax.axis_size("row"), lax.axis_size("col")
    width = source.shape[1]
    nsrc, ntgt = source_mass.shape[0] // BLK, target_mass.shape[0] // BLK
    src = spread(jnp.broadcast_to(source[None], (cols, *source.shape)), "col")
    src = src.reshape(-1, width)
    pieces = gather_targets(target)
    amass = source_mass.reshape(nsrc, BLK)
    bmass = target_mass.reshape(ntgt, BLK)
    order = held_order()
    scalars = (order, tile_src.reshape(-1), tile_dst.reshape(-1), tile_count.reshape(-1))
    far = pltpu.SMEM((nsrc * ntgt,), jnp.float32)

    def costs(first, some, last, held, outs):
        count = sum(piece.shape[0] for piece in some)
        return call(
            lambda *refs: cost_kernel(first, len(some), last, *refs),
            (shape(src.shape[0], count), *outs),
            [far],
            scalars,
            (src, *some, *held),
            24,
        )

    norms = shape(src.shape[0], BLK)
    cost_a, norm = costs(0, pieces[:5], False, (), (norms,))
    (cost_b,) = costs(10, pieces[5:7], False, (norm,), ())
    cost_c, part = costs(14, pieces[7:], True, (norm, cost_a, cost_b), (shape(cols, nsrc, BLK),))
    cost = (cost_a, cost_b, cost_c)

    for step in range(ITERS):
        fpot, part = call(
            target_kernel,
            (shape(nsrc, BLK), shape(rows, ntgt, BLK)),
            [pltpu.VMEM((src.shape[0], BLK), jnp.float32), pltpu.VMEM((ntgt, BLK), jnp.float32)],
            (order,),
            (spread(part, "col"), amass, *cost),
            16,
        )
        parts = spread(part, "row")
        if step < ITERS - 1:
            part = call(
                source_kernel,
                shape(cols, nsrc, BLK),
                [pltpu.VMEM((ntgt, BLK), jnp.float32)],
                (order,),
                (parts, bmass, *cost),
                16,
            )
    share = src.shape[0] // cols
    gpot, sums = call(
        lambda *refs: map_kernel(len(pieces), *refs),
        (shape(ntgt, BLK), shape(COLX, COLY * share, width + BLK, dtype=jnp.bfloat16)),
        [pltpu.VMEM((src.shape[0], ntgt * BLK), jnp.bfloat16)],
        (order,),
        (parts, bmass, fpot, *pieces, *cost),
        32,
    )
    xgroups = [[y * COLX + x for x in range(COLX)] for y in range(COLY)]
    ygroups = [[y * COLX + x for y in range(COLY)] for x in range(COLX)]
    sums = spread(sums, "col", xgroups)
    sums = call(add_kernel, shape(*sums.shape[1:], dtype=jnp.bfloat16), [], (), (sums,), 8)
    sums = spread(sums.reshape(COLY, share, -1), "col", ygroups)
    mapped = call(divide_kernel, shape(share, width, dtype=jnp.bfloat16), [], (), (sums,), 8)
    return (fpot.reshape(-1) * UNIT, gpot.reshape(-1) * UNIT, mapped)


def solution(mesh):
    in_specs = (
        P(("row", "col"), None),
        P(("col", "row"), None),
        P("row"),
        P("col"),
        P("row", "col", None),
        P("row", "col", None),
        P("row", "col"),
    )
    out_specs = (P("row"), P("col"), P(("row", "col"), None))
    return jax.shard_map(body, mesh=mesh, in_specs=in_specs, out_specs=out_specs, check_vma=False)
```

time: 211 us -> 211 us (level)
  waiting for transfers between devices: 71.2 us -> 26.7 us
  starting transfers between devices: 14.5 us -> 47.8 us
  blocking collectives: 82.5 us -> 103 us
  between operations: 14.7 us -> 1.51 us
  Pallas kernels: 21.1 us -> 25.5 us
    all_to_all x2, waiting for transfers between devices: 55.3 us -> 11.2 us  [spread(): return lax.all_to_all(x, axis, 0, 0, tiled=True, axis_index_groups=groups)]
    ppermute x0 -> x9, starting transfers between devices: none -> 34.6 us  [move(): return lax.ppermute(x, 'row', pairs)]
    all_to_all x6 -> x7, blocking collectives: 82.5 us -> 103 us  [spread(): return lax.all_to_all(x, axis, 0, 0, tiled=True, axis_index_groups=groups)]
    ppermute x0 -> x9, waiting for transfers between devices: none -> 15.4 us  [move(): return lax.ppermute(x, 'row', pairs)]
    all_gather x1 -> x0, waiting for transfers between devices: 15.2 us -> none  [body(): tgt = lax.all_gather(target, 'row', axis=0, tiled=True)]
    pallas_call x8 -> x11, Pallas kernels: 21.1 us -> 25.5 us  [call(): pl.pallas_call(kernel, out_shape=shapes, in_specs=[smem] * len(scalars) +...]
    unnamed x12 -> x9, local copies, waits for them, and re-layouts: 3.51 us -> 0.99 us
  transfers between devices with their start and end apart: 3 -> 11, of which waited for: 3 -> 5; matrix products, arithmetic and copies ran while one was open for 1% -> 2% of each run, Pallas kernels for 0% -> 4%
where the time goes in v2:
time: 211 us; the launch traced here: 209 us
  blocking collectives  103 us (49%)
  starting transfers between devices  47.8 us (23%)
  waiting for transfers between devices  26.7 us (13%)
  Pallas kernels  25.5 us (12%)
  local copies, waits for them, and re-layouts  3.61 us (2%)
    all_to_all x7, blocking collectives, spread(): return lax.all_to_all(x, axis, 0, 0, tiled=True, axis_index_groups=groups)  103 us
    ppermute x9, starting transfers between devices, move(): return lax.ppermute(x, 'row', pairs)  34.6 us
    pallas_call x11, Pallas kernels, call(): pl.pallas_call(kernel, out_shape=shapes, in_specs=[smem] * len(scalars) +...  25.5 us
    ppermute x9, waiting for transfers between devices, move(): return lax.ppermute(x, 'row', pairs)  15.4 us
    all_to_all x2, starting transfers between devices, spread(): return lax.all_to_all(x, axis, 0, 0, tiled=True, axis_index_groups=groups)  13.2 us
    all_to_all x2, waiting for transfers between devices, spread(): return lax.all_to_all(x, axis, 0, 0, tiled=True, axis_index_groups=groups)  11.2 us
  transfers between devices with their start and end apart: 11, of which 5 were waited for; matrix products, arithmetic and copies ran while one was open for 2% of the time, Pallas kernels for 4%

profile of v2, /device:TPU:1, one launch (start us, length us, event | category | flops | bytes accessed | tf_op | source)
XLA Modules:
  0.0 209.5 jit_solution(1764450921086191694)
XLA Ops:
  0.6 8.8 %collective-permute-start = (bf16[128,1024]{1,0:T(8,128)(2,1)}, bf16[128,1024]{1,0:T(8,128)(2,1)S(1)}, u32[]{:S(2)}, u32[]{:S(2)}) collective-permute-start(bf16[128,1024]{1,0:T(8,128)(2,1)} %param.9), channel_id=1, source_target_pairs={{0,32},{32,0},{64,96},{96,64},{128,160},{160,128},{192,224},{224,1... | collective-permute-start | bytes 786440 | tf_op jit(solution)/shard_map/ppermute | solution.py:232
  10.8 5.3 %collective-permute-start.1 = (bf16[256,1024]{1,0:T(8,128)(2,1)S(1)}, bf16[256,1024]{1,0:T(8,128)(2,1)S(1)}, u32[]{:S(2)}, u32[]{:S(2)}) collective-permute-start(bf16[256,1024]{1,0:T(8,128)(2,1)S(1)} %constant_dynamic-update-slice_fusion.refs_5_.refs_4_), channel_id=1, source_target_pairs={{0,64},{32,480},{64,128},{96,32},{128,192},{160,96},{192,256},{224... | collective-permute-start | bytes 1572872 | tf_op jit(solution)/shard_map/ppermute | solution.py:232
  16.1 1.9 broadcast_in_dim.2
  18.0 9.8 %all-to-all-start = ((bf16[32,16,1024]{2,1,0:T(8,128)(2,1)}), bf16[32,16,1024]{2,1,0:T(8,128)(2,1)S(1)}, u32[]{:S(2)}, u32[]{:S(2)}) async-start(bf16[32,16,1024]{2,1,0:T(8,128)(2,1)} %broadcast_in_dim.2), calls=%async_computation | async-start | bytes 2097152 | tf_op jit(solution)/shard_map/all_to_all | solution.py:223
  27.8 2.2 %collective-permute-start.2 = (bf16[256,1024]{1,0:T(8,128)(2,1)S(1)}, bf16[256,1024]{1,0:T(8,128)(2,1)S(1)}, u32[]{:S(2)}, u32[]{:S(2)}) collective-permute-start(bf16[256,1024]{1,0:T(8,128)(2,1)S(1)} %collective-permute-done.1.refs_6_.refs_5_), channel_id=1, source_target_pairs={{0,64},{32,480},{64,128},{96,32},{128,192},{160,96},{192,256},{224... | collective-permute-start | bytes 1572872 | tf_op jit(solution)/shard_map/ppermute | solution.py:232
  30.0 8.0 %collective-permute-done.2.refs_8_.refs_7_ = bf16[256,1024]{1,0:T(8,128)(2,1)S(1)} collective-permute-done((bf16[256,1024]{1,0:T(8,128)(2,1)S(1)}, bf16[256,1024]{1,0:T(8,128)(2,1)S(1)}, u32[]{:S(2)}, u32[]{:S(2)}) %collective-permute-start.2) | collective-permute-done | bytes 524320 | tf_op jit(solution)/shard_map/ppermute | solution.py:232
  38.0 3.4 %collective-permute-start.3 = (bf16[256,1024]{1,0:T(8,128)(2,1)S(1)}, bf16[256,1024]{1,0:T(8,128)(2,1)S(1)}, u32[]{:S(2)}, u32[]{:S(2)}) collective-permute-start(bf16[256,1024]{1,0:T(8,128)(2,1)S(1)} %collective-permute-done.2.refs_8_.refs_7_), channel_id=1, source_target_pairs={{0,64},{32,480},{64,128},{96,32},{128,192},{160,96},{192,256},{224... | collective-permute-start | bytes 1572872 | tf_op jit(solution)/shard_map/ppermute | solution.py:232
  41.4 1.9 collective-permute-start.6
  43.4 2.4 %collective-permute-start.7 = (bf16[256,1024]{1,0:T(8,128)(2,1)S(1)}, bf16[256,1024]{1,0:T(8,128)(2,1)}, u32[]{:S(2)}, u32[]{:S(2)}) collective-permute-start(bf16[256,1024]{1,0:T(8,128)(2,1)S(1)} %collective-permute-done.2.refs_8_.refs_7_), channel_id=1, source_target_pairs={{0,32},{32,0},{64,96},{96,64},{128,160},{160,128},{192,224},{224,1... | collective-permute-start | bytes 1572872 | tf_op jit(solution)/shard_map/ppermute | solution.py:232
  45.8 2.4 %collective-permute-done.3.refs_5_.refs_9_ = bf16[256,1024]{1,0:T(8,128)(2,1)S(1)} collective-permute-done((bf16[256,1024]{1,0:T(8,128)(2,1)S(1)}, bf16[256,1024]{1,0:T(8,128)(2,1)S(1)}, u32[]{:S(2)}, u32[]{:S(2)}) %collective-permute-start.3) | collective-permute-done | bytes 524320 | tf_op jit(solution)/shard_map/ppermute | solution.py:232
  48.2 3.8 %collective-permute-start.8 = (bf16[256,1024]{1,0:T(8,128)(2,1)S(1)}, bf16[256,1024]{1,0:T(8,128)(2,1)}, u32[]{:S(2)}, u32[]{:S(2)}) collective-permute-start(bf16[256,1024]{1,0:T(8,128)(2,1)S(1)} %collective-permute-done.3.refs_5_.refs_9_), channel_id=1, source_target_pairs={{0,32},{32,0},{64,96},{96,64},{128,160},{160,128},{192,224},{224,1... | collective-permute-start | bytes 1572872 | tf_op jit(solution)/shard_map/ppermute | solution.py:232
  52.0 2.8 %collective-permute-start.4 = (bf16[128,1024]{1,0:T(8,128)(2,1)S(1)}, bf16[128,1024]{1,0:T(8,128)(2,1)S(1)}, u32[]{:S(2)}, u32[]{:S(2)}) collective-permute-start(bf16[128,1024]{1,0:T(8,128)(2,1)S(1)} %slice.4), channel_id=1, source_target_pairs={{0,64},{32,480},{64,128},{96,32},{128,192},{160,96},{192,256},{224... | collective-permute-start | bytes 786440 | tf_op jit(solution)/shard_map/ppermute | solution.py:232
  54.8 4.6 %collective-permute-done.4.refs_5_.refs_11_ = bf16[128,1024]{1,0:T(8,128)(2,1)S(1)} collective-permute-done((bf16[128,1024]{1,0:T(8,128)(2,1)S(1)}, bf16[128,1024]{1,0:T(8,128)(2,1)S(1)}, u32[]{:S(2)}, u32[]{:S(2)}) %collective-permute-start.4) | collective-permute-done | bytes 262176 | tf_op jit(solution)/shard_map/ppermute | solution.py:232
  59.4 4.0 %collective-permute-start.5 = (bf16[128,1024]{1,0:T(8,128)(2,1)S(1)}, bf16[128,1024]{1,0:T(8,128)(2,1)}, u32[]{:S(2)}, u32[]{:S(2)}) collective-permute-start(bf16[128,1024]{1,0:T(8,128)(2,1)S(1)} %collective-permute-done.4.refs_5_.refs_11_), channel_id=1, source_target_pairs={{0,32},{32,0},{64,96},{96,64},{128,160},{160,128},{192,224},{224,1... | collective-permute-start | bytes 786440 | tf_op jit(solution)/shard_map/ppermute | solution.py:232
  64.8 5.1 %shard_map.103 = (f32[512,1280]{1,0:T(8,128)S(1)}, f32[512,128]{1,0:T(8,128)S(1)}) custom-call(s32[16]{0:T(128)S(1)} %dynamic-slice_bitcast_fusion.refs_0_.order, s32[32]{0:T(128)S(1)} %bitcast.25, s32[32]{0:T(128)S(1)} %bitcast.28, s32[1]{0:T(128)} %bitcast.13.refs_3_, bf16[512,1024]{1,0:T(8,128)(2,1)S(1)} %bitcast.16, ...), custom_call_target="tpu_custom_call" | custom-call | tf_op jit(solution)/shard_map/pallas_call | solution.py:208
  69.9 2.8 %shard_map.104.refs_9_.refs_1_.refs_14_ = f32[512,512]{1,0:T(8,128)S(1)} custom-call(s32[16]{0:T(128)S(1)} %dynamic-slice_bitcast_fusion.refs_0_.order, s32[32]{0:T(128)S(1)} %bitcast.26, s32[32]{0:T(128)S(1)} %bitcast.29, s32[1]{0:T(128)} %bitcast.14.refs_3_, bf16[512,1024]{1,0:T(8,128)(2,1)S(1)} %bitcast.17, ...), custom_call_target="tpu_custom_call" | custom-call | tf_op jit(solution)/shard_map/pallas_call | solution.py:208
  72.8 2.7 %shard_map.105 = (f32[512,256]{1,0:T(8,128)S(1)}, f32[32,4,128]{2,1,0:T(4,128)S(1)}) custom-call(s32[16]{0:T(128)S(1)} %dynamic-slice_bitcast_fusion.refs_0_.order, s32[32]{0:T(128)S(1)} %bitcast.27, s32[32]{0:T(128)S(1)} %bitcast.30, s32[1]{0:T(128)} %bitcast.15.refs_3_, bf16[512,1024]{1,0:T(8,128)(2,1)S(1)} %bitcast.18, ...), custom_call_target="tpu_custom_call" | custom-call | tf_op jit(solution)/shard_map/pallas_call | solution.py:208
  75.5 18.1 %all_to_all.45.parts_ref = f32[32,4,128]{2,1,0:T(4,128)S(1)} all-to-all(f32[32,4,128]{2,1,0:T(4,128)S(1)} %get-tuple-element.15), channel_id=1, replica_groups=mesh['row'=16,'col'=32] {'col'}, dimensions={0} | all-to-all | bytes 131072 | tf_op jit(solution)/shard_map/all_to_all | solution.py:223
  93.5 1.9 shard_map.106
  95.4 16.1 %all_to_all.46.parts_ref = f32[16,16,128]{2,1,0:T(8,128)S(1)} all-to-all(f32[16,16,128]{2,1,0:T(8,128)S(1)} %get-tuple-element.17), channel_id=1, replica_groups=mesh['row'=16,'col'=32] {'row'}, dimensions={0} | all-to-all | bytes 262144 | tf_op jit(solution)/shard_map/all_to_all | solution.py:223
  111.5 1.5 shard_map.107
  113.0 12.3 %all_to_all.47.parts_ref = f32[32,4,128]{2,1,0:T(4,128)S(1)} all-to-all(f32[32,4,128]{2,1,0:T(4,128)S(1)} %shard_map.107), channel_id=1, replica_groups=mesh['row'=16,'col'=32] {'col'}, dimensions={0} | all-to-all | bytes 131072 | tf_op jit(solution)/shard_map/all_to_all | solution.py:223
  125.3 1.9 shard_map.108
  127.2 12.5 %all_to_all.48.parts_ref = f32[16,16,128]{2,1,0:T(8,128)S(1)} all-to-all(f32[16,16,128]{2,1,0:T(8,128)S(1)} %get-tuple-element.18), channel_id=1, replica_groups=mesh['row'=16,'col'=32] {'row'}, dimensions={0} | all-to-all | bytes 262144 | tf_op jit(solution)/shard_map/all_to_all | solution.py:223
  139.7 1.5 shard_map.109
  141.2 12.5 %all_to_all.49.parts_ref = f32[32,4,128]{2,1,0:T(4,128)S(1)} all-to-all(f32[32,4,128]{2,1,0:T(4,128)S(1)} %shard_map.109), channel_id=1, replica_groups=mesh['row'=16,'col'=32] {'col'}, dimensions={0} | all-to-all | bytes 131072 | tf_op jit(solution)/shard_map/all_to_all | solution.py:223
  153.7 1.5 shard_map.110
  155.2 12.4 %all_to_all.50.refs_1_ = f32[16,16,128]{2,1,0:T(8,128)S(1)} all-to-all(f32[16,16,128]{2,1,0:T(8,128)S(1)} %get-tuple-element.20), channel_id=1, replica_groups=mesh['row'=16,'col'=32] {'row'}, dimensions={0} | all-to-all | bytes 262144 | tf_op jit(solution)/shard_map/all_to_all | solution.py:223
  167.6 4.9 %shard_map.111 = (f32[16,128]{1,0:T(8,128)S(1)}, bf16[4,128,1152]{2,1,0:T(8,128)(2,1)S(1)}) custom-call(s32[16]{0:T(128)S(1)} %dynamic-slice_bitcast_fusion.refs_0_.order, f32[16,16,128]{2,1,0:T(8,128)S(1)} %all_to_all.50.refs_1_, f32[16,128]{1,0:T(8,128)S(1)} %bitcast.21, f32[4,128]{1,0:T(4,128)S(1)} %get-tuple-element.19.refs_3_, ...), custom_call_target="tpu_custom_call" | custom-call | tf_op jit(solution)/shard_map/pallas_call | solution.py:208
  172.6 19.3 %all_to_all.51.sums_ref = bf16[4,128,1152]{2,1,0:T(8,128)(2,1)S(1)} all-to-all(bf16[4,128,1152]{2,1,0:T(8,128)(2,1)S(1)} %get-tuple-element.22), channel_id=1, replica_groups={{0,1,2,3},{4,5,6,7},{8,9,10,11},{12,13,14,15},{16,17,18,19},{20,21,22,2..., dimensions={0} | all-to-all | bytes 2359296 | tf_op jit(solution)/shard_map/all_to_all | solution.py:223
  192.9 3.4 %all-to-all-start.8 = ((bf16[8,16,1152]{2,1,0:T(8,128)(2,1)}), bf16[8,16,1152]{2,1,0:T(8,128)(2,1)S(1)}, u32[]{:S(2)}, u32[]{:S(2)}) async-start(bf16[8,16,1152]{2,1,0:T(8,128)(2,1)} %bitcast.9), calls=%async_computation.8 | async-start | bytes 589824 | tf_op jit(solution)/shard_map/all_to_all | solution.py:223
  197.5 11.2 %all-to-all-done.8.sums_ref = bf16[8,16,1152]{2,1,0:T(8,128)(2,1)S(1)} async-done(((bf16[8,16,1152]{2,1,0:T(8,128)(2,1)}), bf16[8,16,1152]{2,1,0:T(8,128)(2,1)S(1)}, u32[]{:S(2)}, u32[]{:S(2)}) %all-to-all-start.8) | async-done | bytes 294944 | tf_op jit(solution)/shard_map/all_to_all | solution.py:223
  (23 shorter events, 5.1 us)
Async XLA Ops:
  0.6 10.1 %collective-permute-start = (bf16[128,1024]{1,0:T(8,128)(2,1)}, bf16[128,1024]{1,0:T(8,128)(2,1)S(1)}, u32[]{:S(2)}, u32[]{:S(2)}) collective-permute-start(bf16[128,1024]{1,0:T(8,128)(2,1)} %param.9), channel_id=1, source_target_pairs={{0,32},{32,0},{64,96},{96,64},{128,160},{160,128},{192,224},{224,1... | collective-permute-start | bytes 786440 | tf_op jit(solution)/shard_map/ppermute | solution.py:232
  10.8 17.0 %collective-permute-start.1 = (bf16[256,1024]{1,0:T(8,128)(2,1)S(1)}, bf16[256,1024]{1,0:T(8,128)(2,1)S(1)}, u32[]{:S(2)}, u32[]{:S(2)}) collective-permute-start(bf16[256,1024]{1,0:T(8,128)(2,1)S(1)} %constant_dynamic-update-slice_fusion.refs_5_.refs_4_), channel_id=1, source_target_pairs={{0,64},{32,480},{64,128},{96,32},{128,192},{160,96},{192,256},{224... | collective-permute-start | bytes 1572872 | tf_op jit(solution)/shard_map/ppermute | solution.py:232
  18.0 46.8 %copy-start.2 = (s32[1,1,32]{2,1,0:T(1,128)S(1)}, s32[1,1,32]{2,1,0:T(1,128)}, u32[]{:S(2)}) copy-start(s32[1,1,32]{2,1,0:T(1,128)} %param.12) | copy-start | bytes 388
  18.0 46.8 %copy-start.3 = (s32[1,1,32]{2,1,0:T(1,128)S(1)}, s32[1,1,32]{2,1,0:T(1,128)}, u32[]{:S(2)}) copy-start(s32[1,1,32]{2,1,0:T(1,128)} %param.13) | copy-start | bytes 388
  18.0 46.8 %all-to-all-start = ((bf16[32,16,1024]{2,1,0:T(8,128)(2,1)}), bf16[32,16,1024]{2,1,0:T(8,128)(2,1)S(1)}, u32[]{:S(2)}, u32[]{:S(2)}) async-start(bf16[32,16,1024]{2,1,0:T(8,128)(2,1)} %broadcast_in_dim.2), calls=%async_computation | async-start | bytes 2097152 | tf_op jit(solution)/shard_map/all_to_all | solution.py:223
  27.8 10.2 %collective-permute-start.2 = (bf16[256,1024]{1,0:T(8,128)(2,1)S(1)}, bf16[256,1024]{1,0:T(8,128)(2,1)S(1)}, u32[]{:S(2)}, u32[]{:S(2)}) collective-permute-start(bf16[256,1024]{1,0:T(8,128)(2,1)S(1)} %collective-permute-done.1.refs_6_.refs_5_), channel_id=1, source_target_pairs={{0,64},{32,480},{64,128},{96,32},{128,192},{160,96},{192,256},{224... | collective-permute-start | bytes 1572872 | tf_op jit(solution)/shard_map/ppermute | solution.py:232
  38.0 10.2 %collective-permute-start.3 = (bf16[256,1024]{1,0:T(8,128)(2,1)S(1)}, bf16[256,1024]{1,0:T(8,128)(2,1)S(1)}, u32[]{:S(2)}, u32[]{:S(2)}) collective-permute-start(bf16[256,1024]{1,0:T(8,128)(2,1)S(1)} %collective-permute-done.2.refs_8_.refs_7_), channel_id=1, source_target_pairs={{0,64},{32,480},{64,128},{96,32},{128,192},{160,96},{192,256},{224... | collective-permute-start | bytes 1572872 | tf_op jit(solution)/shard_map/ppermute | solution.py:232
  41.4 23.3 %collective-permute-start.6 = (bf16[256,1024]{1,0:T(8,128)(2,1)S(1)}, bf16[256,1024]{1,0:T(8,128)(2,1)}, u32[]{:S(2)}, u32[]{:S(2)}) collective-permute-start(bf16[256,1024]{1,0:T(8,128)(2,1)S(1)} %collective-permute-done.1.refs_6_.refs_5_), channel_id=1, source_target_pairs={{0,32},{32,0},{64,96},{96,64},{128,160},{160,128},{192,224},{224,1... | collective-permute-start | bytes 1572872 | tf_op jit(solution)/shard_map/ppermute | solution.py:232
  43.4 21.4 %collective-permute-start.7 = (bf16[256,1024]{1,0:T(8,128)(2,1)S(1)}, bf16[256,1024]{1,0:T(8,128)(2,1)}, u32[]{:S(2)}, u32[]{:S(2)}) collective-permute-start(bf16[256,1024]{1,0:T(8,128)(2,1)S(1)} %collective-permute-done.2.refs_8_.refs_7_), channel_id=1, source_target_pairs={{0,32},{32,0},{64,96},{96,64},{128,160},{160,128},{192,224},{224,1... | collective-permute-start | bytes 1572872 | tf_op jit(solution)/shard_map/ppermute | solution.py:232
  48.2 21.7 %collective-permute-start.8 = (bf16[256,1024]{1,0:T(8,128)(2,1)S(1)}, bf16[256,1024]{1,0:T(8,128)(2,1)}, u32[]{:S(2)}, u32[]{:S(2)}) collective-permute-start(bf16[256,1024]{1,0:T(8,128)(2,1)S(1)} %collective-permute-done.3.refs_5_.refs_9_), channel_id=1, source_target_pairs={{0,32},{32,0},{64,96},{96,64},{128,160},{160,128},{192,224},{224,1... | collective-permute-start | bytes 1572872 | tf_op jit(solution)/shard_map/ppermute | solution.py:232
  52.0 7.4 %collective-permute-start.4 = (bf16[128,1024]{1,0:T(8,128)(2,1)S(1)}, bf16[128,1024]{1,0:T(8,128)(2,1)S(1)}, u32[]{:S(2)}, u32[]{:S(2)}) collective-permute-start(bf16[128,1024]{1,0:T(8,128)(2,1)S(1)} %slice.4), channel_id=1, source_target_pairs={{0,64},{32,480},{64,128},{96,32},{128,192},{160,96},{192,256},{224... | collective-permute-start | bytes 786440 | tf_op jit(solution)/shard_map/ppermute | solution.py:232
  59.4 13.3 %collective-permute-start.5 = (bf16[128,1024]{1,0:T(8,128)(2,1)S(1)}, bf16[128,1024]{1,0:T(8,128)(2,1)}, u32[]{:S(2)}, u32[]{:S(2)}) collective-permute-start(bf16[128,1024]{1,0:T(8,128)(2,1)S(1)} %collective-permute-done.4.refs_5_.refs_11_), channel_id=1, source_target_pairs={{0,32},{32,0},{64,96},{96,64},{128,160},{160,128},{192,224},{224,1... | collective-permute-start | bytes 786440 | tf_op jit(solution)/shard_map/ppermute | solution.py:232
  72.7 20.8 %copy-start.1 = (f32[512]{0:T(512)S(1)}, f32[512]{0:T(512)}, u32[]{:S(2)}) copy-start(f32[512]{0:T(512)} %param.10) | copy-start | bytes 6148
  93.5 18.0 %copy-start = (f32[2048]{0:T(1024)S(1)}, f32[2048]{0:T(1024)}, u32[]{:S(2)}) copy-start(f32[2048]{0:T(1024)} %param.11) | copy-start | bytes 24580
  192.9 15.8 %all-to-all-start.8 = ((bf16[8,16,1152]{2,1,0:T(8,128)(2,1)}), bf16[8,16,1152]{2,1,0:T(8,128)(2,1)S(1)}, u32[]{:S(2)}, u32[]{:S(2)}) async-start(bf16[8,16,1152]{2,1,0:T(8,128)(2,1)} %bitcast.9), calls=%async_computation.8 | async-start | bytes 589824 | tf_op jit(solution)/shard_map/all_to_all | solution.py:223

commit v3 on v2

--- a/solution.py
+++ b/solution.py
@@ -2,7 +2,6 @@
 
 import jax
 import jax.numpy as jnp
-import numpy as np
 from jax import lax
 from jax.experimental import pallas as pl
 from jax.experimental.pallas import tpu as pltpu
@@ -15,7 +14,6 @@
 FAR = 1e30
 MIB = 1 << 20
 CHIPS, CORES = 8, 2
-COLY, COLX = 8, 4
 CHUNK = 256
 
 
@@ -67,7 +65,8 @@
 
 
 def cost_kernel(first, npiece, last, *refs):
-    order, sidx, tidx, live, src_ref, *refs = refs
+    sidx, tidx, live, src_ref, *refs = refs
+    order = held_order()
     pieces, refs = refs[:npiece], refs[npiece:]
     if first == 0:
         cost_ref, norm_ref, far = refs
@@ -98,12 +97,12 @@
         for t in range(count):
             sums = jnp.transpose(square_sums(piece[t * BLK : (t + 1) * BLK, :]))
             away.append(jnp.sum(sums, axis=0, keepdims=True) * scale)
+        cross = nt_dot(src_ref[...], piece[...]) * (-2.0 * scale)
         for s in range(nsrc):
             at = slice(s * BLK, (s + 1) * BLK)
-            cross = nt_dot(src_ref[at, :], piece[...]) * (-2.0 * scale)
             for t in range(count):
                 far_off = far[s * ntgt + order[slot + t]]
-                tile = cross[:, t * BLK : (t + 1) * BLK] + norm_ref[at, :] + (away[t] + far_off)
+                tile = cross[at, t * BLK : (t + 1) * BLK] + norm_ref[at, :] + (away[t] + far_off)
                 cost_ref[at, lane + t * BLK : lane + (t + 1) * BLK] = tile
         slot += count
         lane += count * BLK
@@ -118,8 +117,9 @@
     return jnp.log2(mass_ref[...]) - (top + low)
 
 
-def target_kernel(order, parts_ref, mass_ref, *refs):
+def target_kernel(parts_ref, mass_ref, *refs):
     *cost_refs, pot_ref, part_ref, wide, mine = refs
+    order = held_order()
     pot = combine(mass_ref, parts_ref)
     pot_ref[...] = pot
     for s in range(pot.shape[0]):
@@ -133,33 +133,35 @@
     part_ref[...] = jnp.broadcast_to(mine[...][None], part_ref.shape)
 
 
-def source_kernel(order, parts_ref, mass_ref, *refs):
+def source_kernel(parts_ref, mass_ref, *refs):
     *cost_refs, part_ref, pot_ref = refs
+    order = held_order()
     pot_ref[...] = combine(mass_ref, parts_ref)
     rows = [pot_ref[pl.ds(order[n], 1), :] for n in range(pot_ref.shape[0])]
     source_parts(cost_refs, lambda n: rows[n], part_ref)
 
 
-def map_kernel(npiece, order, parts_ref, mass_ref, fpot_ref, *refs):
+def map_kernel(npiece, parts_ref, mass_ref, fpot_ref, *refs):
     pieces, refs = refs[:npiece], refs[npiece:]
-    *cost_refs, pot_ref, sums_ref, weight = refs
-    pot_ref[...] = combine(mass_ref, parts_ref)
-    nsrc = cost_refs[0].shape[0] // BLK
+    *cost_refs, fout_ref, gout_ref, sums_ref, pot_ref, weight = refs
+    order = held_order()
+    pot = combine(mass_ref, parts_ref)
+    pot_ref[...] = pot
+    gout_ref[...] = pot * UNIT
+    fout_ref[...] = fpot_ref[...] * UNIT
+    rows = [pot_ref[pl.ds(order[n], 1), :] for n in range(pot_ref.shape[0])]
     width = pieces[0].shape[1]
-    for s in range(nsrc):
+    for s in range(fpot_ref.shape[0]):
         at = slice(s * BLK, (s + 1) * BLK)
         mine = lanes_of(fpot_ref[s : s + 1, :])
         for n, (ref, lanes) in enumerate(tiles_of(cost_refs)):
-            power = jnp.exp2(mine + pot_ref[pl.ds(order[n], 1), :] - ref[at, lanes])
+            power = jnp.exp2(mine + rows[n] - ref[at, lanes])
             weight[at, n * BLK : (n + 1) * BLK] = power.astype(jnp.bfloat16)
-
-    share = sums_ref.shape[1] // COLY
+    share = weight.shape[0] // sums_ref.shape[0]
 
     def put(block, lanes):
-        for y in range(COLY):
-            for x in range(COLX):
-                k = (y * COLX + x) * share
-                sums_ref[x, y * share : (y + 1) * share, lanes] = block[k : k + share, :]
+        for k in range(sums_ref.shape[0]):
+            sums_ref[k, :, lanes] = block[k * share : (k + 1) * share, :]
 
     for d in range(0, width, CHUNK):
         part, lane = None, 0
@@ -187,14 +189,6 @@
     return sums
 
 
-def add_kernel(sums_ref, out_ref):
-    width = out_ref.shape[1] - BLK
-    sums = add_up(sums_ref)
-    total = sums[:, width : width + 1] + sums[:, width + 1 : width + 2]
-    out_ref[:, :width] = sums[:, :width].astype(jnp.bfloat16)
-    out_ref[:, width:] = two_pieces(jnp.broadcast_to(total, (total.shape[0], BLK)))
-
-
 def divide_kernel(sums_ref, out_ref):
     width = out_ref.shape[1]
     sums = add_up(sums_ref)
@@ -202,7 +196,7 @@
     out_ref[...] = (sums[:, :width] / total).astype(out_ref.dtype)
 
 
-def call(kernel, shapes, scratch, scalars, args, limit):
+def call(kernel, shapes, scratch, scalars, args, limit, flops=None):
     vmem = pl.BlockSpec(memory_space=pltpu.VMEM)
     smem = pl.BlockSpec(memory_space=pltpu.SMEM)
     return pl.pallas_call(
@@ -212,6 +206,7 @@
         out_specs=jax.tree.map(lambda _: vmem, shapes),
         scratch_shapes=scratch,
         compiler_params=pltpu.CompilerParams(vmem_limit_bytes=limit * MIB),
+        cost_estimate=flops and pl.CostEstimate(flops=flops, bytes_accessed=0, transcendentals=0),
     )(*scalars, *args)
 
 
@@ -241,28 +236,15 @@
 
 
 def held_order():
-    table = []
-    for z in range(CHIPS):
-        for c in range(CORES):
-            way = 2 * c - 1
-            slots = [z * 2 + c, z * 2 + 1 - c]
-            for k in range(1, CHIPS // 2):
-                near, other = (z + way * k) % CHIPS, (z - way * k) % CHIPS
-                slots += [near * 2 + c, near * 2 + 1 - c, other * 2 + 1 - c, other * 2 + c]
-            across = (z + CHIPS // 2) % CHIPS
-            table.append(slots + [across * 2 + c, across * 2 + 1 - c])
-    table = jnp.asarray(np.array(table, np.int32))
-    return lax.dynamic_index_in_dim(table, lax.axis_index("row"), 0, keepdims=False)
-
-
-def gather_targets(target):
-    held = jnp.concatenate([target, partner(target)])
-    pieces = [held]
-    for _ in range(1, CHIPS // 2):
-        held = ring(held)
-        pieces += [held, partner(held)]
-    held = ring(held[: target.shape[0]])
-    return pieces + [held, partner(held)]
+    row = lax.axis_index("row")
+    z, c = row // CORES, row % CORES
+    way = 2 * c - 1
+    slots = [z * 2 + c, z * 2 + 1 - c]
+    for k in range(1, CHIPS // 2):
+        near, other = (z + way * k + CHIPS) % CHIPS, (z - way * k + CHIPS) % CHIPS
+        slots += [near * 2 + c, near * 2 + 1 - c, other * 2 + 1 - c, other * 2 + c]
+    across = (z + CHIPS // 2) % CHIPS
+    return slots + [across * 2 + c, across * 2 + 1 - c]
 
 
 def body(source, target, source_mass, target_mass, tile_src, tile_dst, tile_count):
@@ -271,36 +253,47 @@
     nsrc, ntgt = source_mass.shape[0] // BLK, target_mass.shape[0] // BLK
     src = spread(jnp.broadcast_to(source[None], (cols, *source.shape)), "col")
     src = src.reshape(-1, width)
-    pieces = gather_targets(target)
     amass = source_mass.reshape(nsrc, BLK)
     bmass = target_mass.reshape(ntgt, BLK)
-    order = held_order()
-    scalars = (order, tile_src.reshape(-1), tile_dst.reshape(-1), tile_count.reshape(-1))
-    far = pltpu.SMEM((nsrc * ntgt,), jnp.float32)
+    scalars = (tile_src.reshape(-1), tile_dst.reshape(-1), tile_count.reshape(-1))
 
     def costs(first, some, last, held, outs):
         count = sum(piece.shape[0] for piece in some)
         return call(
             lambda *refs: cost_kernel(first, len(some), last, *refs),
             (shape(src.shape[0], count), *outs),
-            [far],
+            [pltpu.SMEM((nsrc * ntgt,), jnp.float32)],
             scalars,
             (src, *some, *held),
             24,
+            2 * src.shape[0] * count * width,
         )
 
-    norms = shape(src.shape[0], BLK)
-    cost_a, norm = costs(0, pieces[:5], False, (), (norms,))
-    (cost_b,) = costs(10, pieces[5:7], False, (norm,), ())
-    cost_c, part = costs(14, pieces[7:], True, (norm, cost_a, cost_b), (shape(cols, nsrc, BLK),))
+    held = [jnp.concatenate([target, partner(target)])]
+    for _ in range(1, CHIPS // 2):
+        held.append(ring(held[-1]))
+    others = [partner(block) for block in held[1:]]
+    cost_a, norm = costs(
+        0, (held[0], held[1], others[0], held[2], others[1]), False, (), (shape(src.shape[0], BLK),)
+    )
+    (cost_b,) = costs(10, (held[3], others[2]), False, (norm,), ())
+    held.append(ring(held[3][: target.shape[0]]))
+    held[4], cost_a = lax.optimization_barrier((held[4], cost_a))
+    others.append(partner(held[4]))
+    cost_c, part = costs(
+        14, (held[4], others[3]), True, (norm, cost_a, cost_b), (shape(cols, nsrc, BLK),)
+    )
     cost = (cost_a, cost_b, cost_c)
+    pieces = [held[0]]
+    for block, other in zip(held[1:], others):
+        pieces += [block, other]
 
     for step in range(ITERS):
         fpot, part = call(
             target_kernel,
             (shape(nsrc, BLK), shape(rows, ntgt, BLK)),
             [pltpu.VMEM((src.shape[0], BLK), jnp.float32), pltpu.VMEM((ntgt, BLK), jnp.float32)],
-            (order,),
+            (),
             (spread(part, "col"), amass, *cost),
             16,
         )
@@ -310,26 +303,25 @@
                 source_kernel,
                 shape(cols, nsrc, BLK),
                 [pltpu.VMEM((ntgt, BLK), jnp.float32)],
-                (order,),
+                (),
                 (parts, bmass, *cost),
                 16,
             )
     share = src.shape[0] // cols
-    gpot, sums = call(
+    fout, gout, sums = call(
         lambda *refs: map_kernel(len(pieces), *refs),
-        (shape(ntgt, BLK), shape(COLX, COLY * share, width + BLK, dtype=jnp.bfloat16)),
-        [pltpu.VMEM((src.shape[0], ntgt * BLK), jnp.bfloat16)],
-        (order,),
+        (shape(nsrc, BLK), shape(ntgt, BLK), shape(cols, share, width + BLK, dtype=jnp.bfloat16)),
+        [
+            pltpu.VMEM((ntgt, BLK), jnp.float32),
+            pltpu.VMEM((src.shape[0], ntgt * BLK), jnp.bfloat16),
+        ],
+        (),
         (parts, bmass, fpot, *pieces, *cost),
-        32,
+        24,
     )
-    xgroups = [[y * COLX + x for x in range(COLX)] for y in range(COLY)]
-    ygroups = [[y * COLX + x for y in range(COLY)] for x in range(COLX)]
-    sums = spread(sums, "col", xgroups)
-    sums = call(add_kernel, shape(*sums.shape[1:], dtype=jnp.bfloat16), [], (), (sums,), 8)
-    sums = spread(sums.reshape(COLY, share, -1), "col", ygroups)
+    sums = spread(sums, "col")
     mapped = call(divide_kernel, shape(share, width, dtype=jnp.bfloat16), [], (), (sums,), 8)
-    return (fpot.reshape(-1) * UNIT, gpot.reshape(-1) * UNIT, mapped)
+    return (fout.reshape(-1), gout.reshape(-1), mapped)
 
 
 def solution(mesh):

time: 211 us -> 208 us (0.986)
  blocking collectives: 103 us -> 119 us
  waiting for transfers between devices: 26.7 us -> 14 us
  Pallas kernels: 25.5 us -> 16.9 us
  local copies, waits for them, and re-layouts: 3.61 us -> 7.41 us
    all_to_all x7, blocking collectives: 103 us -> 119 us  [spread(): return lax.all_to_all(x, axis, 0, 0, tiled=True, axis_index_groups=groups)]
    all_to_all x2 -> x1, waiting for transfers between devices: 11.2 us -> 0.01 us  [spread(): return lax.all_to_all(x, axis, 0, 0, tiled=True, axis_index_groups=groups)]
    ppermute x9, starting transfers between devices: 34.6 us -> 43.4 us  [move(): return lax.ppermute(x, 'row', pairs)]
    all_to_all x2 -> x1, starting transfers between devices: 13.2 us -> 4.43 us  [spread(): return lax.all_to_all(x, axis, 0, 0, tiled=True, axis_index_groups=groups)]
    pallas_call x11 -> x10, Pallas kernels: 25.5 us -> 16.9 us  [call(): pl.pallas_call(kernel, out_shape=shapes, in_specs=[smem] * len(scalars) +...]
    unnamed x9 -> x27, local copies, waits for them, and re-layouts: 0.99 us -> 4.78 us
  transfers between devices with their start and end apart: 11 -> 10, of which waited for: 5 -> 3; matrix products, arithmetic and copies ran while one was open for 2% -> 1% of each run, Pallas kernels for 4% -> 2%
where the time goes in v3:
time: 208 us; the launch traced here: 207 us
  blocking collectives  119 us (57%)
  starting transfers between devices  47.9 us (23%)
  Pallas kernels  16.9 us (8%)
  waiting for transfers between devices  14 us (7%)
  local copies, waits for them, and re-layouts  7.41 us (4%)
    all_to_all x7, blocking collectives, spread(): return lax.all_to_all(x, axis, 0, 0, tiled=True, axis_index_groups=groups)  119 us
    ppermute x9, starting transfers between devices, move(): return lax.ppermute(x, 'row', pairs)  43.4 us
    pallas_call x10, Pallas kernels, call(): pl.pallas_call(kernel, out_shape=shapes, in_specs=[smem] * len(scalars) +...  16.9 us
    ppermute x9, waiting for transfers between devices, move(): return lax.ppermute(x, 'row', pairs)  14 us
    unnamed x27, local copies, waits for them, and re-layouts  4.78 us
    all_to_all x1, starting transfers between devices, spread(): return lax.all_to_all(x, axis, 0, 0, tiled=True, axis_index_groups=groups)  4.43 us
  transfers between devices with their start and end apart: 10, of which 3 were waited for; matrix products, arithmetic and copies ran while one was open for 1% of the time, Pallas kernels for 2%

profile of v3, /device:TPU:1, one launch (start us, length us, event | category | flops | bytes accessed | tf_op | source)
XLA Modules:
  0.0 207.1 jit_solution(10128800007165763346)
XLA Ops:
  0.6 8.8 %collective-permute-start = (bf16[128,1024]{1,0:T(8,128)(2,1)}, bf16[128,1024]{1,0:T(8,128)(2,1)S(1)}, u32[]{:S(2)}, u32[]{:S(2)}) collective-permute-start(bf16[128,1024]{1,0:T(8,128)(2,1)} %param.8), channel_id=1, source_target_pairs={{0,32},{32,0},{64,96},{96,64},{128,160},{160,128},{192,224},{224,1... | collective-permute-start | bytes 786440 | tf_op jit(solution)/shard_map/ppermute | solution.py:227
  9.4 1.9 broadcast_in_dim.2
  11.3 4.4 %all-to-all-start = ((bf16[32,16,1024]{2,1,0:T(8,128)(2,1)}), bf16[32,16,1024]{2,1,0:T(8,128)(2,1)S(1)}, u32[]{:S(2)}, u32[]{:S(2)}) async-start(bf16[32,16,1024]{2,1,0:T(8,128)(2,1)} %broadcast_in_dim.2), calls=%async_computation | async-start | bytes 2097152 | tf_op jit(solution)/shard_map/all_to_all | solution.py:218
  15.8 10.7 %collective-permute-start.1 = (bf16[256,1024]{1,0:T(8,128)(2,1)S(1)}, bf16[256,1024]{1,0:T(8,128)(2,1)S(1)}, u32[]{:S(2)}, u32[]{:S(2)}) collective-permute-start(bf16[256,1024]{1,0:T(8,128)(2,1)S(1)} %constant_dynamic-update-slice_fusion.refs_4_.refs_3_), channel_id=1, source_target_pairs={{0,64},{32,480},{64,128},{96,32},{128,192},{160,96},{192,256},{224... | collective-permute-start | bytes 1572872 | tf_op jit(solution)/shard_map/ppermute | solution.py:227
  26.5 6.1 %collective-permute-done.1.refs_5_.refs_4_ = bf16[256,1024]{1,0:T(8,128)(2,1)S(1)} collective-permute-done((bf16[256,1024]{1,0:T(8,128)(2,1)S(1)}, bf16[256,1024]{1,0:T(8,128)(2,1)S(1)}, u32[]{:S(2)}, u32[]{:S(2)}) %collective-permute-start.1) | collective-permute-done | bytes 524320 | tf_op jit(solution)/shard_map/ppermute | solution.py:227
  32.6 5.3 %collective-permute-start.2 = (bf16[256,1024]{1,0:T(8,128)(2,1)S(1)}, bf16[256,1024]{1,0:T(8,128)(2,1)S(1)}, u32[]{:S(2)}, u32[]{:S(2)}) collective-permute-start(bf16[256,1024]{1,0:T(8,128)(2,1)S(1)} %collective-permute-done.1.refs_5_.refs_4_), channel_id=1, source_target_pairs={{0,64},{32,480},{64,128},{96,32},{128,192},{160,96},{192,256},{224... | collective-permute-start | bytes 1572872 | tf_op jit(solution)/shard_map/ppermute | solution.py:227
  37.9 6.1 %collective-permute-done.2.refs_7_.refs_6_ = bf16[256,1024]{1,0:T(8,128)(2,1)S(1)} collective-permute-done((bf16[256,1024]{1,0:T(8,128)(2,1)S(1)}, bf16[256,1024]{1,0:T(8,128)(2,1)S(1)}, u32[]{:S(2)}, u32[]{:S(2)}) %collective-permute-start.2) | collective-permute-done | bytes 524320 | tf_op jit(solution)/shard_map/ppermute | solution.py:227
  44.0 5.3 %collective-permute-start.3 = (bf16[256,1024]{1,0:T(8,128)(2,1)S(1)}, bf16[256,1024]{1,0:T(8,128)(2,1)S(1)}, u32[]{:S(2)}, u32[]{:S(2)}) collective-permute-start(bf16[256,1024]{1,0:T(8,128)(2,1)S(1)} %collective-permute-done.2.refs_7_.refs_6_), channel_id=1, source_target_pairs={{0,64},{32,480},{64,128},{96,32},{128,192},{160,96},{192,256},{224... | collective-permute-start | bytes 1572872 | tf_op jit(solution)/shard_map/ppermute | solution.py:227
  49.4 1.9 collective-permute-start.5
  51.3 2.4 %collective-permute-start.6 = (bf16[256,1024]{1,0:T(8,128)(2,1)S(1)}, bf16[256,1024]{1,0:T(8,128)(2,1)S(1)}, u32[]{:S(2)}, u32[]{:S(2)}) collective-permute-start(bf16[256,1024]{1,0:T(8,128)(2,1)S(1)} %collective-permute-done.2.refs_7_.refs_6_), channel_id=1, source_target_pairs={{0,32},{32,0},{64,96},{96,64},{128,160},{160,128},{192,224},{224,1... | collective-permute-start | bytes 1572872 | tf_op jit(solution)/shard_map/ppermute | solution.py:227
  53.7 1.8 collective-permute-done.3.refs_4_.refs_8_
  55.5 5.2 %collective-permute-start.8 = (bf16[256,1024]{1,0:T(8,128)(2,1)S(1)}, bf16[256,1024]{1,0:T(8,128)(2,1)S(1)}, u32[]{:S(2)}, u32[]{:S(2)}) collective-permute-start(bf16[256,1024]{1,0:T(8,128)(2,1)S(1)} %collective-permute-done.3.refs_4_.refs_8_), channel_id=1, source_target_pairs={{0,32},{32,0},{64,96},{96,64},{128,160},{160,128},{192,224},{224,1... | collective-permute-start | bytes 1572872 | tf_op jit(solution)/shard_map/ppermute | solution.py:227
  61.4 1.9 collective-permute-start.4
  65.7 1.0 copy-done.1
  66.7 1.0 copy-done.3
  67.7 1.0 copy-done.6
  68.8 2.7 %shard_map.94 = (f32[512,1280]{1,0:T(8,128)S(1)}, f32[512,128]{1,0:T(8,128)S(1)}) custom-call(s32[32]{0:T(128)S(1)} %bitcast.20, s32[32]{0:T(128)S(1)} %bitcast.23, s32[1]{0:T(128)} %bitcast.8.refs_2_, bf16[512,1024]{1,0:T(8,128)(2,1)S(1)} %bitcast.11, bf16[256,1024]{1,0:T(8,128)(2,1)S(1)} %constant_dynamic-update-slice_fusion.refs_4_.refs_3_, ...), custom_call_target="tpu_custom_call" | custom-call | flops 1342177280 | tf_op jit(solution)/shard_map/pallas_call | solution.py:202
  71.4 1.9 collective-permute-start.7
  73.4 1.5 shard_map.95.refs_8_.refs_1_.refs_13_
  75.0 2.4 %shard_map.96 = (f32[512,256]{1,0:T(8,128)S(1)}, f32[32,4,128]{2,1,0:T(4,128)S(1)}) custom-call(s32[32]{0:T(128)S(1)} %bitcast.22, s32[32]{0:T(128)S(1)} %bitcast.25, s32[1]{0:T(128)} %bitcast.10.refs_2_, bf16[512,1024]{1,0:T(8,128)(2,1)S(1)} %bitcast.13, bf16[128,1024]{1,0:T(8,128)(2,1)S(1)} %collective-permute-done.4.refs_4_.refs_10_, ...), custom_call_target="tpu_custom_call" | custom-call | flops 268435456 | tf_op jit(solution)/shard_map/pallas_call | solution.py:202
  77.3 18.0 %all_to_all.40.parts_ref = f32[32,4,128]{2,1,0:T(4,128)S(1)} all-to-all(f32[32,4,128]{2,1,0:T(4,128)S(1)} %get-tuple-element.20), channel_id=1, replica_groups=mesh['row'=16,'col'=32] {'col'}, dimensions={0} | all-to-all | bytes 131072 | tf_op jit(solution)/shard_map/all_to_all | solution.py:218
  95.4 1.2 shard_map.97
  96.6 15.6 %all_to_all.41.parts_ref = f32[16,16,128]{2,1,0:T(8,128)S(1)} all-to-all(f32[16,16,128]{2,1,0:T(8,128)S(1)} %get-tuple-element.22), channel_id=1, replica_groups=mesh['row'=16,'col'=32] {'row'}, dimensions={0} | all-to-all | bytes 262144 | tf_op jit(solution)/shard_map/all_to_all | solution.py:218
  112.2 1.0 shard_map.98
  113.2 12.3 %all_to_all.42.parts_ref = f32[32,4,128]{2,1,0:T(4,128)S(1)} all-to-all(f32[32,4,128]{2,1,0:T(4,128)S(1)} %shard_map.98), channel_id=1, replica_groups=mesh['row'=16,'col'=32] {'col'}, dimensions={0} | all-to-all | bytes 131072 | tf_op jit(solution)/shard_map/all_to_all | solution.py:218
  125.5 1.2 shard_map.99
  126.7 12.6 %all_to_all.43.parts_ref = f32[16,16,128]{2,1,0:T(8,128)S(1)} all-to-all(f32[16,16,128]{2,1,0:T(8,128)S(1)} %get-tuple-element.23), channel_id=1, replica_groups=mesh['row'=16,'col'=32] {'row'}, dimensions={0} | all-to-all | bytes 262144 | tf_op jit(solution)/shard_map/all_to_all | solution.py:218
  139.3 1.0 shard_map.100
  140.3 12.3 %all_to_all.44.parts_ref = f32[32,4,128]{2,1,0:T(4,128)S(1)} all-to-all(f32[32,4,128]{2,1,0:T(4,128)S(1)} %shard_map.100), channel_id=1, replica_groups=mesh['row'=16,'col'=32] {'col'}, dimensions={0} | all-to-all | bytes 131072 | tf_op jit(solution)/shard_map/all_to_all | solution.py:218
  153.6 12.5 %all_to_all.45.refs_0_ = f32[16,16,128]{2,1,0:T(8,128)S(1)} all-to-all(f32[16,16,128]{2,1,0:T(8,128)S(1)} %get-tuple-element.24), channel_id=1, replica_groups=mesh['row'=16,'col'=32] {'row'}, dimensions={0} | all-to-all | bytes 262144 | tf_op jit(solution)/shard_map/all_to_all | solution.py:218
  166.1 4.1 %shard_map.102 = (f32[4,128]{1,0:T(4,128)}, f32[16,128]{1,0:T(8,128)}, bf16[32,16,1152]{2,1,0:T(8,128)(2,1)S(1)}) custom-call(f32[16,16,128]{2,1,0:T(8,128)S(1)} %all_to_all.45.refs_0_, f32[16,128]{1,0:T(8,128)S(1)} %bitcast.16, f32[4,128]{1,0:T(4,128)S(1)} %get-tuple-element.25.refs_2_, ...), custom_call_target="tpu_custom_call" | custom-call | tf_op jit(solution)/shard_map/pallas_call | solution.py:202
  170.2 36.1 %all_to_all.46.sums_ref = bf16[32,16,1152]{2,1,0:T(8,128)(2,1)S(1)} all-to-all(bf16[32,16,1152]{2,1,0:T(8,128)(2,1)S(1)} %get-tuple-element.28), channel_id=1, replica_groups=mesh['row'=16,'col'=32] {'col'}, dimensions={0} | all-to-all | bytes 2359296 | tf_op jit(solution)/shard_map/all_to_all | solution.py:218
  (35 shorter events, 4.3 us)
Async XLA Ops:
  0.6 15.2 %collective-permute-start = (bf16[128,1024]{1,0:T(8,128)(2,1)}, bf16[128,1024]{1,0:T(8,128)(2,1)S(1)}, u32[]{:S(2)}, u32[]{:S(2)}) collective-permute-start(bf16[128,1024]{1,0:T(8,128)(2,1)} %param.8), channel_id=1, source_target_pairs={{0,32},{32,0},{64,96},{96,64},{128,160},{160,128},{192,224},{224,1... | collective-permute-start | bytes 786440 | tf_op jit(solution)/shard_map/ppermute | solution.py:227
  11.3 4.4 %copy-start.12 = (bf16[128,1024]{1,0:T(8,128)(2,1)S(1)}, bf16[128,1024]{1,0:T(8,128)(2,1)}, u32[]{:S(2)}) copy-start(bf16[128,1024]{1,0:T(8,128)(2,1)} %param.8) | copy-start | bytes 786436
  11.3 54.3 %all-to-all-start = ((bf16[32,16,1024]{2,1,0:T(8,128)(2,1)}), bf16[32,16,1024]{2,1,0:T(8,128)(2,1)S(1)}, u32[]{:S(2)}, u32[]{:S(2)}) async-start(bf16[32,16,1024]{2,1,0:T(8,128)(2,1)} %broadcast_in_dim.2), calls=%async_computation | async-start | bytes 2097152 | tf_op jit(solution)/shard_map/all_to_all | solution.py:218
  15.8 49.9 %copy-start.10 = (s32[1,1,32]{2,1,0:T(1,128)S(1)}, s32[1,1,32]{2,1,0:T(1,128)}, u32[]{:S(2)}) copy-start(s32[1,1,32]{2,1,0:T(1,128)} %param.11) | copy-start | bytes 388
  15.8 49.9 %copy-start.11 = (s32[1,1,32]{2,1,0:T(1,128)S(1)}, s32[1,1,32]{2,1,0:T(1,128)}, u32[]{:S(2)}) copy-start(s32[1,1,32]{2,1,0:T(1,128)} %param.12) | copy-start | bytes 388
  15.8 16.8 %collective-permute-start.1 = (bf16[256,1024]{1,0:T(8,128)(2,1)S(1)}, bf16[256,1024]{1,0:T(8,128)(2,1)S(1)}, u32[]{:S(2)}, u32[]{:S(2)}) collective-permute-start(bf16[256,1024]{1,0:T(8,128)(2,1)S(1)} %constant_dynamic-update-slice_fusion.refs_4_.refs_3_), channel_id=1, source_target_pairs={{0,64},{32,480},{64,128},{96,32},{128,192},{160,96},{192,256},{224... | collective-permute-start | bytes 1572872 | tf_op jit(solution)/shard_map/ppermute | solution.py:227
  32.6 11.4 %collective-permute-start.2 = (bf16[256,1024]{1,0:T(8,128)(2,1)S(1)}, bf16[256,1024]{1,0:T(8,128)(2,1)S(1)}, u32[]{:S(2)}, u32[]{:S(2)}) collective-permute-start(bf16[256,1024]{1,0:T(8,128)(2,1)S(1)} %collective-permute-done.1.refs_5_.refs_4_), channel_id=1, source_target_pairs={{0,64},{32,480},{64,128},{96,32},{128,192},{160,96},{192,256},{224... | collective-permute-start | bytes 1572872 | tf_op jit(solution)/shard_map/ppermute | solution.py:227
  44.0 20.0 %copy-start = (bf16[256,1024]{1,0:T(8,128)(2,1)}, bf16[256,1024]{1,0:T(8,128)(2,1)S(1)}, u32[]{:S(2)}) copy-start(bf16[256,1024]{1,0:T(8,128)(2,1)S(1)} %collective-permute-done.2.refs_7_.refs_6_) | copy-start | bytes 1572868
  44.0 11.4 %collective-permute-start.3 = (bf16[256,1024]{1,0:T(8,128)(2,1)S(1)}, bf16[256,1024]{1,0:T(8,128)(2,1)S(1)}, u32[]{:S(2)}, u32[]{:S(2)}) collective-permute-start(bf16[256,1024]{1,0:T(8,128)(2,1)S(1)} %collective-permute-done.2.refs_7_.refs_6_), channel_id=1, source_target_pairs={{0,64},{32,480},{64,128},{96,32},{128,192},{160,96},{192,256},{224... | collective-permute-start | bytes 1572872 | tf_op jit(solution)/shard_map/ppermute | solution.py:227
  49.4 14.6 %collective-permute-start.5 = (bf16[256,1024]{1,0:T(8,128)(2,1)S(1)}, bf16[256,1024]{1,0:T(8,128)(2,1)S(1)}, u32[]{:S(2)}, u32[]{:S(2)}) collective-permute-start(bf16[256,1024]{1,0:T(8,128)(2,1)S(1)} %collective-permute-done.1.refs_5_.refs_4_), channel_id=1, source_target_pairs={{0,32},{32,0},{64,96},{96,64},{128,160},{160,128},{192,224},{224,1... | collective-permute-start | bytes 1572872 | tf_op jit(solution)/shard_map/ppermute | solution.py:227
  51.3 13.5 %collective-permute-start.6 = (bf16[256,1024]{1,0:T(8,128)(2,1)S(1)}, bf16[256,1024]{1,0:T(8,128)(2,1)S(1)}, u32[]{:S(2)}, u32[]{:S(2)}) collective-permute-start(bf16[256,1024]{1,0:T(8,128)(2,1)S(1)} %collective-permute-done.2.refs_7_.refs_6_), channel_id=1, source_target_pairs={{0,32},{32,0},{64,96},{96,64},{128,160},{160,128},{192,224},{224,1... | collective-permute-start | bytes 1572872 | tf_op jit(solution)/shard_map/ppermute | solution.py:227
  55.5 17.9 %collective-permute-start.8 = (bf16[256,1024]{1,0:T(8,128)(2,1)S(1)}, bf16[256,1024]{1,0:T(8,128)(2,1)S(1)}, u32[]{:S(2)}, u32[]{:S(2)}) collective-permute-start(bf16[256,1024]{1,0:T(8,128)(2,1)S(1)} %collective-permute-done.3.refs_4_.refs_8_), channel_id=1, source_target_pairs={{0,32},{32,0},{64,96},{96,64},{128,160},{160,128},{192,224},{224,1... | collective-permute-start | bytes 1572872 | tf_op jit(solution)/shard_map/ppermute | solution.py:227
  61.4 10.0 %collective-permute-start.4 = (bf16[128,1024]{1,0:T(8,128)(2,1)}, bf16[128,1024]{1,0:T(8,128)(2,1)S(1)}, u32[]{:S(2)}, u32[]{:S(2)}) collective-permute-start(bf16[128,1024]{1,0:T(8,128)(2,1)} %slice.4), channel_id=1, source_target_pairs={{0,64},{32,480},{64,128},{96,32},{128,192},{160,96},{192,256},{224... | collective-permute-start | bytes 786440 | tf_op jit(solution)/shard_map/ppermute | solution.py:227
  64.0 0.8 copy-start.2
  64.8 0.8 copy-start.5
  65.6 1.0 copy-start.1
  66.7 1.0 copy-start.3
  67.7 1.0 copy-start.6
  71.4 3.5 %collective-permute-start.7 = (bf16[128,1024]{1,0:T(8,128)(2,1)S(1)}, bf16[128,1024]{1,0:T(8,128)(2,1)S(1)}, u32[]{:S(2)}, u32[]{:S(2)}) collective-permute-start(bf16[128,1024]{1,0:T(8,128)(2,1)S(1)} %collective-permute-done.4.refs_4_.refs_10_), channel_id=1, source_target_pairs={{0,32},{32,0},{64,96},{96,64},{128,160},{160,128},{192,224},{224,1... | collective-permute-start | bytes 786440 | tf_op jit(solution)/shard_map/ppermute | solution.py:227
  75.0 20.4 %copy-start.9 = (f32[512]{0:T(512)S(1)}, f32[512]{0:T(512)}, u32[]{:S(2)}) copy-start(f32[512]{0:T(512)} %param.9) | copy-start | bytes 6148
  95.4 16.8 %copy-start.8 = (f32[2048]{0:T(1024)S(1)}, f32[2048]{0:T(1024)}, u32[]{:S(2)}) copy-start(f32[2048]{0:T(1024)} %param.10) | copy-start | bytes 24580
  152.6 13.5 %copy-start.4 = (bf16[256,1024]{1,0:T(8,128)(2,1)S(1)}, bf16[256,1024]{1,0:T(8,128)(2,1)}, u32[]{:S(2)}) copy-start(bf16[256,1024]{1,0:T(8,128)(2,1)} %copy-done.2) | copy-start | bytes 1572868
  152.6 13.5 %copy-start.7 = (bf16[256,1024]{1,0:T(8,128)(2,1)S(1)}, bf16[256,1024]{1,0:T(8,128)(2,1)}, u32[]{:S(2)}) copy-start(bf16[256,1024]{1,0:T(8,128)(2,1)} %copy-done.5) | copy-start | bytes 1572868

commit v4 on v1

v4 whole, which is shorter than its diff:
```python
import math

import jax
import jax.numpy as jnp
from jax import lax
from jax.experimental import pallas as pl
from jax.experimental.pallas import tpu as pltpu
from jax.sharding import PartitionSpec as P

BLK = 128
ITERS = 3
EPS = 0.02
UNIT = EPS * math.log(2.0)
FAR = 1e30
MIB = 1 << 20
CHUNK = 256


def nt_dot(a, b):
    return lax.dot_general(a, b, (((1,), (1,)), ((), ())), preferred_element_type=jnp.float32)


def square_sums(rows):
    rows = rows.astype(jnp.float32)
    rows = rows * rows
    total = rows[:, :BLK]
    for d in range(BLK, rows.shape[1], BLK):
        total = total + rows[:, d : d + BLK]
    return total


def lanes_of(row):
    return jnp.transpose(jnp.broadcast_to(row, (BLK, BLK)))


def finish_rows(peak, total):
    peak, total = jnp.transpose(peak), jnp.transpose(total)
    top = jnp.max(peak, axis=0, keepdims=True)
    return top + jnp.log2(jnp.sum(total * jnp.exp2(peak - top), axis=0, keepdims=True))


def source_parts(cost_ref, pot, part_ref):
    count = cost_ref.shape[1] // BLK
    for s in range(cost_ref.shape[0] // BLK):
        at = slice(s * BLK, (s + 1) * BLK)

        def gap(n):
            cost = cost_ref[at, n * BLK : (n + 1) * BLK]
            return -cost if pot is None else pot[n : n + 1, :] - cost

        peak = gap(0)
        for n in range(1, count):
            peak = jnp.maximum(peak, gap(n))
        total = jnp.exp2(gap(0) - peak)
        for n in range(1, count):
            total = total + jnp.exp2(gap(n) - peak)
        row = finish_rows(peak, total)
        for k in range(part_ref.shape[0]):
            part_ref[k, s : s + 1, :] = row


def prepare_kernel(sidx, tidx, live, src_ref, norm_ref, far_ref):
    nsrc = src_ref.shape[0] // BLK
    ntgt = far_ref.shape[0] // nsrc
    scale = 1.0 / (src_ref.shape[1] * UNIT)
    far_ref[...] = jnp.full_like(far_ref, FAR)

    def mark(k, c):
        far_ref[pl.ds(sidx[k] * ntgt + tidx[k], 1), :] = jnp.zeros((1, BLK), jnp.float32)
        return c

    lax.fori_loop(0, live[0], mark, 0)
    for s in range(nsrc):
        at = slice(s * BLK, (s + 1) * BLK)
        norm = jnp.sum(square_sums(src_ref[at, :]), axis=1, keepdims=True) * scale
        norm_ref[at, :] = jnp.broadcast_to(norm, (BLK, BLK))


def cost_kernel(src_ref, norm_ref, far_ref, tgt_ref, cost_ref, part_ref, tgt, sems):
    nsrc, ntgt = src_ref.shape[0] // BLK, tgt_ref.shape[0] // BLK
    scale = 1.0 / (src_ref.shape[1] * UNIT)
    chunks = tgt_ref.shape[0] // CHUNK

    def chunk(k):
        at = pl.ds(k * CHUNK, CHUNK)
        return pltpu.make_async_copy(tgt_ref.at[at, :], tgt.at[at, :], sems.at[k])

    for k in range(chunks):
        chunk(k).start()
    for k in range(chunks):
        chunk(k).wait()
        cross = nt_dot(src_ref[...], tgt[k * CHUNK : (k + 1) * CHUNK, :]) * (-2.0 * scale)
        for d in range(0, CHUNK, BLK):
            lane = k * CHUNK + d
            sums = jnp.transpose(square_sums(tgt[lane : lane + BLK, :]))
            norm = jnp.sum(sums, axis=0, keepdims=True) * scale
            for s in range(nsrc):
                at = slice(s * BLK, (s + 1) * BLK)
                n = s * ntgt + lane // BLK
                away = norm + far_ref[n : n + 1, :]
                cost_ref[at, lane : lane + BLK] = cross[at, d : d + BLK] + norm_ref[at, :] + away
    source_parts(cost_ref, None, part_ref)


def combine(mass_ref, parts_ref):
    parts = parts_ref[...]
    top = jnp.max(parts, axis=0)
    low = jnp.log2(jnp.sum(jnp.exp2(parts - top[None]), axis=0))
    return jnp.log2(mass_ref[...]) - (top + low)


def target_kernel(parts_ref, mass_ref, cost_ref, pot_ref, part_ref, wide, mine):
    pot = combine(mass_ref, parts_ref)
    pot_ref[...] = pot
    for s in range(pot.shape[0]):
        wide[s * BLK : (s + 1) * BLK, :] = lanes_of(pot[s : s + 1, :])
    for n in range(cost_ref.shape[1] // BLK):
        gap = (wide[...] - cost_ref[:, n * BLK : (n + 1) * BLK]).reshape(-1, 8, BLK)
        peak = jnp.max(gap, axis=0)
        top = jnp.max(peak, axis=0, keepdims=True)
        total = jnp.sum(jnp.exp2(gap - top[None]), axis=0)
        mine[n : n + 1, :] = top + jnp.log2(jnp.sum(total, axis=0, keepdims=True))
    part_ref[...] = jnp.broadcast_to(mine[...][None], part_ref.shape)


def source_kernel(parts_ref, mass_ref, cost_ref, part_ref):
    source_parts(cost_ref, combine(mass_ref, parts_ref), part_ref)


def map_kernel(parts_ref, mass_ref, fpot_ref, tgt_ref, cost_ref, pot_ref, sums_ref, weight):
    pot = combine(mass_ref, parts_ref)
    pot_ref[...] = pot
    width = tgt_ref.shape[1]
    for s in range(fpot_ref.shape[0]):
        at = slice(s * BLK, (s + 1) * BLK)
        mine = lanes_of(fpot_ref[s : s + 1, :])
        for n in range(pot.shape[0]):
            lanes = slice(n * BLK, (n + 1) * BLK)
            power = jnp.exp2(mine + pot[n : n + 1, :] - cost_ref[at, lanes])
            weight[at, lanes] = power.astype(jnp.bfloat16)
    for d in range(0, width, CHUNK):
        part = jnp.dot(weight[...], tgt_ref[:, d : d + CHUNK], preferred_element_type=jnp.float32)
        sums_ref[:, d : d + CHUNK] = part.astype(jnp.bfloat16)
    ones = jnp.ones((weight.shape[1], BLK), jnp.bfloat16)
    total = jnp.dot(weight[...], ones, preferred_element_type=jnp.float32)
    sums_ref[:, width:] = two_pieces(total)


def two_pieces(total):
    high = total.astype(jnp.bfloat16).astype(jnp.float32)
    lane = lax.broadcasted_iota(jnp.int32, total.shape, 1)
    return jnp.where(lane == 0, high, total - high).astype(jnp.bfloat16)


def add_up(sums_ref):
    sums = sums_ref[0].astype(jnp.float32)
    for k in range(1, sums_ref.shape[0]):
        sums = sums + sums_ref[k].astype(jnp.float32)
    return sums


def divide_kernel(sums_ref, out_ref):
    width = out_ref.shape[1]
    sums = add_up(sums_ref)
    total = sums[:, width : width + 1] + sums[:, width + 1 : width + 2]
    out_ref[...] = (sums[:, :width] / total).astype(out_ref.dtype)


def call(kernel, shapes, scratch, args, limit, specs=None):
    vmem = pl.BlockSpec(memory_space=pltpu.VMEM)
    return pl.pallas_call(
        kernel,
        out_shape=shapes,
        in_specs=specs or [vmem] * len(args),
        out_specs=jax.tree.map(lambda _: vmem, shapes),
        scratch_shapes=scratch,
        compiler_params=pltpu.CompilerParams(vmem_limit_bytes=limit * MIB),
    )(*args)


def shape(*dims, dtype=jnp.float32):
    return jax.ShapeDtypeStruct(dims, dtype)


def spread(x, axis):
    return lax.all_to_all(x, axis, 0, 0, tiled=True)


def body(source, target, source_mass, target_mass, tile_src, tile_dst, tile_count):
    rows, cols = lax.axis_size("row"), lax.axis_size("col")
    width = source.shape[1]
    tgt = lax.all_gather(target, "row", axis=0, tiled=True)
    src = spread(jnp.broadcast_to(source[None], (cols, *source.shape)), "col")
    src = src.reshape(-1, width)
    nsrc, ntgt = src.shape[0] // BLK, tgt.shape[0] // BLK
    amass = source_mass.reshape(nsrc, BLK)
    bmass = target_mass.reshape(ntgt, BLK)
    vmem, smem = (pl.BlockSpec(memory_space=space) for space in (pltpu.VMEM, pltpu.SMEM))
    norm, far = call(
        prepare_kernel,
        (shape(src.shape[0], BLK), shape(nsrc * ntgt, BLK)),
        [],
        (tile_src.reshape(-1), tile_dst.reshape(-1), tile_count.reshape(-1), src),
        8,
        [smem, smem, smem, vmem],
    )
    cost, part = call(
        cost_kernel,
        (shape(src.shape[0], tgt.shape[0]), shape(cols, nsrc, BLK)),
        [pltpu.VMEM(tgt.shape, tgt.dtype), pltpu.SemaphoreType.DMA((tgt.shape[0] // CHUNK,))],
        (src, norm, far, tgt),
        46,
        [vmem, vmem, vmem, pl.BlockSpec(memory_space=pl.ANY)],
    )
    for step in range(ITERS):
        fpot, part = call(
            target_kernel,
            (shape(nsrc, BLK), shape(rows, ntgt, BLK)),
            [pltpu.VMEM((src.shape[0], BLK), jnp.float32), pltpu.VMEM((ntgt, BLK), jnp.float32)],
            (spread(part, "col"), amass, cost),
            16,
        )
        parts = spread(part, "row")
        if step < ITERS - 1:
            part = call(source_kernel, shape(cols, nsrc, BLK), [], (parts, bmass, cost), 16)
    gpot, sums = call(
        map_kernel,
        (shape(ntgt, BLK), shape(src.shape[0], width + BLK, dtype=jnp.bfloat16)),
        [pltpu.VMEM(cost.shape, jnp.bfloat16)],
        (parts, bmass, fpot, tgt, cost),
        32,
    )
    share = src.shape[0] // cols
    sums = spread(sums.reshape(cols, share, -1), "col")
    mapped = call(divide_kernel, shape(share, width, dtype=jnp.bfloat16), [], (sums,), 8)
    return (fpot.reshape(-1) * UNIT, gpot.reshape(-1) * UNIT, mapped)


def solution(mesh):
    in_specs = (
        P(("row", "col"), None),
        P(("col", "row"), None),
        P("row"),
        P("col"),
        P("row", "col", None),
        P("row", "col", None),
        P("row", "col"),
    )
    out_specs = (P("row"), P("col"), P(("row", "col"), None))
    return jax.shard_map(body, mesh=mesh, in_specs=in_specs, out_specs=out_specs, check_vma=False)
```

time: 211 us -> 204 us (0.967)
  Pallas kernels: 21.1 us -> 18.6 us
  waiting for transfers between devices: 71.2 us -> 68.8 us
  local copies, waits for them, and re-layouts: 5.38 us -> 3.19 us
    pallas_call x8 -> x9, Pallas kernels: 21.1 us -> 18.6 us  [call(): pl.pallas_call(kernel, out_shape=shapes, in_specs=specs or [vmem] * len(a...]
    all_gather x1, waiting for transfers between devices: 15.2 us -> 12.8 us  [body(): tgt = lax.all_gather(target, 'row', axis=0, tiled=True)]
    unnamed x12 -> x10, local copies, waits for them, and re-layouts: 3.51 us -> 1.32 us
where the time goes in v4:
time: 204 us
  blocking collectives  82.5 us (40%)
  waiting for transfers between devices  68.8 us (34%)
  Pallas kernels  18.6 us (9%)
  between operations  14.7 us (7%)
  starting transfers between devices  14.6 us (7%)
  local copies, waits for them, and re-layouts  3.19 us (2%)
    all_to_all x6, blocking collectives, spread(): return lax.all_to_all(x, axis, 0, 0, tiled=True)  82.5 us
    all_to_all x2, waiting for transfers between devices, spread(): return lax.all_to_all(x, axis, 0, 0, tiled=True)  55.3 us
    pallas_call x9, Pallas kernels, call(): pl.pallas_call(kernel, out_shape=shapes, in_specs=specs or [vmem] * len(a...  18.6 us
    all_to_all x2, starting transfers between devices, spread(): return lax.all_to_all(x, axis, 0, 0, tiled=True)  14.6 us
    all_gather x1, waiting for transfers between devices, body(): tgt = lax.all_gather(target, 'row', axis=0, tiled=True)  12.8 us
  transfers between devices with their start and end apart: 3, of which 3 were waited for; matrix products, arithmetic and copies ran while one was open for 1% of the time, Pallas kernels for 0%

profile of v4, /device:TPU:1, one launch (start us, length us, event | category | flops | bytes accessed | tf_op | source)
XLA Modules:
  0.0 203.6 jit_solution(5909970440622263365)
XLA Ops:
  7.2 0.0 all-gather.2.cloned.1.call-start
  7.2 0.7 all-gather.2.cloned.1.call-update
  7.9 1.9 broadcast_in_dim.2
  9.8 0.0 copy-start.2
  9.8 10.6 %all-to-all-start = ((bf16[32,16,1024]{2,1,0:T(8,128)(2,1)}), bf16[32,16,1024]{2,1,0:T(8,128)(2,1)S(1)}, u32[]{:S(2)}, u32[]{:S(2)}) async-start(bf16[32,16,1024]{2,1,0:T(8,128)(2,1)} %broadcast_in_dim.2), calls=%async_computation | async-start | bytes 2097152 | tf_op jit(solution)/shard_map/all_to_all | solution.py:186
  21.1 25.6 %all-to-all-done = bf16[32,16,1024]{2,1,0:T(8,128)(2,1)S(1)} async-done(((bf16[32,16,1024]{2,1,0:T(8,128)(2,1)}), bf16[32,16,1024]{2,1,0:T(8,128)(2,1)S(1)}, u32[]{:S(2)}, u32[]{:S(2)}) %all-to-all-start) | async-done | bytes 1048608 | tf_op jit(solution)/shard_map/all_to_all | solution.py:186
  46.6 0.0 copy-start.3
  46.6 0.7 copy-done.3
  47.3 0.7 copy-done.4
  47.9 1.0 shard_map.94
  48.9 12.8 %all-gather.2.cloned.1.call-done.tgt_ref = bf16[2048,1024]{1,0:T(8,128)(2,1)} async-done(((bf16[128,1024]{1,0:T(8,128)(2,1)}), bf16[2048,1024]{1,0:T(8,128)(2,1)}) %all-gather.2.cloned.1.call-update) | async-done | bytes 4194320 | tf_op jit(solution)/shard_map/all_gather | solution.py:192
  61.7 7.8 %shard_map.95 = (f32[512,2048]{1,0:T(8,128)S(1)}, f32[32,4,128]{2,1,0:T(4,128)S(1)}) custom-call(bf16[512,1024]{1,0:T(8,128)(2,1)S(1)} %bitcast.13, f32[512,128]{1,0:T(8,128)S(1)} %get-tuple-element.13.norm_ref, f32[64,128]{1,0:T(8,128)S(1)} %get-tuple-element.14.far_ref, bf16[2048,1024]{1,0:T(8,128)(2,1)} %all-gather.2.cloned.1.call-done.tgt_ref), custom_call_target="tpu_custom_call" | custom-call | tf_op jit(solution)/shard_map/pallas_call | solution.py:171
  69.6 17.9 %all_to_all.40.parts_ref = f32[32,4,128]{2,1,0:T(4,128)S(1)} all-to-all(f32[32,4,128]{2,1,0:T(4,128)S(1)} %get-tuple-element.15), channel_id=1, replica_groups=mesh['row'=16,'col'=32] {'col'}, dimensions={0} | all-to-all | bytes 131072 | tf_op jit(solution)/shard_map/all_to_all | solution.py:186
  87.5 0.0 copy-done.2
  87.5 0.9 shard_map.96
  88.4 14.7 %all_to_all.41.parts_ref = f32[16,16,128]{2,1,0:T(8,128)S(1)} all-to-all(f32[16,16,128]{2,1,0:T(8,128)S(1)} %get-tuple-element.17), channel_id=1, replica_groups=mesh['row'=16,'col'=32] {'row'}, dimensions={0} | all-to-all | bytes 262144 | tf_op jit(solution)/shard_map/all_to_all | solution.py:186
  103.2 0.0 copy-done.1
  103.2 0.9 shard_map.97
  104.1 12.3 %all_to_all.42.parts_ref = f32[32,4,128]{2,1,0:T(4,128)S(1)} all-to-all(f32[32,4,128]{2,1,0:T(4,128)S(1)} %shard_map.97), channel_id=1, replica_groups=mesh['row'=16,'col'=32] {'col'}, dimensions={0} | all-to-all | bytes 131072 | tf_op jit(solution)/shard_map/all_to_all | solution.py:186
  116.4 0.9 shard_map.98
  117.3 12.5 %all_to_all.43.parts_ref = f32[16,16,128]{2,1,0:T(8,128)S(1)} all-to-all(f32[16,16,128]{2,1,0:T(8,128)S(1)} %get-tuple-element.18), channel_id=1, replica_groups=mesh['row'=16,'col'=32] {'row'}, dimensions={0} | all-to-all | bytes 262144 | tf_op jit(solution)/shard_map/all_to_all | solution.py:186
  129.9 0.9 shard_map.99
  130.8 12.4 %all_to_all.44.parts_ref = f32[32,4,128]{2,1,0:T(4,128)S(1)} all-to-all(f32[32,4,128]{2,1,0:T(4,128)S(1)} %shard_map.99), channel_id=1, replica_groups=mesh['row'=16,'col'=32] {'col'}, dimensions={0} | all-to-all | bytes 131072 | tf_op jit(solution)/shard_map/all_to_all | solution.py:186
  143.2 0.9 shard_map.100
  144.1 12.5 %all_to_all.45.parts_ref = f32[16,16,128]{2,1,0:T(8,128)S(1)} all-to-all(f32[16,16,128]{2,1,0:T(8,128)S(1)} %get-tuple-element.20), channel_id=1, replica_groups=mesh['row'=16,'col'=32] {'row'}, dimensions={0} | all-to-all | bytes 262144 | tf_op jit(solution)/shard_map/all_to_all | solution.py:186
  156.7 0.0 copy-done
  156.7 4.4 %shard_map.101 = (f32[16,128]{1,0:T(8,128)S(1)}, bf16[512,1152]{1,0:T(8,128)(2,1)}) custom-call(f32[16,16,128]{2,1,0:T(8,128)S(1)} %all_to_all.45.parts_ref, f32[16,128]{1,0:T(8,128)S(1)} %bitcast.16, f32[4,128]{1,0:T(4,128)S(1)} %get-tuple-element.19.fpot_ref, bf16[2048,1024]{1,0:T(8,128)(2,1)S(1)} %copy-done, f32[512,2048]{1,0:T(8,128)S(1)} %get-tuple-element.16.cost_ref), custom_call_target="tpu_custom_call" | custom-call | tf_op jit(solution)/shard_map/pallas_call | solution.py:171
  161.1 3.9 %all-to-all-start.7 = ((bf16[32,16,1152]{2,1,0:T(8,128)(2,1)}), bf16[32,16,1152]{2,1,0:T(8,128)(2,1)S(1)}, u32[]{:S(2)}, u32[]{:S(2)}) async-start(bf16[32,16,1152]{2,1,0:T(8,128)(2,1)} %bitcast.8), calls=%async_computation.7 | async-start | bytes 2359296 | tf_op jit(solution)/shard_map/all_to_all | solution.py:186
  165.0 0.6 multiply_bitcast_fusion.1
  165.6 0.6 multiply_bitcast_fusion
  166.2 29.7 %all-to-all-done.7.sums_ref = bf16[32,16,1152]{2,1,0:T(8,128)(2,1)S(1)} async-done(((bf16[32,16,1152]{2,1,0:T(8,128)(2,1)}), bf16[32,16,1152]{2,1,0:T(8,128)(2,1)S(1)}, u32[]{:S(2)}, u32[]{:S(2)}) %all-to-all-start.7) | async-done | bytes 1179680 | tf_op jit(solution)/shard_map/all_to_all | solution.py:186
  195.9 0.8 shard_map.102
  (3 shorter events, 0.0 us)
Async XLA Ops:
  7.2 54.6 %all-gather.2.cloned.1.call-start = ((), (), s32[]{:S(2)}) async-start(), calls=%async_computation.8 | async-start | bytes 4456448 | tf_op jit(solution)/shard_map/all_gather | solution.py:192
  9.8 77.7 %copy-start.2 = (f32[512]{0:T(512)S(1)}, f32[512]{0:T(512)}, u32[]{:S(2)}) copy-start(f32[512]{0:T(512)} %param.9) | copy-start | bytes 6148
  9.8 36.8 %all-to-all-start = ((bf16[32,16,1024]{2,1,0:T(8,128)(2,1)}), bf16[32,16,1024]{2,1,0:T(8,128)(2,1)S(1)}, u32[]{:S(2)}, u32[]{:S(2)}) async-start(bf16[32,16,1024]{2,1,0:T(8,128)(2,1)} %broadcast_in_dim.2), calls=%async_computation | async-start | bytes 2097152 | tf_op jit(solution)/shard_map/all_to_all | solution.py:186
  46.6 0.7 copy-start.3
  47.3 0.7 copy-start.4
  61.7 41.4 %copy-start.1 = (f32[2048]{0:T(1024)S(1)}, f32[2048]{0:T(1024)}, u32[]{:S(2)}) copy-start(f32[2048]{0:T(1024)} %param.10) | copy-start | bytes 24580
  129.9 26.8 %copy-start = (bf16[2048,1024]{1,0:T(8,128)(2,1)S(1)}, bf16[2048,1024]{1,0:T(8,128)(2,1)}, u32[]{:S(2)}) copy-start(bf16[2048,1024]{1,0:T(8,128)(2,1)} %all-gather.2.cloned.1.call-done.tgt_ref) | copy-start | bytes 12582916
  161.1 34.8 %all-to-all-start.7 = ((bf16[32,16,1152]{2,1,0:T(8,128)(2,1)}), bf16[32,16,1152]{2,1,0:T(8,128)(2,1)S(1)}, u32[]{:S(2)}, u32[]{:S(2)}) async-start(bf16[32,16,1152]{2,1,0:T(8,128)(2,1)} %bitcast.8), calls=%async_computation.7 | async-start | bytes 2359296 | tf_op jit(solution)/shard_map/all_to_all | solution.py:186
Sparse Core Ops, SparseCore 0:
  10.1 51.5 all-gather.1

commit v5 on v4

v5 whole, which is shorter than its diff:
```python
import math

import jax
import jax.numpy as jnp
from jax import lax
from jax.experimental import pallas as pl
from jax.experimental.pallas import tpu as pltpu
from jax.sharding import PartitionSpec as P

BLK = 128
ITERS = 3
EPS = 0.02
UNIT = EPS * math.log(2.0)
FAR = 1e30
MIB = 1 << 20
CHIPS, CORES = 8, 2
CHUNK = 256


def nt_dot(a, b):
    return lax.dot_general(a, b, (((1,), (1,)), ((), ())), preferred_element_type=jnp.float32)


def square_sums(rows):
    rows = rows.astype(jnp.float32)
    rows = rows * rows
    total = rows[:, :BLK]
    for d in range(BLK, rows.shape[1], BLK):
        total = total + rows[:, d : d + BLK]
    return total


def lanes_of(row):
    return jnp.transpose(jnp.broadcast_to(row, (BLK, BLK)))


def finish_rows(peak, total):
    peak, total = jnp.transpose(peak), jnp.transpose(total)
    top = jnp.max(peak, axis=0, keepdims=True)
    return top + jnp.log2(jnp.sum(total * jnp.exp2(peak - top), axis=0, keepdims=True))


def tiles_of(cost_refs):
    return [(ref, slice(d, d + BLK)) for ref in cost_refs for d in range(0, ref.shape[1], BLK)]


def source_parts(cost_refs, rows, part_ref):
    tiles = tiles_of(cost_refs)
    for s in range(cost_refs[0].shape[0] // BLK):
        at = slice(s * BLK, (s + 1) * BLK)

        def gap(n):
            ref, lanes = tiles[n]
            return -ref[at, lanes] if rows is None else rows[n] - ref[at, lanes]

        peak = gap(0)
        for n in range(1, len(tiles)):
            peak = jnp.maximum(peak, gap(n))
        total = jnp.exp2(gap(0) - peak)
        for n in range(1, len(tiles)):
            total = total + jnp.exp2(gap(n) - peak)
        row = finish_rows(peak, total)
        for k in range(part_ref.shape[0]):
            part_ref[k, s : s + 1, :] = row


def prepare_kernel(sidx, tidx, live, src_ref, norm_ref, far_ref, slot):
    nsrc = src_ref.shape[0] // BLK
    ntgt = far_ref.shape[0] // nsrc
    scale = 1.0 / (src_ref.shape[1] * UNIT)
    for n, cluster in enumerate(held_order()):
        slot[cluster] = n
    far_ref[...] = jnp.full_like(far_ref, FAR)

    def mark(k, c):
        far_ref[pl.ds(sidx[k] * ntgt + slot[tidx[k]], 1), :] = jnp.zeros((1, BLK), jnp.float32)
        return c

    lax.fori_loop(0, live[0], mark, 0)
    for s in range(nsrc):
        at = slice(s * BLK, (s + 1) * BLK)
        norm = jnp.sum(square_sums(src_ref[at, :]), axis=1, keepdims=True) * scale
        norm_ref[at, :] = jnp.broadcast_to(norm, (BLK, BLK))


def cost_kernel(first, npiece, nheld, src_ref, norm_ref, far_ref, *refs):
    pieces, held, (cost_ref, *more) = refs[:npiece], refs[npiece : npiece + nheld], refs[npiece + nheld :]
    nsrc = src_ref.shape[0] // BLK
    ntgt = far_ref.shape[0] // nsrc
    scale = 1.0 / (src_ref.shape[1] * UNIT)
    lane = 0
    for piece in pieces:
        for row in range(0, piece.shape[0], CHUNK):
            block = piece[row : row + CHUNK, :]
            cross = nt_dot(src_ref[...], block) * (-2.0 * scale)
            for d in range(0, block.shape[0], BLK):
                sums = jnp.transpose(square_sums(block[d : d + BLK, :]))
                norm = jnp.sum(sums, axis=0, keepdims=True) * scale
                for s in range(nsrc):
                    at = slice(s * BLK, (s + 1) * BLK)
                    n = s * ntgt + first + lane // BLK
                    away = norm + far_ref[n : n + 1, :]
                    tile = cross[at, d : d + BLK] + norm_ref[at, :] + away
                    cost_ref[at, lane : lane + BLK] = tile
                lane += BLK
    if more:
        source_parts([*held, cost_ref], None, more[0])


def combine(mass_ref, parts_ref):
    parts = parts_ref[...]
    top = jnp.max(parts, axis=0)
    low = jnp.log2(jnp.sum(jnp.exp2(parts - top[None]), axis=0))
    return jnp.log2(mass_ref[...]) - (top + low)


def target_kernel(parts_ref, mass_ref, *refs):
    *cost_refs, pot_ref, part_ref, wide, mine = refs
    order = held_order()
    pot = combine(mass_ref, parts_ref)
    pot_ref[...] = pot
    for s in range(pot.shape[0]):
        wide[s * BLK : (s + 1) * BLK, :] = lanes_of(pot[s : s + 1, :])
    for n, (ref, lanes) in enumerate(tiles_of(cost_refs)):
        gap = (wide[...] - ref[:, lanes]).reshape(-1, 8, BLK)
        peak = jnp.max(gap, axis=0)
        top = jnp.max(peak, axis=0, keepdims=True)
        total = jnp.sum(jnp.exp2(gap - top[None]), axis=0)
        mine[pl.ds(order[n], 1), :] = top + jnp.log2(jnp.sum(total, axis=0, keepdims=True))
    part_ref[...] = jnp.broadcast_to(mine[...][None], part_ref.shape)


def held_rows(pot_ref):
    return [pot_ref[pl.ds(cluster, 1), :] for cluster in held_order()]


def source_kernel(parts_ref, mass_ref, *refs):
    *cost_refs, part_ref, pot_ref = refs
    pot_ref[...] = combine(mass_ref, parts_ref)
    source_parts(cost_refs, held_rows(pot_ref), part_ref)


def map_kernel(npiece, parts_ref, mass_ref, fpot_ref, *refs):
    pieces, (*cost_refs, pot_ref, sums_ref, weight) = refs[:npiece], refs[npiece:]
    pot_ref[...] = combine(mass_ref, parts_ref)
    rows = held_rows(pot_ref)
    width = pieces[0].shape[1]
    for s in range(fpot_ref.shape[0]):
        at = slice(s * BLK, (s + 1) * BLK)
        mine = lanes_of(fpot_ref[s : s + 1, :])
        for n, (ref, lanes) in enumerate(tiles_of(cost_refs)):
            power = jnp.exp2(mine + rows[n] - ref[at, lanes])
            weight[at, n * BLK : (n + 1) * BLK] = power.astype(jnp.bfloat16)
    for d in range(0, width, CHUNK):
        part, lane = None, 0
        for piece in pieces:
            low = weight[:, lane : lane + piece.shape[0]]
            add = jnp.dot(low, piece[:, d : d + CHUNK], preferred_element_type=jnp.float32)
            part = add if part is None else part + add
            lane += piece.shape[0]
        sums_ref[:, d : d + CHUNK] = part.astype(jnp.bfloat16)
    ones = jnp.ones((weight.shape[1], BLK), jnp.bfloat16)
    total = jnp.dot(weight[...], ones, preferred_element_type=jnp.float32)
    sums_ref[:, width:] = two_pieces(total)


def two_pieces(total):
    high = total.astype(jnp.bfloat16).astype(jnp.float32)
    lane = lax.broadcasted_iota(jnp.int32, total.shape, 1)
    return jnp.where(lane == 0, high, total - high).astype(jnp.bfloat16)


def add_up(sums_ref):
    sums = sums_ref[0].astype(jnp.float32)
    for k in range(1, sums_ref.shape[0]):
        sums = sums + sums_ref[k].astype(jnp.float32)
    return sums


def divide_kernel(sums_ref, out_ref):
    width = out_ref.shape[1]
    sums = add_up(sums_ref)
    total = sums[:, width : width + 1] + sums[:, width + 1 : width + 2]
    out_ref[...] = (sums[:, :width] / total).astype(out_ref.dtype)


def call(kernel, shapes, scratch, args, limit, specs=None):
    vmem = pl.BlockSpec(memory_space=pltpu.VMEM)
    return pl.pallas_call(
        kernel,
        out_shape=shapes,
        in_specs=specs or [vmem] * len(args),
        out_specs=jax.tree.map(lambda _: vmem, shapes),
        scratch_shapes=scratch,
        compiler_params=pltpu.CompilerParams(vmem_limit_bytes=limit * MIB),
    )(*args)


def shape(*dims, dtype=jnp.float32):
    return jax.ShapeDtypeStruct(dims, dtype)


def spread(x, axis):
    return lax.all_to_all(x, axis, 0, 0, tiled=True)


def move(x, place):
    pairs = []
    for z in range(CHIPS):
        for c in range(CORES):
            to = place(z, c)
            pairs.append((z * CORES + c, to[0] % CHIPS * CORES + to[1]))
    return lax.ppermute(x, "row", pairs)


def ring(x):
    return move(x, lambda z, c: (z + 1 - 2 * c, c))


def partner(x):
    return move(x, lambda z, c: (z, 1 - c))


def held_order():
    row = lax.axis_index("row")
    z, c = row // CORES, row % CORES
    way = 2 * c - 1

    def pair(k, core):
        chip = (z + way * k + CHIPS) % CHIPS
        return [chip * CORES + core, chip * CORES + 1 - core]

    return [
        *pair(0, c),
        *pair(1, c),
        *pair(2, c),
        *pair(-1, 1 - c),
        *pair(-2, 1 - c),
        *pair(3, c),
        *pair(-3, 1 - c),
        *pair(4, c),
    ]


def body(source, target, source_mass, target_mass, tile_src, tile_dst, tile_count):
    rows, cols = lax.axis_size("row"), lax.axis_size("col")
    width = source.shape[1]
    nsrc, ntgt = source_mass.shape[0] // BLK, target_mass.shape[0] // BLK
    near = partner(target)
    one, near_one = ring(target), ring(near)
    src = spread(jnp.broadcast_to(source[None], (cols, *source.shape)), "col")
    src = src.reshape(-1, width)
    two, near_two = ring(one), ring(near_one)
    three, near_three = ring(two), ring(near_two)
    own = jnp.concatenate([target, near])
    early = jnp.concatenate([one, near_one, two, near_two])
    late = jnp.concatenate([three, near_three])
    early_other = partner(early)
    last = ring(three)
    late_other = partner(late)
    amass = source_mass.reshape(nsrc, BLK)
    bmass = target_mass.reshape(ntgt, BLK)
    vmem, smem = (pl.BlockSpec(memory_space=space) for space in (pltpu.VMEM, pltpu.SMEM))
    norm, far = call(
        prepare_kernel,
        (shape(src.shape[0], BLK), shape(nsrc * ntgt, BLK)),
        [pltpu.SMEM((ntgt,), jnp.int32)],
        (tile_src.reshape(-1), tile_dst.reshape(-1), tile_count.reshape(-1), src),
        8,
        [smem, smem, smem, vmem],
    )

    def costs(first, some, held=(), outs=()):
        return call(
            lambda *refs: cost_kernel(first, len(some), len(held), *refs),
            (shape(src.shape[0], sum(piece.shape[0] for piece in some)), *outs),
            [],
            (src, norm, far, *some, *held),
            12,
        )

    (cost_a,) = costs(0, (own, early, early_other))
    (cost_b,) = costs(10, (late, late_other))
    last, cost_a = lax.optimization_barrier((last, cost_a))
    last_other = partner(last)
    cost_c, part = costs(14, (last, last_other), (cost_a, cost_b), (shape(cols, nsrc, BLK),))
    cost = (cost_a, cost_b, cost_c)
    pieces = (own, early, early_other, late, late_other, last, last_other)

    for step in range(ITERS):
        fpot, part = call(
            target_kernel,
            (shape(nsrc, BLK), shape(rows, ntgt, BLK)),
            [pltpu.VMEM((src.shape[0], BLK), jnp.float32), pltpu.VMEM((ntgt, BLK), jnp.float32)],
            (spread(part, "col"), amass, *cost),
            12,
        )
        parts = spread(part, "row")
        if step < ITERS - 1:
            part = call(
                source_kernel,
                shape(cols, nsrc, BLK),
                [pltpu.VMEM((ntgt, BLK), jnp.float32)],
                (parts, bmass, *cost),
                12,
            )
    gpot, sums = call(
        lambda *refs: map_kernel(len(pieces), *refs),
        (shape(ntgt, BLK), shape(src.shape[0], width + BLK, dtype=jnp.bfloat16)),
        [pltpu.VMEM((src.shape[0], ntgt * BLK), jnp.bfloat16)],
        (parts, bmass, fpot, *pieces, *cost),
        18,
    )
    share = src.shape[0] // cols
    sums = spread(sums.reshape(cols, share, -1), "col")
    mapped = call(divide_kernel, shape(share, width, dtype=jnp.bfloat16), [], (sums,), 8)
    return (fpot.reshape(-1) * UNIT, gpot.reshape(-1) * UNIT, mapped)


def solution(mesh):
    in_specs = (
        P(("row", "col"), None),
        P(("col", "row"), None),
        P("row"),
        P("col"),
        P("row", "col", None),
        P("row", "col", None),
        P("row", "col"),
    )
    out_specs = (P("row"), P("col"), P(("row", "col"), None))
    return jax.shard_map(body, mesh=mesh, in_specs=in_specs, out_specs=out_specs, check_vma=False)
```

time: 204 us -> 204 us (level)
  starting transfers between devices: 14.6 us -> 54.5 us
  waiting for transfers between devices: 68.8 us -> 37.6 us
  between operations: 14.7 us -> 1.63 us
  local copies, waits for them, and re-layouts: 3.19 us -> 6.24 us
    ppermute x0 -> x11, starting transfers between devices: none -> 46.1 us  [move(): return lax.ppermute(x, 'row', pairs)]
    all_to_all x2, waiting for transfers between devices: 55.3 us -> 29.7 us  [spread(): return lax.all_to_all(x, axis, 0, 0, tiled=True)]
    all_gather x1 -> x0, waiting for transfers between devices: 12.8 us -> none  [body(): tgt = lax.all_gather(target, 'row', axis=0, tiled=True)]
    ppermute x0 -> x11, waiting for transfers between devices: none -> 7.91 us  [move(): return lax.ppermute(x, 'row', pairs)]
    all_to_all x2, starting transfers between devices: 14.6 us -> 8.37 us  [spread(): return lax.all_to_all(x, axis, 0, 0, tiled=True)]
    unnamed x10 -> x27, local copies, waits for them, and re-layouts: 1.32 us -> 3.6 us
    pallas_call x9 -> x11, Pallas kernels: 18.6 us -> 17.3 us  [call(): pl.pallas_call(kernel, out_shape=shapes, in_specs=specs or [vmem] * len(a...]
  transfers between devices with their start and end apart: 3 -> 13, of which waited for: 3 -> 5; matrix products, arithmetic and copies ran while one was open for 1% -> 3% of each run, Pallas kernels for 0% -> 2%
where the time goes in v5:
time: 204 us; the launch traced here: 202 us
  blocking collectives  84 us (41%)
  starting transfers between devices  54.5 us (27%)
  waiting for transfers between devices  37.6 us (18%)
  Pallas kernels  17.3 us (8%)
  local copies, waits for them, and re-layouts  6.24 us (3%)
    all_to_all x6, blocking collectives, spread(): return lax.all_to_all(x, axis, 0, 0, tiled=True)  84 us
    ppermute x11, starting transfers between devices, move(): return lax.ppermute(x, 'row', pairs)  46.1 us
    all_to_all x2, waiting for transfers between devices, spread(): return lax.all_to_all(x, axis, 0, 0, tiled=True)  29.7 us
    pallas_call x11, Pallas kernels, call(): pl.pallas_call(kernel, out_shape=shapes, in_specs=specs or [vmem] * len(a...  17.3 us
    all_to_all x2, starting transfers between devices, spread(): return lax.all_to_all(x, axis, 0, 0, tiled=True)  8.37 us
    ppermute x11, waiting for transfers between devices, move(): return lax.ppermute(x, 'row', pairs)  7.91 us
  transfers between devices with their start and end apart: 13, of which 5 were waited for; matrix products, arithmetic and copies ran while one was open for 3% of the time, Pallas kernels for 2%

profile of v5, /device:TPU:1, one launch (start us, length us, event | category | flops | bytes accessed | tf_op | source)
XLA Modules:
  0.0 202.4 jit_solution(986934673041861123)
XLA Ops:
  0.6 8.8 %collective-permute-start.4 = (bf16[128,1024]{1,0:T(8,128)(2,1)}, bf16[128,1024]{1,0:T(8,128)(2,1)S(1)}, u32[]{:S(2)}, u32[]{:S(2)}) collective-permute-start(bf16[128,1024]{1,0:T(8,128)(2,1)} %param.8), channel_id=1, source_target_pairs={{0,32},{32,0},{64,96},{96,64},{128,160},{160,128},{192,224},{224,1... | collective-permute-start | bytes 786440 | tf_op jit(solution)/shard_map/ppermute | solution.py:213
  9.4 1.9 broadcast_in_dim.2
  11.3 4.4 %all-to-all-start = ((bf16[32,16,1024]{2,1,0:T(8,128)(2,1)}), bf16[32,16,1024]{2,1,0:T(8,128)(2,1)S(1)}, u32[]{:S(2)}, u32[]{:S(2)}) async-start(bf16[32,16,1024]{2,1,0:T(8,128)(2,1)} %broadcast_in_dim.2), calls=%async_computation | async-start | bytes 2097152 | tf_op jit(solution)/shard_map/all_to_all | solution.py:204
  15.7 10.7 %collective-permute-start = (bf16[128,1024]{1,0:T(8,128)(2,1)S(1)}, bf16[128,1024]{1,0:T(8,128)(2,1)S(1)}, u32[]{:S(2)}, u32[]{:S(2)}) collective-permute-start(bf16[128,1024]{1,0:T(8,128)(2,1)S(1)} %copy-done.7), channel_id=1, source_target_pairs={{0,64},{32,480},{64,128},{96,32},{128,192},{160,96},{192,256},{224... | collective-permute-start | bytes 786440 | tf_op jit(solution)/shard_map/ppermute | solution.py:213
  26.4 2.2 %collective-permute-start.5 = (bf16[128,1024]{1,0:T(8,128)(2,1)S(1)}, bf16[128,1024]{1,0:T(8,128)(2,1)S(1)}, u32[]{:S(2)}, u32[]{:S(2)}) collective-permute-start(bf16[128,1024]{1,0:T(8,128)(2,1)S(1)} %collective-permute-done.4), channel_id=1, source_target_pairs={{0,64},{32,480},{64,128},{96,32},{128,192},{160,96},{192,256},{224... | collective-permute-start | bytes 786440 | tf_op jit(solution)/shard_map/ppermute | solution.py:213
  28.6 1.1 collective-permute-done
  29.7 5.3 %collective-permute-start.1 = (bf16[128,1024]{1,0:T(8,128)(2,1)S(1)}, bf16[128,1024]{1,0:T(8,128)(2,1)S(1)}, u32[]{:S(2)}, u32[]{:S(2)}) collective-permute-start(bf16[128,1024]{1,0:T(8,128)(2,1)S(1)} %collective-permute-done), channel_id=1, source_target_pairs={{0,64},{32,480},{64,128},{96,32},{128,192},{160,96},{192,256},{224... | collective-permute-start | bytes 786440 | tf_op jit(solution)/shard_map/ppermute | solution.py:213
  35.0 2.8 %collective-permute-start.6 = (bf16[128,1024]{1,0:T(8,128)(2,1)S(1)}, bf16[128,1024]{1,0:T(8,128)(2,1)S(1)}, u32[]{:S(2)}, u32[]{:S(2)}) collective-permute-start(bf16[128,1024]{1,0:T(8,128)(2,1)S(1)} %collective-permute-done.5), channel_id=1, source_target_pairs={{0,64},{32,480},{64,128},{96,32},{128,192},{160,96},{192,256},{224... | collective-permute-start | bytes 786440 | tf_op jit(solution)/shard_map/ppermute | solution.py:213
  38.4 4.1 %collective-permute-done.6 = bf16[128,1024]{1,0:T(8,128)(2,1)S(1)} collective-permute-done((bf16[128,1024]{1,0:T(8,128)(2,1)S(1)}, bf16[128,1024]{1,0:T(8,128)(2,1)S(1)}, u32[]{:S(2)}, u32[]{:S(2)}) %collective-permute-start.6) | collective-permute-done | bytes 262176 | tf_op jit(solution)/shard_map/ppermute | solution.py:213
  42.5 3.1 %collective-permute-start.7 = (bf16[512,1024]{1,0:T(8,128)(2,1)S(1)}, bf16[512,1024]{1,0:T(8,128)(2,1)S(1)}, u32[]{:S(2)}, u32[]{:S(2)}) collective-permute-start(bf16[512,1024]{1,0:T(8,128)(2,1)S(1)} %constant_dynamic-update-slice_fusion.2.refs_4_), channel_id=1, source_target_pairs={{0,32},{32,0},{64,96},{96,64},{128,160},{160,128},{192,224},{224,1... | collective-permute-start | bytes 3145736 | tf_op jit(solution)/shard_map/ppermute | solution.py:213
  45.6 2.9 %collective-permute-start.2 = (bf16[128,1024]{1,0:T(8,128)(2,1)S(1)}, bf16[128,1024]{1,0:T(8,128)(2,1)}, u32[]{:S(2)}, u32[]{:S(2)}) collective-permute-start(bf16[128,1024]{1,0:T(8,128)(2,1)S(1)} %collective-permute-done.1), channel_id=1, source_target_pairs={{0,64},{32,480},{64,128},{96,32},{128,192},{160,96},{192,256},{224... | collective-permute-start | bytes 786440 | tf_op jit(solution)/shard_map/ppermute | solution.py:213
  48.4 2.4 %collective-permute-start.9 = (bf16[128,1024]{1,0:T(8,128)(2,1)S(1)}, bf16[128,1024]{1,0:T(8,128)(2,1)S(1)}, u32[]{:S(2)}, u32[]{:S(2)}) collective-permute-start(bf16[128,1024]{1,0:T(8,128)(2,1)S(1)} %collective-permute-done.6), channel_id=1, source_target_pairs={{0,64},{32,480},{64,128},{96,32},{128,192},{160,96},{192,256},{224... | collective-permute-start | bytes 786440 | tf_op jit(solution)/shard_map/ppermute | solution.py:213
  50.8 2.3 %collective-permute-done.2 = bf16[128,1024]{1,0:T(8,128)(2,1)} collective-permute-done((bf16[128,1024]{1,0:T(8,128)(2,1)S(1)}, bf16[128,1024]{1,0:T(8,128)(2,1)}, u32[]{:S(2)}, u32[]{:S(2)}) %collective-permute-start.2) | collective-permute-done | bytes 262176 | tf_op jit(solution)/shard_map/ppermute | solution.py:213
  53.1 3.8 %collective-permute-start.3 = (bf16[128,1024]{1,0:T(8,128)(2,1)}, bf16[128,1024]{1,0:T(8,128)(2,1)S(1)}, u32[]{:S(2)}, u32[]{:S(2)}) collective-permute-start(bf16[128,1024]{1,0:T(8,128)(2,1)} %collective-permute-done.2), channel_id=1, source_target_pairs={{0,64},{32,480},{64,128},{96,32},{128,192},{160,96},{192,256},{224... | collective-permute-start | bytes 786440 | tf_op jit(solution)/shard_map/ppermute | solution.py:213
  56.9 1.7 constant_dynamic-update-slice_fusion.7
  59.3 2.1 %collective-permute-start.10 = (bf16[256,1024]{1,0:T(8,128)(2,1)}, bf16[256,1024]{1,0:T(8,128)(2,1)}, u32[]{:S(2)}, u32[]{:S(2)}) collective-permute-start(bf16[256,1024]{1,0:T(8,128)(2,1)} %constant_dynamic-update-slice_fusion.6.refs_3_.refs_6_), channel_id=1, source_target_pairs={{0,32},{32,0},{64,96},{96,64},{128,160},{160,128},{192,224},{224,1... | collective-permute-start | bytes 1572872 | tf_op jit(solution)/shard_map/ppermute | solution.py:213
  62.9 1.0 shard_map.94
  64.0 1.6 shard_map.95.refs_5_.refs_0_.refs_10_
  65.7 2.3 %collective-permute-start.8 = (bf16[128,1024]{1,0:T(8,128)(2,1)S(1)}, bf16[128,1024]{1,0:T(8,128)(2,1)S(1)}, u32[]{:S(2)}, u32[]{:S(2)}) collective-permute-start(bf16[128,1024]{1,0:T(8,128)(2,1)S(1)} %collective-permute-done.3.refs_3_.refs_8_), channel_id=1, source_target_pairs={{0,32},{32,0},{64,96},{96,64},{128,160},{160,128},{192,224},{224,1... | collective-permute-start | bytes 786440 | tf_op jit(solution)/shard_map/ppermute | solution.py:213
  67.9 2.0 shard_map.96.refs_6_.refs_1_.refs_11_
  69.9 1.5 shard_map.97
  71.5 18.0 %all_to_all.40.parts_ref = f32[32,4,128]{2,1,0:T(4,128)S(1)} all-to-all(f32[32,4,128]{2,1,0:T(4,128)S(1)} %get-tuple-element.19), channel_id=1, replica_groups=mesh['row'=16,'col'=32] {'col'}, dimensions={0} | all-to-all | bytes 131072 | tf_op jit(solution)/shard_map/all_to_all | solution.py:204
  89.5 1.4 shard_map.98
  90.9 16.2 %all_to_all.41.parts_ref = f32[16,16,128]{2,1,0:T(8,128)S(1)} all-to-all(f32[16,16,128]{2,1,0:T(8,128)S(1)} %get-tuple-element.21), channel_id=1, replica_groups=mesh['row'=16,'col'=32] {'row'}, dimensions={0} | all-to-all | bytes 262144 | tf_op jit(solution)/shard_map/all_to_all | solution.py:204
  108.1 12.3 %all_to_all.42.parts_ref = f32[32,4,128]{2,1,0:T(4,128)S(1)} all-to-all(f32[32,4,128]{2,1,0:T(4,128)S(1)} %shard_map.99), channel_id=1, replica_groups=mesh['row'=16,'col'=32] {'col'}, dimensions={0} | all-to-all | bytes 131072 | tf_op jit(solution)/shard_map/all_to_all | solution.py:204
  120.4 1.4 shard_map.100
  121.8 12.5 %all_to_all.43.parts_ref = f32[16,16,128]{2,1,0:T(8,128)S(1)} all-to-all(f32[16,16,128]{2,1,0:T(8,128)S(1)} %get-tuple-element.22), channel_id=1, replica_groups=mesh['row'=16,'col'=32] {'row'}, dimensions={0} | all-to-all | bytes 262144 | tf_op jit(solution)/shard_map/all_to_all | solution.py:204
  135.3 12.3 %all_to_all.44.parts_ref = f32[32,4,128]{2,1,0:T(4,128)S(1)} all-to-all(f32[32,4,128]{2,1,0:T(4,128)S(1)} %shard_map.101), channel_id=1, replica_groups=mesh['row'=16,'col'=32] {'col'}, dimensions={0} | all-to-all | bytes 131072 | tf_op jit(solution)/shard_map/all_to_all | solution.py:204
  148.5 12.5 %all_to_all.45.refs_0_ = f32[16,16,128]{2,1,0:T(8,128)S(1)} all-to-all(f32[16,16,128]{2,1,0:T(8,128)S(1)} %get-tuple-element.24), channel_id=1, replica_groups=mesh['row'=16,'col'=32] {'row'}, dimensions={0} | all-to-all | bytes 262144 | tf_op jit(solution)/shard_map/all_to_all | solution.py:204
  161.1 4.7 %shard_map.103 = (f32[16,128]{1,0:T(8,128)S(1)}, bf16[512,1152]{1,0:T(8,128)(2,1)S(1)}) custom-call(f32[16,16,128]{2,1,0:T(8,128)S(1)} %all_to_all.45.refs_0_, f32[16,128]{1,0:T(8,128)S(1)} %bitcast.19, f32[4,128]{1,0:T(4,128)S(1)} %get-tuple-element.23.refs_2_, bf16[256,1024]{1,0:T(8,128)(2,1)S(1)} %copy-done.1, ...), custom_call_target="tpu_custom_call" | custom-call | tf_op jit(solution)/shard_map/pallas_call | solution.py:189
  166.8 3.9 %all-to-all-start.7 = ((bf16[32,16,1152]{2,1,0:T(8,128)(2,1)}), bf16[32,16,1152]{2,1,0:T(8,128)(2,1)S(1)}, u32[]{:S(2)}, u32[]{:S(2)}) async-start(bf16[32,16,1152]{2,1,0:T(8,128)(2,1)} %bitcast.16), calls=%async_computation.7 | async-start | bytes 2359296 | tf_op jit(solution)/shard_map/all_to_all | solution.py:204
  171.9 29.7 %all-to-all-done.7.sums_ref = bf16[32,16,1152]{2,1,0:T(8,128)(2,1)S(1)} async-done(((bf16[32,16,1152]{2,1,0:T(8,128)(2,1)}), bf16[32,16,1152]{2,1,0:T(8,128)(2,1)S(1)}, u32[]{:S(2)}, u32[]{:S(2)}) %all-to-all-start.7) | async-done | bytes 1179680 | tf_op jit(solution)/shard_map/all_to_all | solution.py:204
  (44 shorter events, 7.9 us)
Async XLA Ops:
  0.6 25.8 %collective-permute-start.4 = (bf16[128,1024]{1,0:T(8,128)(2,1)}, bf16[128,1024]{1,0:T(8,128)(2,1)S(1)}, u32[]{:S(2)}, u32[]{:S(2)}) collective-permute-start(bf16[128,1024]{1,0:T(8,128)(2,1)} %param.8), channel_id=1, source_target_pairs={{0,32},{32,0},{64,96},{96,64},{128,160},{160,128},{192,224},{224,1... | collective-permute-start | bytes 786440 | tf_op jit(solution)/shard_map/ppermute | solution.py:213
  11.3 4.4 %copy-start.7 = (bf16[128,1024]{1,0:T(8,128)(2,1)S(1)}, bf16[128,1024]{1,0:T(8,128)(2,1)}, u32[]{:S(2)}) copy-start(bf16[128,1024]{1,0:T(8,128)(2,1)} %param.8) | copy-start | bytes 786436
  11.3 51.6 %all-to-all-start = ((bf16[32,16,1024]{2,1,0:T(8,128)(2,1)}), bf16[32,16,1024]{2,1,0:T(8,128)(2,1)S(1)}, u32[]{:S(2)}, u32[]{:S(2)}) async-start(bf16[32,16,1024]{2,1,0:T(8,128)(2,1)} %broadcast_in_dim.2), calls=%async_computation | async-start | bytes 2097152 | tf_op jit(solution)/shard_map/all_to_all | solution.py:204
  15.7 14.0 %collective-permute-start = (bf16[128,1024]{1,0:T(8,128)(2,1)S(1)}, bf16[128,1024]{1,0:T(8,128)(2,1)S(1)}, u32[]{:S(2)}, u32[]{:S(2)}) collective-permute-start(bf16[128,1024]{1,0:T(8,128)(2,1)S(1)} %copy-done.7), channel_id=1, source_target_pairs={{0,64},{32,480},{64,128},{96,32},{128,192},{160,96},{192,256},{224... | collective-permute-start | bytes 786440 | tf_op jit(solution)/shard_map/ppermute | solution.py:213
  26.4 8.6 %copy-start.9 = (bf16[128,1024]{1,0:T(8,128)(2,1)}, bf16[128,1024]{1,0:T(8,128)(2,1)S(1)}, u32[]{:S(2)}) copy-start(bf16[128,1024]{1,0:T(8,128)(2,1)S(1)} %collective-permute-done.4) | copy-start | bytes 786436
  26.4 8.6 %collective-permute-start.5 = (bf16[128,1024]{1,0:T(8,128)(2,1)S(1)}, bf16[128,1024]{1,0:T(8,128)(2,1)S(1)}, u32[]{:S(2)}, u32[]{:S(2)}) collective-permute-start(bf16[128,1024]{1,0:T(8,128)(2,1)S(1)} %collective-permute-done.4), channel_id=1, source_target_pairs={{0,64},{32,480},{64,128},{96,32},{128,192},{160,96},{192,256},{224... | collective-permute-start | bytes 786440 | tf_op jit(solution)/shard_map/ppermute | solution.py:213
  29.7 8.6 %collective-permute-start.1 = (bf16[128,1024]{1,0:T(8,128)(2,1)S(1)}, bf16[128,1024]{1,0:T(8,128)(2,1)S(1)}, u32[]{:S(2)}, u32[]{:S(2)}) collective-permute-start(bf16[128,1024]{1,0:T(8,128)(2,1)S(1)} %collective-permute-done), channel_id=1, source_target_pairs={{0,64},{32,480},{64,128},{96,32},{128,192},{160,96},{192,256},{224... | collective-permute-start | bytes 786440 | tf_op jit(solution)/shard_map/ppermute | solution.py:213
  35.0 7.4 %collective-permute-start.6 = (bf16[128,1024]{1,0:T(8,128)(2,1)S(1)}, bf16[128,1024]{1,0:T(8,128)(2,1)S(1)}, u32[]{:S(2)}, u32[]{:S(2)}) collective-permute-start(bf16[128,1024]{1,0:T(8,128)(2,1)S(1)} %collective-permute-done.5), channel_id=1, source_target_pairs={{0,64},{32,480},{64,128},{96,32},{128,192},{160,96},{192,256},{224... | collective-permute-start | bytes 786440 | tf_op jit(solution)/shard_map/ppermute | solution.py:213
  37.9 24.2 %copy-start.8 = (bf16[128,1024]{1,0:T(8,128)(2,1)S(1)}, bf16[128,1024]{1,0:T(8,128)(2,1)}, u32[]{:S(2)}) copy-start(bf16[128,1024]{1,0:T(8,128)(2,1)} %param.8) | copy-start | bytes 786436
  38.3 23.7 %copy-start.10 = (bf16[128,1024]{1,0:T(8,128)(2,1)S(1)}, bf16[128,1024]{1,0:T(8,128)(2,1)}, u32[]{:S(2)}) copy-start(bf16[128,1024]{1,0:T(8,128)(2,1)} %copy-done.9) | copy-start | bytes 786436
  42.5 20.4 %copy-start.5 = (s32[1,1,32]{2,1,0:T(1,128)S(1)}, s32[1,1,32]{2,1,0:T(1,128)}, u32[]{:S(2)}) copy-start(s32[1,1,32]{2,1,0:T(1,128)} %param.11) | copy-start | bytes 388
  42.5 20.4 %copy-start.6 = (s32[1,1,32]{2,1,0:T(1,128)S(1)}, s32[1,1,32]{2,1,0:T(1,128)}, u32[]{:S(2)}) copy-start(s32[1,1,32]{2,1,0:T(1,128)} %param.12) | copy-start | bytes 388
  42.5 21.5 %collective-permute-start.7 = (bf16[512,1024]{1,0:T(8,128)(2,1)S(1)}, bf16[512,1024]{1,0:T(8,128)(2,1)S(1)}, u32[]{:S(2)}, u32[]{:S(2)}) collective-permute-start(bf16[512,1024]{1,0:T(8,128)(2,1)S(1)} %constant_dynamic-update-slice_fusion.2.refs_4_), channel_id=1, source_target_pairs={{0,32},{32,0},{64,96},{96,64},{128,160},{160,128},{192,224},{224,1... | collective-permute-start | bytes 3145736 | tf_op jit(solution)/shard_map/ppermute | solution.py:213
  45.6 7.5 %collective-permute-start.2 = (bf16[128,1024]{1,0:T(8,128)(2,1)S(1)}, bf16[128,1024]{1,0:T(8,128)(2,1)}, u32[]{:S(2)}, u32[]{:S(2)}) collective-permute-start(bf16[128,1024]{1,0:T(8,128)(2,1)S(1)} %collective-permute-done.1), channel_id=1, source_target_pairs={{0,64},{32,480},{64,128},{96,32},{128,192},{160,96},{192,256},{224... | collective-permute-start | bytes 786440 | tf_op jit(solution)/shard_map/ppermute | solution.py:213
  48.4 10.1 %collective-permute-start.9 = (bf16[128,1024]{1,0:T(8,128)(2,1)S(1)}, bf16[128,1024]{1,0:T(8,128)(2,1)S(1)}, u32[]{:S(2)}, u32[]{:S(2)}) collective-permute-start(bf16[128,1024]{1,0:T(8,128)(2,1)S(1)} %collective-permute-done.6), channel_id=1, source_target_pairs={{0,64},{32,480},{64,128},{96,32},{128,192},{160,96},{192,256},{224... | collective-permute-start | bytes 786440 | tf_op jit(solution)/shard_map/ppermute | solution.py:213
  53.1 12.6 %collective-permute-start.3 = (bf16[128,1024]{1,0:T(8,128)(2,1)}, bf16[128,1024]{1,0:T(8,128)(2,1)S(1)}, u32[]{:S(2)}, u32[]{:S(2)}) collective-permute-start(bf16[128,1024]{1,0:T(8,128)(2,1)} %collective-permute-done.2), channel_id=1, source_target_pairs={{0,64},{32,480},{64,128},{96,32},{128,192},{160,96},{192,256},{224... | collective-permute-start | bytes 786440 | tf_op jit(solution)/shard_map/ppermute | solution.py:213
  59.3 8.6 %collective-permute-start.10 = (bf16[256,1024]{1,0:T(8,128)(2,1)}, bf16[256,1024]{1,0:T(8,128)(2,1)}, u32[]{:S(2)}, u32[]{:S(2)}) collective-permute-start(bf16[256,1024]{1,0:T(8,128)(2,1)} %constant_dynamic-update-slice_fusion.6.refs_3_.refs_6_), channel_id=1, source_target_pairs={{0,32},{32,0},{64,96},{96,64},{128,160},{160,128},{192,224},{224,1... | collective-permute-start | bytes 1572872 | tf_op jit(solution)/shard_map/ppermute | solution.py:213
  62.1 0.8 copy-start
  62.9 1.1 copy-start.1
  65.7 4.3 %collective-permute-start.8 = (bf16[128,1024]{1,0:T(8,128)(2,1)S(1)}, bf16[128,1024]{1,0:T(8,128)(2,1)S(1)}, u32[]{:S(2)}, u32[]{:S(2)}) collective-permute-start(bf16[128,1024]{1,0:T(8,128)(2,1)S(1)} %collective-permute-done.3.refs_3_.refs_8_), channel_id=1, source_target_pairs={{0,32},{32,0},{64,96},{96,64},{128,160},{160,128},{192,224},{224,1... | collective-permute-start | bytes 786440 | tf_op jit(solution)/shard_map/ppermute | solution.py:213
  69.9 19.6 %copy-start.4 = (f32[512]{0:T(512)S(1)}, f32[512]{0:T(512)}, u32[]{:S(2)}) copy-start(f32[512]{0:T(512)} %param.9) | copy-start | bytes 6148
  89.5 17.6 %copy-start.3 = (f32[2048]{0:T(1024)S(1)}, f32[2048]{0:T(1024)}, u32[]{:S(2)}) copy-start(f32[2048]{0:T(1024)} %param.10) | copy-start | bytes 24580
  165.8 1.0 copy-start.2
  166.8 34.8 %all-to-all-start.7 = ((bf16[32,16,1152]{2,1,0:T(8,128)(2,1)}), bf16[32,16,1152]{2,1,0:T(8,128)(2,1)S(1)}, u32[]{:S(2)}, u32[]{:S(2)}) async-start(bf16[32,16,1152]{2,1,0:T(8,128)(2,1)} %bitcast.16), calls=%async_computation.7 | async-start | bytes 2359296 | tf_op jit(solution)/shard_map/all_to_all | solution.py:204

commit v6 on v5

--- a/solution.py
+++ b/solution.py
@@ -115,8 +115,7 @@
 
 
 def target_kernel(parts_ref, mass_ref, *refs):
-    *cost_refs, pot_ref, part_ref, wide, mine = refs
-    order = held_order()
+    *cost_refs, pot_ref, part_ref, wide, held, mine = refs
     pot = combine(mass_ref, parts_ref)
     pot_ref[...] = pot
     for s in range(pot.shape[0]):
@@ -126,7 +125,9 @@
         peak = jnp.max(gap, axis=0)
         top = jnp.max(peak, axis=0, keepdims=True)
         total = jnp.sum(jnp.exp2(gap - top[None]), axis=0)
-        mine[pl.ds(order[n], 1), :] = top + jnp.log2(jnp.sum(total, axis=0, keepdims=True))
+        held[n : n + 1, :] = top + jnp.log2(jnp.sum(total, axis=0, keepdims=True))
+    for cluster, slot in enumerate(held_slots()):
+        mine[cluster : cluster + 1, :] = held[pl.ds(slot, 1), :]
     part_ref[...] = jnp.broadcast_to(mine[...][None], part_ref.shape)
 
 
@@ -225,21 +226,25 @@
     row = lax.axis_index("row")
     z, c = row // CORES, row % CORES
     way = 2 * c - 1
-
-    def pair(k, core):
+    order = []
+    for k in (0, 1, 2, 3, -1, -2, -3, 4):
         chip = (z + way * k + CHIPS) % CHIPS
-        return [chip * CORES + core, chip * CORES + 1 - core]
-
-    return [
-        *pair(0, c),
-        *pair(1, c),
-        *pair(2, c),
-        *pair(-1, 1 - c),
-        *pair(-2, 1 - c),
-        *pair(3, c),
-        *pair(-3, 1 - c),
-        *pair(4, c),
-    ]
+        core = c if k >= 0 else 1 - c
+        order += [chip * CORES + core, chip * CORES + 1 - core]
+    return order
+
+
+def held_slots():
+    row = lax.axis_index("row")
+    z, c = row // CORES, row % CORES
+    way = 2 * c - 1
+    slots = []
+    for cluster in range(CHIPS * CORES):
+        k = ((cluster // CORES - z) * way + CHIPS) % CHIPS
+        second = jnp.where(cluster % CORES == c, 0, 1)
+        mirrored = jnp.where(k == 4, 14 + second, 8 + 2 * (7 - k) + 1 - second)
+        slots.append(jnp.where(k < 4, 2 * k + second, mirrored))
+    return slots
 
 
 def body(source, target, source_mass, target_mass, tile_src, tile_dst, tile_count):
@@ -251,13 +256,6 @@
     src = spread(jnp.broadcast_to(source[None], (cols, *source.shape)), "col")
     src = src.reshape(-1, width)
     two, near_two = ring(one), ring(near_one)
-    three, near_three = ring(two), ring(near_two)
-    own = jnp.concatenate([target, near])
-    early = jnp.concatenate([one, near_one, two, near_two])
-    late = jnp.concatenate([three, near_three])
-    early_other = partner(early)
-    last = ring(three)
-    late_other = partner(late)
     amass = source_mass.reshape(nsrc, BLK)
     bmass = target_mass.reshape(ntgt, BLK)
     vmem, smem = (pl.BlockSpec(memory_space=space) for space in (pltpu.VMEM, pltpu.SMEM))
@@ -270,6 +268,12 @@
         [smem, smem, smem, vmem],
     )
 
+    three, near_three = ring(two), ring(near_two)
+    three, near_three, norm = lax.optimization_barrier((three, near_three, norm))
+    last = ring(three)
+    own = jnp.concatenate([target, near])
+    joined = jnp.concatenate([one, near_one, two, near_two, three, near_three])
+    other = partner(joined)
     def costs(first, some, held=(), outs=()):
         return call(
             lambda *refs: cost_kernel(first, len(some), len(held), *refs),
@@ -279,19 +283,19 @@
             12,
         )
 
-    (cost_a,) = costs(0, (own, early, early_other))
-    (cost_b,) = costs(10, (late, late_other))
+    (cost_a,) = costs(0, (own, joined))
     last, cost_a = lax.optimization_barrier((last, cost_a))
     last_other = partner(last)
+    (cost_b,) = costs(8, (other,))
     cost_c, part = costs(14, (last, last_other), (cost_a, cost_b), (shape(cols, nsrc, BLK),))
     cost = (cost_a, cost_b, cost_c)
-    pieces = (own, early, early_other, late, late_other, last, last_other)
+    pieces = (own, joined, other, last, last_other)
 
     for step in range(ITERS):
         fpot, part = call(
             target_kernel,
             (shape(nsrc, BLK), shape(rows, ntgt, BLK)),
-            [pltpu.VMEM((src.shape[0], BLK), jnp.float32), pltpu.VMEM((ntgt, BLK), jnp.float32)],
+            [pltpu.VMEM((src.shape[0], BLK), jnp.float32)] + [pltpu.VMEM((ntgt, BLK), jnp.float32)] * 2,
             (spread(part, "col"), amass, *cost),
             12,
         )
@@ -309,7 +313,7 @@
         (shape(ntgt, BLK), shape(src.shape[0], width + BLK, dtype=jnp.bfloat16)),
         [pltpu.VMEM((src.shape[0], ntgt * BLK), jnp.bfloat16)],
         (parts, bmass, fpot, *pieces, *cost),
-        18,
+        32,
     )
     share = src.shape[0] // cols
     sums = spread(sums.reshape(cols, share, -1), "col")

time: 204 us -> 201 us (0.985)
  Pallas kernels: 17.3 us -> 15 us
  starting transfers between devices: 54.5 us -> 56.6 us
    all_to_all x2, starting transfers between devices: 8.37 us -> 14.4 us  [spread(): return lax.all_to_all(x, axis, 0, 0, tiled=True)]
    ppermute x11 -> x10, starting transfers between devices: 46.1 us -> 42.2 us  [move(): return lax.ppermute(x, 'row', pairs)]
    pallas_call x11, Pallas kernels: 17.3 us -> 15 us  [call(): pl.pallas_call(kernel, out_shape=shapes, in_specs=specs or [vmem] * len(a...]
    ppermute x11 -> x10, waiting for transfers between devices: 7.91 us -> 6.23 us  [move(): return lax.ppermute(x, 'row', pairs)]
  transfers between devices with their start and end apart: 13 -> 12, of which waited for: 5 -> 4; matrix products, arithmetic and copies ran while one was open for 3% -> 2% of each run, Pallas kernels for 2% -> 2%
where the time goes in v6:
time: 201 us; the launch traced here: 200 us
  blocking collectives  83.6 us (42%)
  starting transfers between devices  56.6 us (28%)
  waiting for transfers between devices  35.9 us (18%)
  Pallas kernels  15 us (7%)
  local copies, waits for them, and re-layouts  5.99 us (3%)
    all_to_all x6, blocking collectives, spread(): return lax.all_to_all(x, axis, 0, 0, tiled=True)  83.6 us
    ppermute x10, starting transfers between devices, move(): return lax.ppermute(x, 'row', pairs)  42.2 us
    all_to_all x2, waiting for transfers between devices, spread(): return lax.all_to_all(x, axis, 0, 0, tiled=True)  29.7 us
    pallas_call x11, Pallas kernels, call(): pl.pallas_call(kernel, out_shape=shapes, in_specs=specs or [vmem] * len(a...  15 us
    all_to_all x2, starting transfers between devices, spread(): return lax.all_to_all(x, axis, 0, 0, tiled=True)  14.4 us
    ppermute x10, waiting for transfers between devices, move(): return lax.ppermute(x, 'row', pairs)  6.23 us
  transfers between devices with their start and end apart: 12, of which 4 were waited for; matrix products, arithmetic and copies ran while one was open for 2% of the time, Pallas kernels for 2%

profile of v6, /device:TPU:1, one launch (start us, length us, event | category | flops | bytes accessed | tf_op | source)
XLA Modules:
  0.0 199.9 jit_solution(15614527473449738713)
XLA Ops:
  0.6 1.9 broadcast_in_dim.2
  2.6 10.5 %all-to-all-start = ((bf16[32,16,1024]{2,1,0:T(8,128)(2,1)}), bf16[32,16,1024]{2,1,0:T(8,128)(2,1)S(1)}, u32[]{:S(2)}, u32[]{:S(2)}) async-start(bf16[32,16,1024]{2,1,0:T(8,128)(2,1)} %broadcast_in_dim.2), calls=%async_computation | async-start | bytes 2097152 | tf_op jit(solution)/shard_map/all_to_all | solution.py:205
  13.1 2.9 %collective-permute-start.3 = (bf16[128,1024]{1,0:T(8,128)(2,1)S(1)}, bf16[128,1024]{1,0:T(8,128)(2,1)S(1)}, u32[]{:S(2)}, u32[]{:S(2)}) collective-permute-start(bf16[128,1024]{1,0:T(8,128)(2,1)S(1)} %copy-done.5), channel_id=1, source_target_pairs={{0,32},{32,0},{64,96},{96,64},{128,160},{160,128},{192,224},{224,1... | collective-permute-start | bytes 786440 | tf_op jit(solution)/shard_map/ppermute | solution.py:214
  16.0 10.7 %collective-permute-start = (bf16[128,1024]{1,0:T(8,128)(2,1)S(1)}, bf16[128,1024]{1,0:T(8,128)(2,1)S(1)}, u32[]{:S(2)}, u32[]{:S(2)}) collective-permute-start(bf16[128,1024]{1,0:T(8,128)(2,1)S(1)} %copy-done.5), channel_id=1, source_target_pairs={{0,64},{32,480},{64,128},{96,32},{128,192},{160,96},{192,256},{224... | collective-permute-start | bytes 786440 | tf_op jit(solution)/shard_map/ppermute | solution.py:214
  26.7 2.2 %collective-permute-start.4 = (bf16[128,1024]{1,0:T(8,128)(2,1)S(1)}, bf16[128,1024]{1,0:T(8,128)(2,1)S(1)}, u32[]{:S(2)}, u32[]{:S(2)}) collective-permute-start(bf16[128,1024]{1,0:T(8,128)(2,1)S(1)} %collective-permute-done.3), channel_id=1, source_target_pairs={{0,64},{32,480},{64,128},{96,32},{128,192},{160,96},{192,256},{224... | collective-permute-start | bytes 786440 | tf_op jit(solution)/shard_map/ppermute | solution.py:214
  28.9 1.1 collective-permute-done
  30.0 5.3 %collective-permute-start.1 = (bf16[128,1024]{1,0:T(8,128)(2,1)S(1)}, bf16[128,1024]{1,0:T(8,128)(2,1)}, u32[]{:S(2)}, u32[]{:S(2)}) collective-permute-start(bf16[128,1024]{1,0:T(8,128)(2,1)S(1)} %collective-permute-done), channel_id=1, source_target_pairs={{0,64},{32,480},{64,128},{96,32},{128,192},{160,96},{192,256},{224... | collective-permute-start | bytes 786440 | tf_op jit(solution)/shard_map/ppermute | solution.py:214
  35.3 2.8 %collective-permute-start.5 = (bf16[128,1024]{1,0:T(8,128)(2,1)S(1)}, bf16[128,1024]{1,0:T(8,128)(2,1)}, u32[]{:S(2)}, u32[]{:S(2)}) collective-permute-start(bf16[128,1024]{1,0:T(8,128)(2,1)S(1)} %collective-permute-done.4), channel_id=1, source_target_pairs={{0,64},{32,480},{64,128},{96,32},{128,192},{160,96},{192,256},{224... | collective-permute-start | bytes 786440 | tf_op jit(solution)/shard_map/ppermute | solution.py:214
  38.8 5.1 %collective-permute-start.2 = (bf16[128,1024]{1,0:T(8,128)(2,1)}, bf16[128,1024]{1,0:T(8,128)(2,1)S(1)}, u32[]{:S(2)}, u32[]{:S(2)}) collective-permute-start(bf16[128,1024]{1,0:T(8,128)(2,1)} %collective-permute-done.1), channel_id=1, source_target_pairs={{0,64},{32,480},{64,128},{96,32},{128,192},{160,96},{192,256},{224... | collective-permute-start | bytes 786440 | tf_op jit(solution)/shard_map/ppermute | solution.py:214
  43.9 2.8 %collective-permute-start.6 = (bf16[128,1024]{1,0:T(8,128)(2,1)}, bf16[128,1024]{1,0:T(8,128)(2,1)}, u32[]{:S(2)}, u32[]{:S(2)}) collective-permute-start(bf16[128,1024]{1,0:T(8,128)(2,1)} %collective-permute-done.5), channel_id=1, source_target_pairs={{0,64},{32,480},{64,128},{96,32},{128,192},{160,96},{192,256},{224... | collective-permute-start | bytes 786440 | tf_op jit(solution)/shard_map/ppermute | solution.py:214
  47.7 1.0 constant_dynamic-update-slice_fusion.4
  48.7 1.1 shard_map.94
  49.8 1.9 collective-permute-done.6
  52.6 3.7 %collective-permute-start.9 = (bf16[768,1024]{1,0:T(8,128)(2,1)S(1)}, bf16[768,1024]{1,0:T(8,128)(2,1)S(1)}, u32[]{:S(2)}, u32[]{:S(2)}) collective-permute-start(bf16[768,1024]{1,0:T(8,128)(2,1)S(1)} %constant_dynamic-update-slice_fusion.2.refs_4_), channel_id=1, source_target_pairs={{0,32},{32,0},{64,96},{96,64},{128,160},{160,128},{192,224},{224,1... | collective-permute-start | bytes 4718600 | tf_op jit(solution)/shard_map/ppermute | solution.py:214
  56.4 2.8 %collective-permute-start.7 = (bf16[128,1024]{1,0:T(8,128)(2,1)S(1)}, bf16[128,1024]{1,0:T(8,128)(2,1)S(1)}, u32[]{:S(2)}, u32[]{:S(2)}) collective-permute-start(bf16[128,1024]{1,0:T(8,128)(2,1)S(1)} %collective-permute-done.2), channel_id=1, source_target_pairs={{0,64},{32,480},{64,128},{96,32},{128,192},{160,96},{192,256},{224... | collective-permute-start | bytes 786440 | tf_op jit(solution)/shard_map/ppermute | solution.py:214
  59.2 1.3 shard_map.95.refs_5_.refs_0_.refs_8_
  60.5 3.2 %collective-permute-done.7.refs_3_.refs_6_ = bf16[128,1024]{1,0:T(8,128)(2,1)S(1)} collective-permute-done((bf16[128,1024]{1,0:T(8,128)(2,1)S(1)}, bf16[128,1024]{1,0:T(8,128)(2,1)S(1)}, u32[]{:S(2)}, u32[]{:S(2)}) %collective-permute-start.7) | collective-permute-done | bytes 262176 | tf_op jit(solution)/shard_map/ppermute | solution.py:214
  63.8 4.0 %collective-permute-start.8 = (bf16[128,1024]{1,0:T(8,128)(2,1)S(1)}, bf16[128,1024]{1,0:T(8,128)(2,1)S(1)}, u32[]{:S(2)}, u32[]{:S(2)}) collective-permute-start(bf16[128,1024]{1,0:T(8,128)(2,1)S(1)} %collective-permute-done.7.refs_3_.refs_6_), channel_id=1, source_target_pairs={{0,32},{32,0},{64,96},{96,64},{128,160},{160,128},{192,224},{224,1... | collective-permute-start | bytes 786440 | tf_op jit(solution)/shard_map/ppermute | solution.py:214
  67.8 1.1 shard_map.96.refs_6_.refs_1_.refs_9_
  68.9 1.5 shard_map.97
  70.4 18.1 %all_to_all.40.parts_ref = f32[32,4,128]{2,1,0:T(4,128)S(1)} all-to-all(f32[32,4,128]{2,1,0:T(4,128)S(1)} %get-tuple-element.25), channel_id=1, replica_groups=mesh['row'=16,'col'=32] {'col'}, dimensions={0} | all-to-all | bytes 131072 | tf_op jit(solution)/shard_map/all_to_all | solution.py:205
  88.6 1.4 shard_map.98
  90.0 15.8 %all_to_all.41.parts_ref = f32[16,16,128]{2,1,0:T(8,128)S(1)} all-to-all(f32[16,16,128]{2,1,0:T(8,128)S(1)} %get-tuple-element.27), channel_id=1, replica_groups=mesh['row'=16,'col'=32] {'row'}, dimensions={0} | all-to-all | bytes 262144 | tf_op jit(solution)/shard_map/all_to_all | solution.py:205
  106.8 12.3 %all_to_all.42.parts_ref = f32[32,4,128]{2,1,0:T(4,128)S(1)} all-to-all(f32[32,4,128]{2,1,0:T(4,128)S(1)} %shard_map.99), channel_id=1, replica_groups=mesh['row'=16,'col'=32] {'col'}, dimensions={0} | all-to-all | bytes 131072 | tf_op jit(solution)/shard_map/all_to_all | solution.py:205
  119.1 1.4 shard_map.100
  120.5 12.5 %all_to_all.43.parts_ref = f32[16,16,128]{2,1,0:T(8,128)S(1)} all-to-all(f32[16,16,128]{2,1,0:T(8,128)S(1)} %get-tuple-element.28), channel_id=1, replica_groups=mesh['row'=16,'col'=32] {'row'}, dimensions={0} | all-to-all | bytes 262144 | tf_op jit(solution)/shard_map/all_to_all | solution.py:205
  133.9 12.3 %all_to_all.44.parts_ref = f32[32,4,128]{2,1,0:T(4,128)S(1)} all-to-all(f32[32,4,128]{2,1,0:T(4,128)S(1)} %shard_map.101), channel_id=1, replica_groups=mesh['row'=16,'col'=32] {'col'}, dimensions={0} | all-to-all | bytes 131072 | tf_op jit(solution)/shard_map/all_to_all | solution.py:205
  147.2 12.5 %all_to_all.45.refs_0_ = f32[16,16,128]{2,1,0:T(8,128)S(1)} all-to-all(f32[16,16,128]{2,1,0:T(8,128)S(1)} %get-tuple-element.30), channel_id=1, replica_groups=mesh['row'=16,'col'=32] {'row'}, dimensions={0} | all-to-all | bytes 262144 | tf_op jit(solution)/shard_map/all_to_all | solution.py:205
  159.7 3.5 %shard_map.103 = (f32[16,128]{1,0:T(8,128)S(1)}, bf16[512,1152]{1,0:T(8,128)(2,1)S(1)}) custom-call(f32[16,16,128]{2,1,0:T(8,128)S(1)} %all_to_all.45.refs_0_, f32[16,128]{1,0:T(8,128)S(1)} %bitcast.19, f32[4,128]{1,0:T(4,128)S(1)} %get-tuple-element.29.refs_2_, bf16[256,1024]{1,0:T(8,128)(2,1)S(1)} %constant_dynamic-update-slice_fusion.refs_3_, ...), custom_call_target="tpu_custom_call" | custom-call | tf_op jit(solution)/shard_map/pallas_call | solution.py:190
  163.3 1.0 copy-done
  164.3 3.9 %all-to-all-start.7 = ((bf16[32,16,1152]{2,1,0:T(8,128)(2,1)}), bf16[32,16,1152]{2,1,0:T(8,128)(2,1)S(1)}, u32[]{:S(2)}, u32[]{:S(2)}) async-start(bf16[32,16,1152]{2,1,0:T(8,128)(2,1)} %bitcast.16), calls=%async_computation.7 | async-start | bytes 2359296 | tf_op jit(solution)/shard_map/all_to_all | solution.py:205
  169.4 29.7 %all-to-all-done.7.sums_ref = bf16[32,16,1152]{2,1,0:T(8,128)(2,1)S(1)} async-done(((bf16[32,16,1152]{2,1,0:T(8,128)(2,1)}), bf16[32,16,1152]{2,1,0:T(8,128)(2,1)S(1)}, u32[]{:S(2)}, u32[]{:S(2)}) %all-to-all-start.7) | async-done | bytes 1179680 | tf_op jit(solution)/shard_map/all_to_all | solution.py:205
  (32 shorter events, 6.9 us)
Async XLA Ops:
  0.6 12.5 %copy-start.5 = (bf16[128,1024]{1,0:T(8,128)(2,1)S(1)}, bf16[128,1024]{1,0:T(8,128)(2,1)}, u32[]{:S(2)}) copy-start(bf16[128,1024]{1,0:T(8,128)(2,1)} %param.8) | copy-start | bytes 786436
  2.6 46.1 %all-to-all-start = ((bf16[32,16,1024]{2,1,0:T(8,128)(2,1)}), bf16[32,16,1024]{2,1,0:T(8,128)(2,1)S(1)}, u32[]{:S(2)}, u32[]{:S(2)}) async-start(bf16[32,16,1024]{2,1,0:T(8,128)(2,1)} %broadcast_in_dim.2), calls=%async_computation | async-start | bytes 2097152 | tf_op jit(solution)/shard_map/all_to_all | solution.py:205
  13.1 35.6 %copy-start.3 = (s32[1,1,32]{2,1,0:T(1,128)S(1)}, s32[1,1,32]{2,1,0:T(1,128)}, u32[]{:S(2)}) copy-start(s32[1,1,32]{2,1,0:T(1,128)} %param.11) | copy-start | bytes 388
  13.1 35.6 %copy-start.4 = (s32[1,1,32]{2,1,0:T(1,128)S(1)}, s32[1,1,32]{2,1,0:T(1,128)}, u32[]{:S(2)}) copy-start(s32[1,1,32]{2,1,0:T(1,128)} %param.12) | copy-start | bytes 388
  13.1 13.6 %collective-permute-start.3 = (bf16[128,1024]{1,0:T(8,128)(2,1)S(1)}, bf16[128,1024]{1,0:T(8,128)(2,1)S(1)}, u32[]{:S(2)}, u32[]{:S(2)}) collective-permute-start(bf16[128,1024]{1,0:T(8,128)(2,1)S(1)} %copy-done.5), channel_id=1, source_target_pairs={{0,32},{32,0},{64,96},{96,64},{128,160},{160,128},{192,224},{224,1... | collective-permute-start | bytes 786440 | tf_op jit(solution)/shard_map/ppermute | solution.py:214
  16.0 14.0 %collective-permute-start = (bf16[128,1024]{1,0:T(8,128)(2,1)S(1)}, bf16[128,1024]{1,0:T(8,128)(2,1)S(1)}, u32[]{:S(2)}, u32[]{:S(2)}) collective-permute-start(bf16[128,1024]{1,0:T(8,128)(2,1)S(1)} %copy-done.5), channel_id=1, source_target_pairs={{0,64},{32,480},{64,128},{96,32},{128,192},{160,96},{192,256},{224... | collective-permute-start | bytes 786440 | tf_op jit(solution)/shard_map/ppermute | solution.py:214
  26.7 8.6 %collective-permute-start.4 = (bf16[128,1024]{1,0:T(8,128)(2,1)S(1)}, bf16[128,1024]{1,0:T(8,128)(2,1)S(1)}, u32[]{:S(2)}, u32[]{:S(2)}) collective-permute-start(bf16[128,1024]{1,0:T(8,128)(2,1)S(1)} %collective-permute-done.3), channel_id=1, source_target_pairs={{0,64},{32,480},{64,128},{96,32},{128,192},{160,96},{192,256},{224... | collective-permute-start | bytes 786440 | tf_op jit(solution)/shard_map/ppermute | solution.py:214
  30.0 8.8 %collective-permute-start.1 = (bf16[128,1024]{1,0:T(8,128)(2,1)S(1)}, bf16[128,1024]{1,0:T(8,128)(2,1)}, u32[]{:S(2)}, u32[]{:S(2)}) collective-permute-start(bf16[128,1024]{1,0:T(8,128)(2,1)S(1)} %collective-permute-done), channel_id=1, source_target_pairs={{0,64},{32,480},{64,128},{96,32},{128,192},{160,96},{192,256},{224... | collective-permute-start | bytes 786440 | tf_op jit(solution)/shard_map/ppermute | solution.py:214
  35.3 8.6 %collective-permute-start.5 = (bf16[128,1024]{1,0:T(8,128)(2,1)S(1)}, bf16[128,1024]{1,0:T(8,128)(2,1)}, u32[]{:S(2)}, u32[]{:S(2)}) collective-permute-start(bf16[128,1024]{1,0:T(8,128)(2,1)S(1)} %collective-permute-done.4), channel_id=1, source_target_pairs={{0,64},{32,480},{64,128},{96,32},{128,192},{160,96},{192,256},{224... | collective-permute-start | bytes 786440 | tf_op jit(solution)/shard_map/ppermute | solution.py:214
  38.8 11.0 %collective-permute-start.2 = (bf16[128,1024]{1,0:T(8,128)(2,1)}, bf16[128,1024]{1,0:T(8,128)(2,1)S(1)}, u32[]{:S(2)}, u32[]{:S(2)}) collective-permute-start(bf16[128,1024]{1,0:T(8,128)(2,1)} %collective-permute-done.1), channel_id=1, source_target_pairs={{0,64},{32,480},{64,128},{96,32},{128,192},{160,96},{192,256},{224... | collective-permute-start | bytes 786440 | tf_op jit(solution)/shard_map/ppermute | solution.py:214
  43.9 7.7 %collective-permute-start.6 = (bf16[128,1024]{1,0:T(8,128)(2,1)}, bf16[128,1024]{1,0:T(8,128)(2,1)}, u32[]{:S(2)}, u32[]{:S(2)}) collective-permute-start(bf16[128,1024]{1,0:T(8,128)(2,1)} %collective-permute-done.5), channel_id=1, source_target_pairs={{0,64},{32,480},{64,128},{96,32},{128,192},{160,96},{192,256},{224... | collective-permute-start | bytes 786440 | tf_op jit(solution)/shard_map/ppermute | solution.py:214
  52.6 15.1 %collective-permute-start.9 = (bf16[768,1024]{1,0:T(8,128)(2,1)S(1)}, bf16[768,1024]{1,0:T(8,128)(2,1)S(1)}, u32[]{:S(2)}, u32[]{:S(2)}) collective-permute-start(bf16[768,1024]{1,0:T(8,128)(2,1)S(1)} %constant_dynamic-update-slice_fusion.2.refs_4_), channel_id=1, source_target_pairs={{0,32},{32,0},{64,96},{96,64},{128,160},{160,128},{192,224},{224,1... | collective-permute-start | bytes 4718600 | tf_op jit(solution)/shard_map/ppermute | solution.py:214
  56.4 7.4 %collective-permute-start.7 = (bf16[128,1024]{1,0:T(8,128)(2,1)S(1)}, bf16[128,1024]{1,0:T(8,128)(2,1)S(1)}, u32[]{:S(2)}, u32[]{:S(2)}) collective-permute-start(bf16[128,1024]{1,0:T(8,128)(2,1)S(1)} %collective-permute-done.2), channel_id=1, source_target_pairs={{0,64},{32,480},{64,128},{96,32},{128,192},{160,96},{192,256},{224... | collective-permute-start | bytes 786440 | tf_op jit(solution)/shard_map/ppermute | solution.py:214
  63.8 5.1 %collective-permute-start.8 = (bf16[128,1024]{1,0:T(8,128)(2,1)S(1)}, bf16[128,1024]{1,0:T(8,128)(2,1)S(1)}, u32[]{:S(2)}, u32[]{:S(2)}) collective-permute-start(bf16[128,1024]{1,0:T(8,128)(2,1)S(1)} %collective-permute-done.7.refs_3_.refs_6_), channel_id=1, source_target_pairs={{0,32},{32,0},{64,96},{96,64},{128,160},{160,128},{192,224},{224,1... | collective-permute-start | bytes 786440 | tf_op jit(solution)/shard_map/ppermute | solution.py:214
  68.9 19.7 %copy-start.2 = (f32[512]{0:T(512)S(1)}, f32[512]{0:T(512)}, u32[]{:S(2)}) copy-start(f32[512]{0:T(512)} %param.9) | copy-start | bytes 6148
  88.6 17.2 %copy-start.1 = (f32[2048]{0:T(1024)S(1)}, f32[2048]{0:T(1024)}, u32[]{:S(2)}) copy-start(f32[2048]{0:T(1024)} %param.10) | copy-start | bytes 24580
  163.2 1.0 copy-start
  164.3 34.8 %all-to-all-start.7 = ((bf16[32,16,1152]{2,1,0:T(8,128)(2,1)}), bf16[32,16,1152]{2,1,0:T(8,128)(2,1)S(1)}, u32[]{:S(2)}, u32[]{:S(2)}) async-start(bf16[32,16,1152]{2,1,0:T(8,128)(2,1)} %bitcast.16), calls=%async_computation.7 | async-start | bytes 2359296 | tf_op jit(solution)/shard_map/all_to_all | solution.py:205

commit v7 on v6

--- a/solution.py
+++ b/solution.py
@@ -269,11 +269,13 @@
     )
 
     three, near_three = ring(two), ring(near_two)
-    three, near_three, norm = lax.optimization_barrier((three, near_three, norm))
+    three, norm = lax.optimization_barrier((three, norm))
     last = ring(three)
     own = jnp.concatenate([target, near])
     joined = jnp.concatenate([one, near_one, two, near_two, three, near_three])
-    other = partner(joined)
+    last, turn = lax.optimization_barrier((last, joined))
+    other = partner(turn)
+
     def costs(first, some, held=(), outs=()):
         return call(
             lambda *refs: cost_kernel(first, len(some), len(held), *refs),
@@ -286,8 +288,8 @@
     (cost_a,) = costs(0, (own, joined))
     last, cost_a = lax.optimization_barrier((last, cost_a))
     last_other = partner(last)
-    (cost_b,) = costs(8, (other,))
-    cost_c, part = costs(14, (last, last_other), (cost_a, cost_b), (shape(cols, nsrc, BLK),))
+    (cost_c,) = costs(14, (last, last_other))
+    cost_b, part = costs(8, (other,), (cost_a, cost_c), (shape(cols, nsrc, BLK),))
     cost = (cost_a, cost_b, cost_c)
     pieces = (own, joined, other, last, last_other)
 

time: 201 us -> 200 us (level)
  no operation moved by 1% of the time
where the time goes in v7:
time: 200 us; the launch traced here: 198 us
  blocking collectives  82.8 us (41%)
  starting transfers between devices  58.1 us (29%)
  waiting for transfers between devices  33.9 us (17%)
  Pallas kernels  14.9 us (7%)
  local copies, waits for them, and re-layouts  6.01 us (3%)
    all_to_all x6, blocking collectives, spread(): return lax.all_to_all(x, axis, 0, 0, tiled=True)  82.8 us
    ppermute x10, starting transfers between devices, move(): return lax.ppermute(x, 'row', pairs)  43.5 us
    all_to_all x2, waiting for transfers between devices, spread(): return lax.all_to_all(x, axis, 0, 0, tiled=True)  29.7 us
    pallas_call x11, Pallas kernels, call(): pl.pallas_call(kernel, out_shape=shapes, in_specs=specs or [vmem] * len(a...  14.9 us
    all_to_all x2, starting transfers between devices, spread(): return lax.all_to_all(x, axis, 0, 0, tiled=True)  14.6 us
    ppermute x10, waiting for transfers between devices, move(): return lax.ppermute(x, 'row', pairs)  4.22 us
  transfers between devices with their start and end apart: 12, of which 4 were waited for; matrix products, arithmetic and copies ran while one was open for 2% of the time, Pallas kernels for 2%

profile of v7, /device:TPU:1, one launch (start us, length us, event | category | flops | bytes accessed | tf_op | source)
XLA Modules:
  0.0 198.5 jit_solution(3019390965535973728)
XLA Ops:
  0.6 1.9 broadcast_in_dim.2
  2.6 10.6 %all-to-all-start = ((bf16[32,16,1024]{2,1,0:T(8,128)(2,1)}), bf16[32,16,1024]{2,1,0:T(8,128)(2,1)S(1)}, u32[]{:S(2)}, u32[]{:S(2)}) async-start(bf16[32,16,1024]{2,1,0:T(8,128)(2,1)} %broadcast_in_dim.2), calls=%async_computation | async-start | bytes 2097152 | tf_op jit(solution)/shard_map/all_to_all | solution.py:205
  13.2 2.9 %collective-permute-start.4 = (bf16[128,1024]{1,0:T(8,128)(2,1)S(1)}, bf16[128,1024]{1,0:T(8,128)(2,1)S(1)}, u32[]{:S(2)}, u32[]{:S(2)}) collective-permute-start(bf16[128,1024]{1,0:T(8,128)(2,1)S(1)} %copy-done.5), channel_id=1, source_target_pairs={{0,32},{32,0},{64,96},{96,64},{128,160},{160,128},{192,224},{224,1... | collective-permute-start | bytes 786440 | tf_op jit(solution)/shard_map/ppermute | solution.py:214
  16.1 10.7 %collective-permute-start = (bf16[128,1024]{1,0:T(8,128)(2,1)S(1)}, bf16[128,1024]{1,0:T(8,128)(2,1)S(1)}, u32[]{:S(2)}, u32[]{:S(2)}) collective-permute-start(bf16[128,1024]{1,0:T(8,128)(2,1)S(1)} %copy-done.5), channel_id=1, source_target_pairs={{0,64},{32,480},{64,128},{96,32},{128,192},{160,96},{192,256},{224... | collective-permute-start | bytes 786440 | tf_op jit(solution)/shard_map/ppermute | solution.py:214
  26.8 2.2 %collective-permute-start.5 = (bf16[128,1024]{1,0:T(8,128)(2,1)S(1)}, bf16[128,1024]{1,0:T(8,128)(2,1)S(1)}, u32[]{:S(2)}, u32[]{:S(2)}) collective-permute-start(bf16[128,1024]{1,0:T(8,128)(2,1)S(1)} %collective-permute-done.4), channel_id=1, source_target_pairs={{0,64},{32,480},{64,128},{96,32},{128,192},{160,96},{192,256},{224... | collective-permute-start | bytes 786440 | tf_op jit(solution)/shard_map/ppermute | solution.py:214
  29.0 1.1 collective-permute-done
  30.1 5.3 %collective-permute-start.1 = (bf16[128,1024]{1,0:T(8,128)(2,1)S(1)}, bf16[128,1024]{1,0:T(8,128)(2,1)}, u32[]{:S(2)}, u32[]{:S(2)}) collective-permute-start(bf16[128,1024]{1,0:T(8,128)(2,1)S(1)} %collective-permute-done), channel_id=1, source_target_pairs={{0,64},{32,480},{64,128},{96,32},{128,192},{160,96},{192,256},{224... | collective-permute-start | bytes 786440 | tf_op jit(solution)/shard_map/ppermute | solution.py:214
  35.4 2.8 %collective-permute-start.6 = (bf16[128,1024]{1,0:T(8,128)(2,1)S(1)}, bf16[128,1024]{1,0:T(8,128)(2,1)S(1)}, u32[]{:S(2)}, u32[]{:S(2)}) collective-permute-start(bf16[128,1024]{1,0:T(8,128)(2,1)S(1)} %collective-permute-done.5), channel_id=1, source_target_pairs={{0,64},{32,480},{64,128},{96,32},{128,192},{160,96},{192,256},{224... | collective-permute-start | bytes 786440 | tf_op jit(solution)/shard_map/ppermute | solution.py:214
  38.8 5.1 %collective-permute-start.2 = (bf16[128,1024]{1,0:T(8,128)(2,1)}, bf16[128,1024]{1,0:T(8,128)(2,1)}, u32[]{:S(2)}, u32[]{:S(2)}) collective-permute-start(bf16[128,1024]{1,0:T(8,128)(2,1)} %collective-permute-done.1), channel_id=1, source_target_pairs={{0,64},{32,480},{64,128},{96,32},{128,192},{160,96},{192,256},{224... | collective-permute-start | bytes 786440 | tf_op jit(solution)/shard_map/ppermute | solution.py:214
  44.1 2.7 %collective-permute-start.7 = (bf16[128,1024]{1,0:T(8,128)(2,1)S(1)}, bf16[128,1024]{1,0:T(8,128)(2,1)}, u32[]{:S(2)}, u32[]{:S(2)}) collective-permute-start(bf16[128,1024]{1,0:T(8,128)(2,1)S(1)} %collective-permute-done.6), channel_id=1, source_target_pairs={{0,64},{32,480},{64,128},{96,32},{128,192},{160,96},{192,256},{224... | collective-permute-start | bytes 786440 | tf_op jit(solution)/shard_map/ppermute | solution.py:214
  47.8 1.0 shard_map.94
  48.8 3.8 %collective-permute-start.3 = (bf16[128,1024]{1,0:T(8,128)(2,1)}, bf16[128,1024]{1,0:T(8,128)(2,1)S(1)}, u32[]{:S(2)}, u32[]{:S(2)}) collective-permute-start(bf16[128,1024]{1,0:T(8,128)(2,1)} %collective-permute-done.2), channel_id=1, source_target_pairs={{0,64},{32,480},{64,128},{96,32},{128,192},{160,96},{192,256},{224... | collective-permute-start | bytes 786440 | tf_op jit(solution)/shard_map/ppermute | solution.py:214
  52.7 1.0 constant_dynamic-update-slice_fusion.1
  53.7 1.0 constant_dynamic-update-slice_fusion.refs_4_
  54.6 1.6 collective-permute-done.3.refs_3_.refs_6_
  56.2 6.1 %collective-permute-start.8 = (bf16[768,1024]{1,0:T(8,128)(2,1)S(1)}, bf16[768,1024]{1,0:T(8,128)(2,1)S(1)}, u32[]{:S(2)}, u32[]{:S(2)}) collective-permute-start(bf16[768,1024]{1,0:T(8,128)(2,1)S(1)} %constant_dynamic-update-slice_fusion.refs_4_), channel_id=1, source_target_pairs={{0,32},{32,0},{64,96},{96,64},{128,160},{160,128},{192,224},{224,1... | collective-permute-start | bytes 4718600 | tf_op jit(solution)/shard_map/ppermute | solution.py:214
  62.4 1.3 shard_map.95.refs_4_.refs_0_.refs_8_
  63.7 1.9 collective-permute-start.9
  65.7 1.5 collective-permute-done.9.refs_4_.refs_7_
  67.9 1.9 shard_map.97
  69.8 18.1 %all_to_all.40.parts_ref = f32[32,4,128]{2,1,0:T(4,128)S(1)} all-to-all(f32[32,4,128]{2,1,0:T(4,128)S(1)} %get-tuple-element.27), channel_id=1, replica_groups=mesh['row'=16,'col'=32] {'col'}, dimensions={0} | all-to-all | bytes 131072 | tf_op jit(solution)/shard_map/all_to_all | solution.py:205
  88.0 1.4 shard_map.98
  89.4 15.0 %all_to_all.41.parts_ref = f32[16,16,128]{2,1,0:T(8,128)S(1)} all-to-all(f32[16,16,128]{2,1,0:T(8,128)S(1)} %get-tuple-element.29), channel_id=1, replica_groups=mesh['row'=16,'col'=32] {'row'}, dimensions={0} | all-to-all | bytes 262144 | tf_op jit(solution)/shard_map/all_to_all | solution.py:205
  105.3 12.3 %all_to_all.42.parts_ref = f32[32,4,128]{2,1,0:T(4,128)S(1)} all-to-all(f32[32,4,128]{2,1,0:T(4,128)S(1)} %shard_map.99), channel_id=1, replica_groups=mesh['row'=16,'col'=32] {'col'}, dimensions={0} | all-to-all | bytes 131072 | tf_op jit(solution)/shard_map/all_to_all | solution.py:205
  117.6 1.4 shard_map.100
  119.1 12.5 %all_to_all.43.parts_ref = f32[16,16,128]{2,1,0:T(8,128)S(1)} all-to-all(f32[16,16,128]{2,1,0:T(8,128)S(1)} %get-tuple-element.30), channel_id=1, replica_groups=mesh['row'=16,'col'=32] {'row'}, dimensions={0} | all-to-all | bytes 262144 | tf_op jit(solution)/shard_map/all_to_all | solution.py:205
  132.5 12.3 %all_to_all.44.parts_ref = f32[32,4,128]{2,1,0:T(4,128)S(1)} all-to-all(f32[32,4,128]{2,1,0:T(4,128)S(1)} %shard_map.101), channel_id=1, replica_groups=mesh['row'=16,'col'=32] {'col'}, dimensions={0} | all-to-all | bytes 131072 | tf_op jit(solution)/shard_map/all_to_all | solution.py:205
  145.8 12.5 %all_to_all.45.refs_0_ = f32[16,16,128]{2,1,0:T(8,128)S(1)} all-to-all(f32[16,16,128]{2,1,0:T(8,128)S(1)} %get-tuple-element.32), channel_id=1, replica_groups=mesh['row'=16,'col'=32] {'row'}, dimensions={0} | all-to-all | bytes 262144 | tf_op jit(solution)/shard_map/all_to_all | solution.py:205
  158.3 3.5 %shard_map.103 = (f32[16,128]{1,0:T(8,128)S(1)}, bf16[512,1152]{1,0:T(8,128)(2,1)S(1)}) custom-call(f32[16,16,128]{2,1,0:T(8,128)S(1)} %all_to_all.45.refs_0_, f32[16,128]{1,0:T(8,128)S(1)} %bitcast.19, f32[4,128]{1,0:T(4,128)S(1)} %get-tuple-element.31.refs_2_, bf16[256,1024]{1,0:T(8,128)(2,1)S(1)} %constant_dynamic-update-slice_fusion.6.refs_3_, ...), custom_call_target="tpu_custom_call" | custom-call | tf_op jit(solution)/shard_map/pallas_call | solution.py:190
  161.8 1.0 copy-done
  162.8 3.9 %all-to-all-start.7 = ((bf16[32,16,1152]{2,1,0:T(8,128)(2,1)}), bf16[32,16,1152]{2,1,0:T(8,128)(2,1)S(1)}, u32[]{:S(2)}, u32[]{:S(2)}) async-start(bf16[32,16,1152]{2,1,0:T(8,128)(2,1)} %bitcast.16), calls=%async_computation.7 | async-start | bytes 2359296 | tf_op jit(solution)/shard_map/all_to_all | solution.py:205
  168.0 29.7 %all-to-all-done.7.sums_ref = bf16[32,16,1152]{2,1,0:T(8,128)(2,1)S(1)} async-done(((bf16[32,16,1152]{2,1,0:T(8,128)(2,1)}), bf16[32,16,1152]{2,1,0:T(8,128)(2,1)S(1)}, u32[]{:S(2)}, u32[]{:S(2)}) %all-to-all-start.7) | async-done | bytes 1179680 | tf_op jit(solution)/shard_map/all_to_all | solution.py:205
  (32 shorter events, 6.6 us)
Async XLA Ops:
  0.6 12.6 %copy-start.5 = (bf16[128,1024]{1,0:T(8,128)(2,1)S(1)}, bf16[128,1024]{1,0:T(8,128)(2,1)}, u32[]{:S(2)}) copy-start(bf16[128,1024]{1,0:T(8,128)(2,1)} %param.8) | copy-start | bytes 786436
  2.6 45.2 %copy-start.3 = (s32[1,1,32]{2,1,0:T(1,128)S(1)}, s32[1,1,32]{2,1,0:T(1,128)}, u32[]{:S(2)}) copy-start(s32[1,1,32]{2,1,0:T(1,128)} %param.11) | copy-start | bytes 388
  2.6 45.2 %copy-start.4 = (s32[1,1,32]{2,1,0:T(1,128)S(1)}, s32[1,1,32]{2,1,0:T(1,128)}, u32[]{:S(2)}) copy-start(s32[1,1,32]{2,1,0:T(1,128)} %param.12) | copy-start | bytes 388
  2.6 45.2 %all-to-all-start = ((bf16[32,16,1024]{2,1,0:T(8,128)(2,1)}), bf16[32,16,1024]{2,1,0:T(8,128)(2,1)S(1)}, u32[]{:S(2)}, u32[]{:S(2)}) async-start(bf16[32,16,1024]{2,1,0:T(8,128)(2,1)} %broadcast_in_dim.2), calls=%async_computation | async-start | bytes 2097152 | tf_op jit(solution)/shard_map/all_to_all | solution.py:205
  13.2 13.6 %collective-permute-start.4 = (bf16[128,1024]{1,0:T(8,128)(2,1)S(1)}, bf16[128,1024]{1,0:T(8,128)(2,1)S(1)}, u32[]{:S(2)}, u32[]{:S(2)}) collective-permute-start(bf16[128,1024]{1,0:T(8,128)(2,1)S(1)} %copy-done.5), channel_id=1, source_target_pairs={{0,32},{32,0},{64,96},{96,64},{128,160},{160,128},{192,224},{224,1... | collective-permute-start | bytes 786440 | tf_op jit(solution)/shard_map/ppermute | solution.py:214
  16.1 14.0 %collective-permute-start = (bf16[128,1024]{1,0:T(8,128)(2,1)S(1)}, bf16[128,1024]{1,0:T(8,128)(2,1)S(1)}, u32[]{:S(2)}, u32[]{:S(2)}) collective-permute-start(bf16[128,1024]{1,0:T(8,128)(2,1)S(1)} %copy-done.5), channel_id=1, source_target_pairs={{0,64},{32,480},{64,128},{96,32},{128,192},{160,96},{192,256},{224... | collective-permute-start | bytes 786440 | tf_op jit(solution)/shard_map/ppermute | solution.py:214
  26.8 8.6 %collective-permute-start.5 = (bf16[128,1024]{1,0:T(8,128)(2,1)S(1)}, bf16[128,1024]{1,0:T(8,128)(2,1)S(1)}, u32[]{:S(2)}, u32[]{:S(2)}) collective-permute-start(bf16[128,1024]{1,0:T(8,128)(2,1)S(1)} %collective-permute-done.4), channel_id=1, source_target_pairs={{0,64},{32,480},{64,128},{96,32},{128,192},{160,96},{192,256},{224... | collective-permute-start | bytes 786440 | tf_op jit(solution)/shard_map/ppermute | solution.py:214
  30.1 8.8 %collective-permute-start.1 = (bf16[128,1024]{1,0:T(8,128)(2,1)S(1)}, bf16[128,1024]{1,0:T(8,128)(2,1)}, u32[]{:S(2)}, u32[]{:S(2)}) collective-permute-start(bf16[128,1024]{1,0:T(8,128)(2,1)S(1)} %collective-permute-done), channel_id=1, source_target_pairs={{0,64},{32,480},{64,128},{96,32},{128,192},{160,96},{192,256},{224... | collective-permute-start | bytes 786440 | tf_op jit(solution)/shard_map/ppermute | solution.py:214
  35.4 8.7 %collective-permute-start.6 = (bf16[128,1024]{1,0:T(8,128)(2,1)S(1)}, bf16[128,1024]{1,0:T(8,128)(2,1)S(1)}, u32[]{:S(2)}, u32[]{:S(2)}) collective-permute-start(bf16[128,1024]{1,0:T(8,128)(2,1)S(1)} %collective-permute-done.5), channel_id=1, source_target_pairs={{0,64},{32,480},{64,128},{96,32},{128,192},{160,96},{192,256},{224... | collective-permute-start | bytes 786440 | tf_op jit(solution)/shard_map/ppermute | solution.py:214
  38.8 10.0 %collective-permute-start.2 = (bf16[128,1024]{1,0:T(8,128)(2,1)}, bf16[128,1024]{1,0:T(8,128)(2,1)}, u32[]{:S(2)}, u32[]{:S(2)}) collective-permute-start(bf16[128,1024]{1,0:T(8,128)(2,1)} %collective-permute-done.1), channel_id=1, source_target_pairs={{0,64},{32,480},{64,128},{96,32},{128,192},{160,96},{192,256},{224... | collective-permute-start | bytes 786440 | tf_op jit(solution)/shard_map/ppermute | solution.py:214
  44.1 9.6 %collective-permute-start.7 = (bf16[128,1024]{1,0:T(8,128)(2,1)S(1)}, bf16[128,1024]{1,0:T(8,128)(2,1)}, u32[]{:S(2)}, u32[]{:S(2)}) collective-permute-start(bf16[128,1024]{1,0:T(8,128)(2,1)S(1)} %collective-permute-done.6), channel_id=1, source_target_pairs={{0,64},{32,480},{64,128},{96,32},{128,192},{160,96},{192,256},{224... | collective-permute-start | bytes 786440 | tf_op jit(solution)/shard_map/ppermute | solution.py:214
  48.8 7.4 %collective-permute-start.3 = (bf16[128,1024]{1,0:T(8,128)(2,1)}, bf16[128,1024]{1,0:T(8,128)(2,1)S(1)}, u32[]{:S(2)}, u32[]{:S(2)}) collective-permute-start(bf16[128,1024]{1,0:T(8,128)(2,1)} %collective-permute-done.2), channel_id=1, source_target_pairs={{0,64},{32,480},{64,128},{96,32},{128,192},{160,96},{192,256},{224... | collective-permute-start | bytes 786440 | tf_op jit(solution)/shard_map/ppermute | solution.py:214
  56.2 11.7 %collective-permute-start.8 = (bf16[768,1024]{1,0:T(8,128)(2,1)S(1)}, bf16[768,1024]{1,0:T(8,128)(2,1)S(1)}, u32[]{:S(2)}, u32[]{:S(2)}) collective-permute-start(bf16[768,1024]{1,0:T(8,128)(2,1)S(1)} %constant_dynamic-update-slice_fusion.refs_4_), channel_id=1, source_target_pairs={{0,32},{32,0},{64,96},{96,64},{128,160},{160,128},{192,224},{224,1... | collective-permute-start | bytes 4718600 | tf_op jit(solution)/shard_map/ppermute | solution.py:214
  63.7 3.4 %collective-permute-start.9 = (bf16[128,1024]{1,0:T(8,128)(2,1)S(1)}, bf16[128,1024]{1,0:T(8,128)(2,1)S(1)}, u32[]{:S(2)}, u32[]{:S(2)}) collective-permute-start(bf16[128,1024]{1,0:T(8,128)(2,1)S(1)} %collective-permute-done.3.refs_3_.refs_6_), channel_id=1, source_target_pairs={{0,32},{32,0},{64,96},{96,64},{128,160},{160,128},{192,224},{224,1... | collective-permute-start | bytes 786440 | tf_op jit(solution)/shard_map/ppermute | solution.py:214
  67.9 20.1 %copy-start.2 = (f32[512]{0:T(512)S(1)}, f32[512]{0:T(512)}, u32[]{:S(2)}) copy-start(f32[512]{0:T(512)} %param.9) | copy-start | bytes 6148
  88.0 16.4 %copy-start.1 = (f32[2048]{0:T(1024)S(1)}, f32[2048]{0:T(1024)}, u32[]{:S(2)}) copy-start(f32[2048]{0:T(1024)} %param.10) | copy-start | bytes 24580
  161.8 1.0 copy-start
  162.8 34.8 %all-to-all-start.7 = ((bf16[32,16,1152]{2,1,0:T(8,128)(2,1)}), bf16[32,16,1152]{2,1,0:T(8,128)(2,1)S(1)}, u32[]{:S(2)}, u32[]{:S(2)}) async-start(bf16[32,16,1152]{2,1,0:T(8,128)(2,1)} %bitcast.16), calls=%async_computation.7 | async-start | bytes 2359296 | tf_op jit(solution)/shard_map/all_to_all | solution.py:205

commit v8 on v7

--- a/solution.py
+++ b/solution.py
@@ -15,6 +15,8 @@
 MIB = 1 << 20
 CHIPS, CORES = 8, 2
 CHUNK = 256
+COSTS = 3
+TOTALS = 8
 
 
 def nt_dot(a, b):
@@ -115,9 +117,11 @@
 
 
 def target_kernel(parts_ref, mass_ref, *refs):
-    *cost_refs, pot_ref, part_ref, wide, held, mine = refs
+    *refs, part_ref, wide, held, mine = refs
+    cost_refs, pot_refs = refs[:COSTS], refs[COSTS:]
     pot = combine(mass_ref, parts_ref)
-    pot_ref[...] = pot
+    for pot_ref in pot_refs:
+        pot_ref[...] = pot
     for s in range(pot.shape[0]):
         wide[s * BLK : (s + 1) * BLK, :] = lanes_of(pot[s : s + 1, :])
     for n, (ref, lanes) in enumerate(tiles_of(cost_refs)):
@@ -142,8 +146,11 @@
 
 
 def map_kernel(npiece, parts_ref, mass_ref, fpot_ref, *refs):
-    pieces, (*cost_refs, pot_ref, sums_ref, weight) = refs[:npiece], refs[npiece:]
-    pot_ref[...] = combine(mass_ref, parts_ref)
+    pieces, (*cost_refs, fout_ref, gout_ref, sums, pot_ref, weight) = refs[:npiece], refs[npiece:]
+    pot = combine(mass_ref, parts_ref)
+    pot_ref[...] = pot
+    gout_ref[...] = pot * UNIT
+    fout_ref[...] = fpot_ref[...] * UNIT
     rows = held_rows(pot_ref)
     width = pieces[0].shape[1]
     for s in range(fpot_ref.shape[0]):
@@ -152,6 +159,19 @@
         for n, (ref, lanes) in enumerate(tiles_of(cost_refs)):
             power = jnp.exp2(mine + rows[n] - ref[at, lanes])
             weight[at, n * BLK : (n + 1) * BLK] = power.astype(jnp.bfloat16)
+    peers = sums.shape[0]
+    share = weight.shape[0] // peers
+
+    ones = jnp.ones((weight.shape[1], BLK), jnp.bfloat16)
+    total = jnp.dot(weight[...], ones, preferred_element_type=jnp.float32)
+    top = share * width // BLK
+    for s in range(fpot_ref.shape[0]):
+        tile = jnp.transpose(total[s * BLK : (s + 1) * BLK, :])[:TOTALS, :]
+        high = tile.astype(jnp.bfloat16).astype(jnp.float32)
+        row = lax.broadcasted_iota(jnp.int32, tile.shape, 0)
+        tile = jnp.where(row == 0, high, jnp.where(row == 1, tile - high, 0.0)).astype(jnp.bfloat16)
+        for k in range(s * BLK // share, (s + 1) * BLK // share):
+            sums[k, top : top + TOTALS, :] = tile
     for d in range(0, width, CHUNK):
         part, lane = None, 0
         for piece in pieces:
@@ -159,30 +179,26 @@
             add = jnp.dot(low, piece[:, d : d + CHUNK], preferred_element_type=jnp.float32)
             part = add if part is None else part + add
             lane += piece.shape[0]
-        sums_ref[:, d : d + CHUNK] = part.astype(jnp.bfloat16)
-    ones = jnp.ones((weight.shape[1], BLK), jnp.bfloat16)
-    total = jnp.dot(weight[...], ones, preferred_element_type=jnp.float32)
-    sums_ref[:, width:] = two_pieces(total)
-
-
-def two_pieces(total):
-    high = total.astype(jnp.bfloat16).astype(jnp.float32)
-    lane = lax.broadcasted_iota(jnp.int32, total.shape, 1)
-    return jnp.where(lane == 0, high, total - high).astype(jnp.bfloat16)
-
-
-def add_up(sums_ref):
+        part = part.astype(jnp.bfloat16)
+        top = share * d // BLK
+        for e in range(0, CHUNK, BLK):
+            at = slice(top + share * e // BLK, top + share * (e // BLK + 1))
+            for k in range(peers):
+                sums[k, at, :] = part[k * share : (k + 1) * share, e : e + BLK]
+
+
+def divide_kernel(sums_ref, out_ref, totals):
     sums = sums_ref[0].astype(jnp.float32)
     for k in range(1, sums_ref.shape[0]):
         sums = sums + sums_ref[k].astype(jnp.float32)
-    return sums
-
-
-def divide_kernel(sums_ref, out_ref):
-    width = out_ref.shape[1]
-    sums = add_up(sums_ref)
-    total = sums[:, width : width + 1] + sums[:, width + 1 : width + 2]
-    out_ref[...] = (sums[:, :width] / total).astype(out_ref.dtype)
+    share, width = out_ref.shape
+    top = share * width // BLK
+    totals[...] = lanes_of(sums[top : top + 1, :] + sums[top + 1 : top + 2, :])
+    first = lax.axis_index("col") % (BLK // share) * share
+    total = totals[pl.ds(pl.multiple_of(first, share), share), :]
+    for d in range(width // BLK):
+        block = sums[d * share : (d + 1) * share, :] / total
+        out_ref[:, d * BLK : (d + 1) * BLK] = block.astype(out_ref.dtype)
 
 
 def call(kernel, shapes, scratch, args, limit, specs=None):
@@ -294,15 +310,16 @@
     pieces = (own, joined, other, last, last_other)
 
     for step in range(ITERS):
-        fpot, part = call(
+        last_step = step == ITERS - 1
+        *fpot, part = call(
             target_kernel,
-            (shape(nsrc, BLK), shape(rows, ntgt, BLK)),
+            (shape(nsrc, BLK),) * last_step + (shape(rows, ntgt, BLK),),
             [pltpu.VMEM((src.shape[0], BLK), jnp.float32)] + [pltpu.VMEM((ntgt, BLK), jnp.float32)] * 2,
             (spread(part, "col"), amass, *cost),
             12,
         )
         parts = spread(part, "row")
-        if step < ITERS - 1:
+        if not last_step:
             part = call(
                 source_kernel,
                 shape(cols, nsrc, BLK),
@@ -310,17 +327,23 @@
                 (parts, bmass, *cost),
                 12,
             )
-    gpot, sums = call(
+    (fpot,) = fpot
+    share = src.shape[0] // cols
+    packed = shape(cols, share * width // BLK + TOTALS, BLK, dtype=jnp.bfloat16)
+    fout, gout, sums = call(
         lambda *refs: map_kernel(len(pieces), *refs),
-        (shape(ntgt, BLK), shape(src.shape[0], width + BLK, dtype=jnp.bfloat16)),
-        [pltpu.VMEM((src.shape[0], ntgt * BLK), jnp.bfloat16)],
+        (shape(nsrc, BLK), shape(ntgt, BLK), packed),
+        [
+            pltpu.VMEM((ntgt, BLK), jnp.float32),
+            pltpu.VMEM((src.shape[0], ntgt * BLK), jnp.bfloat16),
+        ],
         (parts, bmass, fpot, *pieces, *cost),
-        32,
+        24,
     )
-    share = src.shape[0] // cols
-    sums = spread(sums.reshape(cols, share, -1), "col")
-    mapped = call(divide_kernel, shape(share, width, dtype=jnp.bfloat16), [], (sums,), 8)
-    return (fpot.reshape(-1) * UNIT, gpot.reshape(-1) * UNIT, mapped)
+    sums = spread(sums, "col")
+    totals = [pltpu.VMEM((BLK, BLK), jnp.float32)]
+    mapped = call(divide_kernel, shape(share, width, dtype=jnp.bfloat16), totals, (sums,), 8)
+    return (fout.reshape(-1), gout.reshape(-1), mapped)
 
 
 def solution(mesh):

time: 200 us -> 199 us (level)
  blocking collectives: 82.8 us -> 118 us
  waiting for transfers between devices: 33.9 us -> 4.25 us
  starting transfers between devices: 58.1 us -> 54 us
    all_to_all x6 -> x7, blocking collectives: 82.8 us -> 118 us  [spread(): return lax.all_to_all(x, axis, 0, 0, tiled=True)]
    all_to_all x2 -> x1, waiting for transfers between devices: 29.7 us -> 0.01 us  [spread(): return lax.all_to_all(x, axis, 0, 0, tiled=True)]
    all_to_all x2 -> x1, starting transfers between devices: 14.6 us -> 10.6 us  [spread(): return lax.all_to_all(x, axis, 0, 0, tiled=True)]
  transfers between devices with their start and end apart: 12 -> 11, of which waited for: 4 -> 3; matrix products, arithmetic and copies ran while one was open for 2% -> 2% of each run, Pallas kernels for 2% -> 2%
where the time goes in v8:
time: 199 us; the launch traced here: 198 us
  blocking collectives  118 us (59%)
  starting transfers between devices  54 us (27%)
  Pallas kernels  14.9 us (7%)
  local copies, waits for them, and re-layouts  4.96 us (2%)
  waiting for transfers between devices  4.25 us (2%)
    all_to_all x7, blocking collectives, spread(): return lax.all_to_all(x, axis, 0, 0, tiled=True)  118 us
    ppermute x10, starting transfers between devices, move(): return lax.ppermute(x, 'row', pairs)  43.4 us
    pallas_call x11, Pallas kernels, call(): pl.pallas_call(kernel, out_shape=shapes, in_specs=specs or [vmem] * len(a...  14.9 us
    all_to_all x1, starting transfers between devices, spread(): return lax.all_to_all(x, axis, 0, 0, tiled=True)  10.6 us
    ppermute x10, waiting for transfers between devices, move(): return lax.ppermute(x, 'row', pairs)  4.25 us
  transfers between devices with their start and end apart: 11, of which 3 were waited for; matrix products, arithmetic and copies ran while one was open for 2% of the time, Pallas kernels for 2%

profile of v8, /device:TPU:1, one launch (start us, length us, event | category | flops | bytes accessed | tf_op | source)
XLA Modules:
  0.0 197.7 jit_solution(18277142436627429931)
XLA Ops:
  0.6 1.9 broadcast_in_dim.2
  2.6 10.6 %all-to-all-start = ((bf16[32,16,1024]{2,1,0:T(8,128)(2,1)}), bf16[32,16,1024]{2,1,0:T(8,128)(2,1)S(1)}, u32[]{:S(2)}, u32[]{:S(2)}) async-start(bf16[32,16,1024]{2,1,0:T(8,128)(2,1)} %broadcast_in_dim.2), calls=%async_computation | async-start | bytes 2097152 | tf_op jit(solution)/shard_map/all_to_all | solution.py:221
  13.2 2.9 %collective-permute-start.4 = (bf16[128,1024]{1,0:T(8,128)(2,1)S(1)}, bf16[128,1024]{1,0:T(8,128)(2,1)S(1)}, u32[]{:S(2)}, u32[]{:S(2)}) collective-permute-start(bf16[128,1024]{1,0:T(8,128)(2,1)S(1)} %copy-done.4), channel_id=1, source_target_pairs={{0,32},{32,0},{64,96},{96,64},{128,160},{160,128},{192,224},{224,1... | collective-permute-start | bytes 786440 | tf_op jit(solution)/shard_map/ppermute | solution.py:230
  16.1 10.7 %collective-permute-start = (bf16[128,1024]{1,0:T(8,128)(2,1)S(1)}, bf16[128,1024]{1,0:T(8,128)(2,1)S(1)}, u32[]{:S(2)}, u32[]{:S(2)}) collective-permute-start(bf16[128,1024]{1,0:T(8,128)(2,1)S(1)} %copy-done.4), channel_id=1, source_target_pairs={{0,64},{32,480},{64,128},{96,32},{128,192},{160,96},{192,256},{224... | collective-permute-start | bytes 786440 | tf_op jit(solution)/shard_map/ppermute | solution.py:230
  26.8 2.2 %collective-permute-start.5 = (bf16[128,1024]{1,0:T(8,128)(2,1)S(1)}, bf16[128,1024]{1,0:T(8,128)(2,1)S(1)}, u32[]{:S(2)}, u32[]{:S(2)}) collective-permute-start(bf16[128,1024]{1,0:T(8,128)(2,1)S(1)} %collective-permute-done.4), channel_id=1, source_target_pairs={{0,64},{32,480},{64,128},{96,32},{128,192},{160,96},{192,256},{224... | collective-permute-start | bytes 786440 | tf_op jit(solution)/shard_map/ppermute | solution.py:230
  29.0 1.1 collective-permute-done
  30.1 5.3 %collective-permute-start.1 = (bf16[128,1024]{1,0:T(8,128)(2,1)S(1)}, bf16[128,1024]{1,0:T(8,128)(2,1)}, u32[]{:S(2)}, u32[]{:S(2)}) collective-permute-start(bf16[128,1024]{1,0:T(8,128)(2,1)S(1)} %collective-permute-done), channel_id=1, source_target_pairs={{0,64},{32,480},{64,128},{96,32},{128,192},{160,96},{192,256},{224... | collective-permute-start | bytes 786440 | tf_op jit(solution)/shard_map/ppermute | solution.py:230
  35.4 2.8 %collective-permute-start.6 = (bf16[128,1024]{1,0:T(8,128)(2,1)S(1)}, bf16[128,1024]{1,0:T(8,128)(2,1)S(1)}, u32[]{:S(2)}, u32[]{:S(2)}) collective-permute-start(bf16[128,1024]{1,0:T(8,128)(2,1)S(1)} %collective-permute-done.5), channel_id=1, source_target_pairs={{0,64},{32,480},{64,128},{96,32},{128,192},{160,96},{192,256},{224... | collective-permute-start | bytes 786440 | tf_op jit(solution)/shard_map/ppermute | solution.py:230
  38.8 5.1 %collective-permute-start.2 = (bf16[128,1024]{1,0:T(8,128)(2,1)}, bf16[128,1024]{1,0:T(8,128)(2,1)}, u32[]{:S(2)}, u32[]{:S(2)}) collective-permute-start(bf16[128,1024]{1,0:T(8,128)(2,1)} %collective-permute-done.1), channel_id=1, source_target_pairs={{0,64},{32,480},{64,128},{96,32},{128,192},{160,96},{192,256},{224... | collective-permute-start | bytes 786440 | tf_op jit(solution)/shard_map/ppermute | solution.py:230
  44.0 2.7 %collective-permute-start.7 = (bf16[128,1024]{1,0:T(8,128)(2,1)S(1)}, bf16[128,1024]{1,0:T(8,128)(2,1)}, u32[]{:S(2)}, u32[]{:S(2)}) collective-permute-start(bf16[128,1024]{1,0:T(8,128)(2,1)S(1)} %collective-permute-done.6), channel_id=1, source_target_pairs={{0,64},{32,480},{64,128},{96,32},{128,192},{160,96},{192,256},{224... | collective-permute-start | bytes 786440 | tf_op jit(solution)/shard_map/ppermute | solution.py:230
  47.8 1.1 shard_map.94
  48.9 3.7 %collective-permute-start.3 = (bf16[128,1024]{1,0:T(8,128)(2,1)}, bf16[128,1024]{1,0:T(8,128)(2,1)S(1)}, u32[]{:S(2)}, u32[]{:S(2)}) collective-permute-start(bf16[128,1024]{1,0:T(8,128)(2,1)} %collective-permute-done.2), channel_id=1, source_target_pairs={{0,64},{32,480},{64,128},{96,32},{128,192},{160,96},{192,256},{224... | collective-permute-start | bytes 786440 | tf_op jit(solution)/shard_map/ppermute | solution.py:230
  52.6 1.0 constant_dynamic-update-slice_fusion.1
  54.6 1.6 collective-permute-done.3.refs_3_.refs_6_
  56.3 6.1 %collective-permute-start.8 = (bf16[768,1024]{1,0:T(8,128)(2,1)S(1)}, bf16[768,1024]{1,0:T(8,128)(2,1)S(1)}, u32[]{:S(2)}, u32[]{:S(2)}) collective-permute-start(bf16[768,1024]{1,0:T(8,128)(2,1)S(1)} %constant_dynamic-update-slice_fusion.refs_4_), channel_id=1, source_target_pairs={{0,32},{32,0},{64,96},{96,64},{128,160},{160,128},{192,224},{224,1... | collective-permute-start | bytes 4718600 | tf_op jit(solution)/shard_map/ppermute | solution.py:230
  62.4 1.3 shard_map.95.refs_4_.refs_0_.refs_8_
  63.7 1.9 collective-permute-start.9
  65.7 1.5 collective-permute-done.9.refs_4_.refs_7_
  67.9 2.0 %shard_map.97 = (f32[512,768]{1,0:T(8,128)S(1)}, f32[32,4,128]{2,1,0:T(4,128)S(1)}) custom-call(bf16[512,1024]{1,0:T(8,128)(2,1)S(1)} %bitcast.12, f32[512,128]{1,0:T(8,128)S(1)} %get-tuple-element.19.refs_1_, f32[64,128]{1,0:T(8,128)S(1)} %get-tuple-element.20.refs_2_, bf16[768,1024]{1,0:T(8,128)(2,1)S(1)} %collective-permute-done.8.refs_3_.refs_5_, ...), custom_call_target="tpu_custom_call" | custom-call | tf_op jit(solution)/shard_map/pallas_call | solution.py:206
  69.9 18.2 %all_to_all.40.parts_ref = f32[32,4,128]{2,1,0:T(4,128)S(1)} all-to-all(f32[32,4,128]{2,1,0:T(4,128)S(1)} %get-tuple-element.26), channel_id=1, replica_groups=mesh['row'=16,'col'=32] {'col'}, dimensions={0} | all-to-all | bytes 131072 | tf_op jit(solution)/shard_map/all_to_all | solution.py:221
  88.0 1.0 shard_map.98
  89.0 15.0 %all_to_all.41.parts_ref = f32[16,16,128]{2,1,0:T(8,128)S(1)} all-to-all(f32[16,16,128]{2,1,0:T(8,128)S(1)} %shard_map.98), channel_id=1, replica_groups=mesh['row'=16,'col'=32] {'row'}, dimensions={0} | all-to-all | bytes 262144 | tf_op jit(solution)/shard_map/all_to_all | solution.py:221
  104.0 1.0 shard_map.99
  105.0 12.3 %all_to_all.42.parts_ref = f32[32,4,128]{2,1,0:T(4,128)S(1)} all-to-all(f32[32,4,128]{2,1,0:T(4,128)S(1)} %shard_map.99), channel_id=1, replica_groups=mesh['row'=16,'col'=32] {'col'}, dimensions={0} | all-to-all | bytes 131072 | tf_op jit(solution)/shard_map/all_to_all | solution.py:221
  117.3 1.0 shard_map.100
  118.3 12.5 %all_to_all.43.parts_ref = f32[16,16,128]{2,1,0:T(8,128)S(1)} all-to-all(f32[16,16,128]{2,1,0:T(8,128)S(1)} %shard_map.100), channel_id=1, replica_groups=mesh['row'=16,'col'=32] {'row'}, dimensions={0} | all-to-all | bytes 262144 | tf_op jit(solution)/shard_map/all_to_all | solution.py:221
  130.8 1.0 shard_map.101
  131.8 12.3 %all_to_all.44.parts_ref = f32[32,4,128]{2,1,0:T(4,128)S(1)} all-to-all(f32[32,4,128]{2,1,0:T(4,128)S(1)} %shard_map.101), channel_id=1, replica_groups=mesh['row'=16,'col'=32] {'col'}, dimensions={0} | all-to-all | bytes 131072 | tf_op jit(solution)/shard_map/all_to_all | solution.py:221
  144.1 1.0 shard_map.102
  145.1 12.5 %all_to_all.45.refs_0_ = f32[16,16,128]{2,1,0:T(8,128)S(1)} all-to-all(f32[16,16,128]{2,1,0:T(8,128)S(1)} %get-tuple-element.28), channel_id=1, replica_groups=mesh['row'=16,'col'=32] {'row'}, dimensions={0} | all-to-all | bytes 262144 | tf_op jit(solution)/shard_map/all_to_all | solution.py:221
  157.7 4.1 %shard_map.103 = (f32[4,128]{1,0:T(4,128)}, f32[16,128]{1,0:T(8,128)}, bf16[32,136,128]{2,1,0:T(8,128)(2,1)S(1)}) custom-call(f32[16,16,128]{2,1,0:T(8,128)S(1)} %all_to_all.45.refs_0_, f32[16,128]{1,0:T(8,128)S(1)} %bitcast.15, f32[4,128]{1,0:T(4,128)S(1)} %get-tuple-element.29.refs_2_, bf16[256,1024]{1,0:T(8,128)(2,1)S(1)} %constant_dynamic-update-slice_fusion.6.refs_3_, ...), custom_call_target="tpu_custom_call" | custom-call | tf_op jit(solution)/shard_map/pallas_call | solution.py:206
  161.7 35.2 %all_to_all.46.sums_ref = bf16[32,136,128]{2,1,0:T(8,128)(2,1)S(1)} all-to-all(bf16[32,136,128]{2,1,0:T(8,128)(2,1)S(1)} %get-tuple-element.32), channel_id=1, replica_groups=mesh['row'=16,'col'=32] {'col'}, dimensions={0} | all-to-all | bytes 2228224 | tf_op jit(solution)/shard_map/all_to_all | solution.py:221
  (27 shorter events, 3.6 us)
Async XLA Ops:
  0.6 12.6 %copy-start.4 = (bf16[128,1024]{1,0:T(8,128)(2,1)S(1)}, bf16[128,1024]{1,0:T(8,128)(2,1)}, u32[]{:S(2)}) copy-start(bf16[128,1024]{1,0:T(8,128)(2,1)} %param.8) | copy-start | bytes 786436
  2.6 45.2 %copy-start.2 = (s32[1,1,32]{2,1,0:T(1,128)S(1)}, s32[1,1,32]{2,1,0:T(1,128)}, u32[]{:S(2)}) copy-start(s32[1,1,32]{2,1,0:T(1,128)} %param.11) | copy-start | bytes 388
  2.6 45.2 %copy-start.3 = (s32[1,1,32]{2,1,0:T(1,128)S(1)}, s32[1,1,32]{2,1,0:T(1,128)}, u32[]{:S(2)}) copy-start(s32[1,1,32]{2,1,0:T(1,128)} %param.12) | copy-start | bytes 388
  2.6 45.2 %all-to-all-start = ((bf16[32,16,1024]{2,1,0:T(8,128)(2,1)}), bf16[32,16,1024]{2,1,0:T(8,128)(2,1)S(1)}, u32[]{:S(2)}, u32[]{:S(2)}) async-start(bf16[32,16,1024]{2,1,0:T(8,128)(2,1)} %broadcast_in_dim.2), calls=%async_computation | async-start | bytes 2097152 | tf_op jit(solution)/shard_map/all_to_all | solution.py:221
  13.2 13.6 %collective-permute-start.4 = (bf16[128,1024]{1,0:T(8,128)(2,1)S(1)}, bf16[128,1024]{1,0:T(8,128)(2,1)S(1)}, u32[]{:S(2)}, u32[]{:S(2)}) collective-permute-start(bf16[128,1024]{1,0:T(8,128)(2,1)S(1)} %copy-done.4), channel_id=1, source_target_pairs={{0,32},{32,0},{64,96},{96,64},{128,160},{160,128},{192,224},{224,1... | collective-permute-start | bytes 786440 | tf_op jit(solution)/shard_map/ppermute | solution.py:230
  16.1 14.0 %collective-permute-start = (bf16[128,1024]{1,0:T(8,128)(2,1)S(1)}, bf16[128,1024]{1,0:T(8,128)(2,1)S(1)}, u32[]{:S(2)}, u32[]{:S(2)}) collective-permute-start(bf16[128,1024]{1,0:T(8,128)(2,1)S(1)} %copy-done.4), channel_id=1, source_target_pairs={{0,64},{32,480},{64,128},{96,32},{128,192},{160,96},{192,256},{224... | collective-permute-start | bytes 786440 | tf_op jit(solution)/shard_map/ppermute | solution.py:230
  26.8 8.6 %collective-permute-start.5 = (bf16[128,1024]{1,0:T(8,128)(2,1)S(1)}, bf16[128,1024]{1,0:T(8,128)(2,1)S(1)}, u32[]{:S(2)}, u32[]{:S(2)}) collective-permute-start(bf16[128,1024]{1,0:T(8,128)(2,1)S(1)} %collective-permute-done.4), channel_id=1, source_target_pairs={{0,64},{32,480},{64,128},{96,32},{128,192},{160,96},{192,256},{224... | collective-permute-start | bytes 786440 | tf_op jit(solution)/shard_map/ppermute | solution.py:230
  30.1 8.8 %collective-permute-start.1 = (bf16[128,1024]{1,0:T(8,128)(2,1)S(1)}, bf16[128,1024]{1,0:T(8,128)(2,1)}, u32[]{:S(2)}, u32[]{:S(2)}) collective-permute-start(bf16[128,1024]{1,0:T(8,128)(2,1)S(1)} %collective-permute-done), channel_id=1, source_target_pairs={{0,64},{32,480},{64,128},{96,32},{128,192},{160,96},{192,256},{224... | collective-permute-start | bytes 786440 | tf_op jit(solution)/shard_map/ppermute | solution.py:230
  35.4 8.7 %collective-permute-start.6 = (bf16[128,1024]{1,0:T(8,128)(2,1)S(1)}, bf16[128,1024]{1,0:T(8,128)(2,1)S(1)}, u32[]{:S(2)}, u32[]{:S(2)}) collective-permute-start(bf16[128,1024]{1,0:T(8,128)(2,1)S(1)} %collective-permute-done.5), channel_id=1, source_target_pairs={{0,64},{32,480},{64,128},{96,32},{128,192},{160,96},{192,256},{224... | collective-permute-start | bytes 786440 | tf_op jit(solution)/shard_map/ppermute | solution.py:230
  38.8 10.1 %collective-permute-start.2 = (bf16[128,1024]{1,0:T(8,128)(2,1)}, bf16[128,1024]{1,0:T(8,128)(2,1)}, u32[]{:S(2)}, u32[]{:S(2)}) collective-permute-start(bf16[128,1024]{1,0:T(8,128)(2,1)} %collective-permute-done.1), channel_id=1, source_target_pairs={{0,64},{32,480},{64,128},{96,32},{128,192},{160,96},{192,256},{224... | collective-permute-start | bytes 786440 | tf_op jit(solution)/shard_map/ppermute | solution.py:230
  44.0 9.6 %collective-permute-start.7 = (bf16[128,1024]{1,0:T(8,128)(2,1)S(1)}, bf16[128,1024]{1,0:T(8,128)(2,1)}, u32[]{:S(2)}, u32[]{:S(2)}) collective-permute-start(bf16[128,1024]{1,0:T(8,128)(2,1)S(1)} %collective-permute-done.6), channel_id=1, source_target_pairs={{0,64},{32,480},{64,128},{96,32},{128,192},{160,96},{192,256},{224... | collective-permute-start | bytes 786440 | tf_op jit(solution)/shard_map/ppermute | solution.py:230
  48.9 7.3 %collective-permute-start.3 = (bf16[128,1024]{1,0:T(8,128)(2,1)}, bf16[128,1024]{1,0:T(8,128)(2,1)S(1)}, u32[]{:S(2)}, u32[]{:S(2)}) collective-permute-start(bf16[128,1024]{1,0:T(8,128)(2,1)} %collective-permute-done.2), channel_id=1, source_target_pairs={{0,64},{32,480},{64,128},{96,32},{128,192},{160,96},{192,256},{224... | collective-permute-start | bytes 786440 | tf_op jit(solution)/shard_map/ppermute | solution.py:230
  56.3 11.6 %collective-permute-start.8 = (bf16[768,1024]{1,0:T(8,128)(2,1)S(1)}, bf16[768,1024]{1,0:T(8,128)(2,1)S(1)}, u32[]{:S(2)}, u32[]{:S(2)}) collective-permute-start(bf16[768,1024]{1,0:T(8,128)(2,1)S(1)} %constant_dynamic-update-slice_fusion.refs_4_), channel_id=1, source_target_pairs={{0,32},{32,0},{64,96},{96,64},{128,160},{160,128},{192,224},{224,1... | collective-permute-start | bytes 4718600 | tf_op jit(solution)/shard_map/ppermute | solution.py:230
  63.7 3.4 %collective-permute-start.9 = (bf16[128,1024]{1,0:T(8,128)(2,1)S(1)}, bf16[128,1024]{1,0:T(8,128)(2,1)S(1)}, u32[]{:S(2)}, u32[]{:S(2)}) collective-permute-start(bf16[128,1024]{1,0:T(8,128)(2,1)S(1)} %collective-permute-done.3.refs_3_.refs_6_), channel_id=1, source_target_pairs={{0,32},{32,0},{64,96},{96,64},{128,160},{160,128},{192,224},{224,1... | collective-permute-start | bytes 786440 | tf_op jit(solution)/shard_map/ppermute | solution.py:230
  67.9 20.2 %copy-start.1 = (f32[512]{0:T(512)S(1)}, f32[512]{0:T(512)}, u32[]{:S(2)}) copy-start(f32[512]{0:T(512)} %param.9) | copy-start | bytes 6148
  88.0 16.0 %copy-start = (f32[2048]{0:T(1024)S(1)}, f32[2048]{0:T(1024)}, u32[]{:S(2)}) copy-start(f32[2048]{0:T(1024)} %param.10) | copy-start | bytes 24580

commit v9 on v8

--- a/solution.py
+++ b/solution.py
@@ -289,8 +289,6 @@
     last = ring(three)
     own = jnp.concatenate([target, near])
     joined = jnp.concatenate([one, near_one, two, near_two, three, near_three])
-    last, turn = lax.optimization_barrier((last, joined))
-    other = partner(turn)
 
     def costs(first, some, held=(), outs=()):
         return call(
@@ -302,7 +300,8 @@
         )
 
     (cost_a,) = costs(0, (own, joined))
-    last, cost_a = lax.optimization_barrier((last, cost_a))
+    last, turn, cost_a = lax.optimization_barrier((last, joined, cost_a))
+    other = partner(turn)
     last_other = partner(last)
     (cost_c,) = costs(14, (last, last_other))
     cost_b, part = costs(8, (other,), (cost_a, cost_c), (shape(cols, nsrc, BLK),))

time: 199 us -> 197 us (0.990)
  transfers between devices with their start and end apart: 11 -> 11, of which waited for: 3 -> 4; matrix products, arithmetic and copies ran while one was open for 2% -> 2% of each run, Pallas kernels for 2% -> 2%
where the time goes in v9:
time: 197 us; the launch traced here: 196 us
  blocking collectives  118 us (60%)
  starting transfers between devices  53.4 us (27%)
  Pallas kernels  14.9 us (8%)
  local copies, waits for them, and re-layouts  4.97 us (3%)
  waiting for transfers between devices  3.33 us (2%)
    all_to_all x7, blocking collectives, spread(): return lax.all_to_all(x, axis, 0, 0, tiled=True)  118 us
    ppermute x10, starting transfers between devices, move(): return lax.ppermute(x, 'row', pairs)  42.9 us
    pallas_call x11, Pallas kernels, call(): pl.pallas_call(kernel, out_shape=shapes, in_specs=specs or [vmem] * len(a...  14.9 us
    all_to_all x1, starting transfers between devices, spread(): return lax.all_to_all(x, axis, 0, 0, tiled=True)  10.5 us
  transfers between devices with their start and end apart: 11, of which 4 were waited for; matrix products, arithmetic and copies ran while one was open for 2% of the time, Pallas kernels for 2%

profile of v9, /device:TPU:1, one launch (start us, length us, event | category | flops | bytes accessed | tf_op | source)
XLA Modules:
  0.0 196.4 jit_solution(17062396886877047437)
XLA Ops:
  0.6 1.9 broadcast_in_dim.2
  2.6 10.5 %all-to-all-start = ((bf16[32,16,1024]{2,1,0:T(8,128)(2,1)}), bf16[32,16,1024]{2,1,0:T(8,128)(2,1)S(1)}, u32[]{:S(2)}, u32[]{:S(2)}) async-start(bf16[32,16,1024]{2,1,0:T(8,128)(2,1)} %broadcast_in_dim.2), calls=%async_computation | async-start | bytes 2097152 | tf_op jit(solution)/shard_map/all_to_all | solution.py:221
  13.1 2.9 %collective-permute-start.4 = (bf16[128,1024]{1,0:T(8,128)(2,1)S(1)}, bf16[128,1024]{1,0:T(8,128)(2,1)S(1)}, u32[]{:S(2)}, u32[]{:S(2)}) collective-permute-start(bf16[128,1024]{1,0:T(8,128)(2,1)S(1)} %copy-done.4), channel_id=1, source_target_pairs={{0,32},{32,0},{64,96},{96,64},{128,160},{160,128},{192,224},{224,1... | collective-permute-start | bytes 786440 | tf_op jit(solution)/shard_map/ppermute | solution.py:230
  16.0 10.7 %collective-permute-start = (bf16[128,1024]{1,0:T(8,128)(2,1)S(1)}, bf16[128,1024]{1,0:T(8,128)(2,1)S(1)}, u32[]{:S(2)}, u32[]{:S(2)}) collective-permute-start(bf16[128,1024]{1,0:T(8,128)(2,1)S(1)} %copy-done.4), channel_id=1, source_target_pairs={{0,64},{32,480},{64,128},{96,32},{128,192},{160,96},{192,256},{224... | collective-permute-start | bytes 786440 | tf_op jit(solution)/shard_map/ppermute | solution.py:230
  26.7 2.2 %collective-permute-start.5 = (bf16[128,1024]{1,0:T(8,128)(2,1)S(1)}, bf16[128,1024]{1,0:T(8,128)(2,1)S(1)}, u32[]{:S(2)}, u32[]{:S(2)}) collective-permute-start(bf16[128,1024]{1,0:T(8,128)(2,1)S(1)} %collective-permute-done.4), channel_id=1, source_target_pairs={{0,64},{32,480},{64,128},{96,32},{128,192},{160,96},{192,256},{224... | collective-permute-start | bytes 786440 | tf_op jit(solution)/shard_map/ppermute | solution.py:230
  28.8 1.1 collective-permute-done
  29.9 5.3 %collective-permute-start.1 = (bf16[128,1024]{1,0:T(8,128)(2,1)S(1)}, bf16[128,1024]{1,0:T(8,128)(2,1)}, u32[]{:S(2)}, u32[]{:S(2)}) collective-permute-start(bf16[128,1024]{1,0:T(8,128)(2,1)S(1)} %collective-permute-done), channel_id=1, source_target_pairs={{0,64},{32,480},{64,128},{96,32},{128,192},{160,96},{192,256},{224... | collective-permute-start | bytes 786440 | tf_op jit(solution)/shard_map/ppermute | solution.py:230
  35.9 2.1 %collective-permute-start.6 = (bf16[128,1024]{1,0:T(8,128)(2,1)S(1)}, bf16[128,1024]{1,0:T(8,128)(2,1)S(1)}, u32[]{:S(2)}, u32[]{:S(2)}) collective-permute-start(bf16[128,1024]{1,0:T(8,128)(2,1)S(1)} %collective-permute-done.5), channel_id=1, source_target_pairs={{0,64},{32,480},{64,128},{96,32},{128,192},{160,96},{192,256},{224... | collective-permute-start | bytes 786440 | tf_op jit(solution)/shard_map/ppermute | solution.py:230
  38.6 5.3 %collective-permute-start.2 = (bf16[128,1024]{1,0:T(8,128)(2,1)}, bf16[128,1024]{1,0:T(8,128)(2,1)}, u32[]{:S(2)}, u32[]{:S(2)}) collective-permute-start(bf16[128,1024]{1,0:T(8,128)(2,1)} %collective-permute-done.1), channel_id=1, source_target_pairs={{0,64},{32,480},{64,128},{96,32},{128,192},{160,96},{192,256},{224... | collective-permute-start | bytes 786440 | tf_op jit(solution)/shard_map/ppermute | solution.py:230
  43.9 2.7 %collective-permute-start.7 = (bf16[128,1024]{1,0:T(8,128)(2,1)S(1)}, bf16[128,1024]{1,0:T(8,128)(2,1)}, u32[]{:S(2)}, u32[]{:S(2)}) collective-permute-start(bf16[128,1024]{1,0:T(8,128)(2,1)S(1)} %collective-permute-done.6), channel_id=1, source_target_pairs={{0,64},{32,480},{64,128},{96,32},{128,192},{160,96},{192,256},{224... | collective-permute-start | bytes 786440 | tf_op jit(solution)/shard_map/ppermute | solution.py:230
  46.7 1.0 constant_dynamic-update-slice_fusion.3
  47.7 1.1 shard_map.94
  48.8 3.7 %collective-permute-start.3 = (bf16[128,1024]{1,0:T(8,128)(2,1)}, bf16[128,1024]{1,0:T(8,128)(2,1)S(1)}, u32[]{:S(2)}, u32[]{:S(2)}) collective-permute-start(bf16[128,1024]{1,0:T(8,128)(2,1)} %collective-permute-done.2), channel_id=1, source_target_pairs={{0,64},{32,480},{64,128},{96,32},{128,192},{160,96},{192,256},{224... | collective-permute-start | bytes 786440 | tf_op jit(solution)/shard_map/ppermute | solution.py:230
  52.5 1.0 constant_dynamic-update-slice_fusion.1
  54.5 1.3 shard_map.95.refs_4_.refs_0_.refs_8_
  56.1 6.1 %collective-permute-start.8 = (bf16[768,1024]{1,0:T(8,128)(2,1)S(1)}, bf16[768,1024]{1,0:T(8,128)(2,1)S(1)}, u32[]{:S(2)}, u32[]{:S(2)}) collective-permute-start(bf16[768,1024]{1,0:T(8,128)(2,1)S(1)} %constant_dynamic-update-slice_fusion.refs_4_), channel_id=1, source_target_pairs={{0,32},{32,0},{64,96},{96,64},{128,160},{160,128},{192,224},{224,1... | collective-permute-start | bytes 4718600 | tf_op jit(solution)/shard_map/ppermute | solution.py:230
  62.2 1.9 collective-permute-start.9
  64.1 1.5 collective-permute-done.9.refs_4_.refs_7_
  66.4 2.0 %shard_map.97 = (f32[512,768]{1,0:T(8,128)S(1)}, f32[32,4,128]{2,1,0:T(4,128)S(1)}) custom-call(bf16[512,1024]{1,0:T(8,128)(2,1)S(1)} %bitcast.12, f32[512,128]{1,0:T(8,128)S(1)} %get-tuple-element.18.refs_1_, f32[64,128]{1,0:T(8,128)S(1)} %get-tuple-element.19.refs_2_, bf16[768,1024]{1,0:T(8,128)(2,1)S(1)} %collective-permute-done.8.refs_3_.refs_5_, ...), custom_call_target="tpu_custom_call" | custom-call | tf_op jit(solution)/shard_map/pallas_call | solution.py:206
  68.4 18.1 %all_to_all.40.parts_ref = f32[32,4,128]{2,1,0:T(4,128)S(1)} all-to-all(f32[32,4,128]{2,1,0:T(4,128)S(1)} %get-tuple-element.24), channel_id=1, replica_groups=mesh['row'=16,'col'=32] {'col'}, dimensions={0} | all-to-all | bytes 131072 | tf_op jit(solution)/shard_map/all_to_all | solution.py:221
  86.5 1.0 shard_map.98
  87.5 15.2 %all_to_all.41.parts_ref = f32[16,16,128]{2,1,0:T(8,128)S(1)} all-to-all(f32[16,16,128]{2,1,0:T(8,128)S(1)} %shard_map.98), channel_id=1, replica_groups=mesh['row'=16,'col'=32] {'row'}, dimensions={0} | all-to-all | bytes 262144 | tf_op jit(solution)/shard_map/all_to_all | solution.py:221
  102.7 1.0 shard_map.99
  103.7 12.3 %all_to_all.42.parts_ref = f32[32,4,128]{2,1,0:T(4,128)S(1)} all-to-all(f32[32,4,128]{2,1,0:T(4,128)S(1)} %shard_map.99), channel_id=1, replica_groups=mesh['row'=16,'col'=32] {'col'}, dimensions={0} | all-to-all | bytes 131072 | tf_op jit(solution)/shard_map/all_to_all | solution.py:221
  116.0 1.0 shard_map.100
  117.0 12.5 %all_to_all.43.parts_ref = f32[16,16,128]{2,1,0:T(8,128)S(1)} all-to-all(f32[16,16,128]{2,1,0:T(8,128)S(1)} %shard_map.100), channel_id=1, replica_groups=mesh['row'=16,'col'=32] {'row'}, dimensions={0} | all-to-all | bytes 262144 | tf_op jit(solution)/shard_map/all_to_all | solution.py:221
  129.5 1.0 shard_map.101
  130.5 12.3 %all_to_all.44.parts_ref = f32[32,4,128]{2,1,0:T(4,128)S(1)} all-to-all(f32[32,4,128]{2,1,0:T(4,128)S(1)} %shard_map.101), channel_id=1, replica_groups=mesh['row'=16,'col'=32] {'col'}, dimensions={0} | all-to-all | bytes 131072 | tf_op jit(solution)/shard_map/all_to_all | solution.py:221
  142.8 1.0 shard_map.102
  143.8 12.5 %all_to_all.45.refs_0_ = f32[16,16,128]{2,1,0:T(8,128)S(1)} all-to-all(f32[16,16,128]{2,1,0:T(8,128)S(1)} %get-tuple-element.26), channel_id=1, replica_groups=mesh['row'=16,'col'=32] {'row'}, dimensions={0} | all-to-all | bytes 262144 | tf_op jit(solution)/shard_map/all_to_all | solution.py:221
  156.3 4.1 %shard_map.103 = (f32[4,128]{1,0:T(4,128)}, f32[16,128]{1,0:T(8,128)}, bf16[32,136,128]{2,1,0:T(8,128)(2,1)S(1)}) custom-call(f32[16,16,128]{2,1,0:T(8,128)S(1)} %all_to_all.45.refs_0_, f32[16,128]{1,0:T(8,128)S(1)} %bitcast.15, f32[4,128]{1,0:T(4,128)S(1)} %get-tuple-element.27.refs_2_, bf16[256,1024]{1,0:T(8,128)(2,1)S(1)} %constant_dynamic-update-slice_fusion.6.refs_3_, ...), custom_call_target="tpu_custom_call" | custom-call | tf_op jit(solution)/shard_map/pallas_call | solution.py:206
  160.4 35.2 %all_to_all.46.sums_ref = bf16[32,136,128]{2,1,0:T(8,128)(2,1)S(1)} all-to-all(bf16[32,136,128]{2,1,0:T(8,128)(2,1)S(1)} %get-tuple-element.30), channel_id=1, replica_groups=mesh['row'=16,'col'=32] {'col'}, dimensions={0} | all-to-all | bytes 2228224 | tf_op jit(solution)/shard_map/all_to_all | solution.py:221
  (27 shorter events, 3.3 us)
Async XLA Ops:
  0.6 12.4 %copy-start.4 = (bf16[128,1024]{1,0:T(8,128)(2,1)S(1)}, bf16[128,1024]{1,0:T(8,128)(2,1)}, u32[]{:S(2)}) copy-start(bf16[128,1024]{1,0:T(8,128)(2,1)} %param.8) | copy-start | bytes 786436
  2.6 45.1 %all-to-all-start = ((bf16[32,16,1024]{2,1,0:T(8,128)(2,1)}), bf16[32,16,1024]{2,1,0:T(8,128)(2,1)S(1)}, u32[]{:S(2)}, u32[]{:S(2)}) async-start(bf16[32,16,1024]{2,1,0:T(8,128)(2,1)} %broadcast_in_dim.2), calls=%async_computation | async-start | bytes 2097152 | tf_op jit(solution)/shard_map/all_to_all | solution.py:221
  13.1 34.6 %copy-start.2 = (s32[1,1,32]{2,1,0:T(1,128)S(1)}, s32[1,1,32]{2,1,0:T(1,128)}, u32[]{:S(2)}) copy-start(s32[1,1,32]{2,1,0:T(1,128)} %param.11) | copy-start | bytes 388
  13.1 34.6 %copy-start.3 = (s32[1,1,32]{2,1,0:T(1,128)S(1)}, s32[1,1,32]{2,1,0:T(1,128)}, u32[]{:S(2)}) copy-start(s32[1,1,32]{2,1,0:T(1,128)} %param.12) | copy-start | bytes 388
  13.1 13.6 %collective-permute-start.4 = (bf16[128,1024]{1,0:T(8,128)(2,1)S(1)}, bf16[128,1024]{1,0:T(8,128)(2,1)S(1)}, u32[]{:S(2)}, u32[]{:S(2)}) collective-permute-start(bf16[128,1024]{1,0:T(8,128)(2,1)S(1)} %copy-done.4), channel_id=1, source_target_pairs={{0,32},{32,0},{64,96},{96,64},{128,160},{160,128},{192,224},{224,1... | collective-permute-start | bytes 786440 | tf_op jit(solution)/shard_map/ppermute | solution.py:230
  16.0 14.0 %collective-permute-start = (bf16[128,1024]{1,0:T(8,128)(2,1)S(1)}, bf16[128,1024]{1,0:T(8,128)(2,1)S(1)}, u32[]{:S(2)}, u32[]{:S(2)}) collective-permute-start(bf16[128,1024]{1,0:T(8,128)(2,1)S(1)} %copy-done.4), channel_id=1, source_target_pairs={{0,64},{32,480},{64,128},{96,32},{128,192},{160,96},{192,256},{224... | collective-permute-start | bytes 786440 | tf_op jit(solution)/shard_map/ppermute | solution.py:230
  26.7 9.3 %collective-permute-start.5 = (bf16[128,1024]{1,0:T(8,128)(2,1)S(1)}, bf16[128,1024]{1,0:T(8,128)(2,1)S(1)}, u32[]{:S(2)}, u32[]{:S(2)}) collective-permute-start(bf16[128,1024]{1,0:T(8,128)(2,1)S(1)} %collective-permute-done.4), channel_id=1, source_target_pairs={{0,64},{32,480},{64,128},{96,32},{128,192},{160,96},{192,256},{224... | collective-permute-start | bytes 786440 | tf_op jit(solution)/shard_map/ppermute | solution.py:230
  29.9 8.6 %collective-permute-start.1 = (bf16[128,1024]{1,0:T(8,128)(2,1)S(1)}, bf16[128,1024]{1,0:T(8,128)(2,1)}, u32[]{:S(2)}, u32[]{:S(2)}) collective-permute-start(bf16[128,1024]{1,0:T(8,128)(2,1)S(1)} %collective-permute-done), channel_id=1, source_target_pairs={{0,64},{32,480},{64,128},{96,32},{128,192},{160,96},{192,256},{224... | collective-permute-start | bytes 786440 | tf_op jit(solution)/shard_map/ppermute | solution.py:230
  35.9 8.0 %collective-permute-start.6 = (bf16[128,1024]{1,0:T(8,128)(2,1)S(1)}, bf16[128,1024]{1,0:T(8,128)(2,1)S(1)}, u32[]{:S(2)}, u32[]{:S(2)}) collective-permute-start(bf16[128,1024]{1,0:T(8,128)(2,1)S(1)} %collective-permute-done.5), channel_id=1, source_target_pairs={{0,64},{32,480},{64,128},{96,32},{128,192},{160,96},{192,256},{224... | collective-permute-start | bytes 786440 | tf_op jit(solution)/shard_map/ppermute | solution.py:230
  38.6 10.2 %collective-permute-start.2 = (bf16[128,1024]{1,0:T(8,128)(2,1)}, bf16[128,1024]{1,0:T(8,128)(2,1)}, u32[]{:S(2)}, u32[]{:S(2)}) collective-permute-start(bf16[128,1024]{1,0:T(8,128)(2,1)} %collective-permute-done.1), channel_id=1, source_target_pairs={{0,64},{32,480},{64,128},{96,32},{128,192},{160,96},{192,256},{224... | collective-permute-start | bytes 786440 | tf_op jit(solution)/shard_map/ppermute | solution.py:230
  43.9 9.6 %collective-permute-start.7 = (bf16[128,1024]{1,0:T(8,128)(2,1)S(1)}, bf16[128,1024]{1,0:T(8,128)(2,1)}, u32[]{:S(2)}, u32[]{:S(2)}) collective-permute-start(bf16[128,1024]{1,0:T(8,128)(2,1)S(1)} %collective-permute-done.6), channel_id=1, source_target_pairs={{0,64},{32,480},{64,128},{96,32},{128,192},{160,96},{192,256},{224... | collective-permute-start | bytes 786440 | tf_op jit(solution)/shard_map/ppermute | solution.py:230
  48.8 7.4 %collective-permute-start.3 = (bf16[128,1024]{1,0:T(8,128)(2,1)}, bf16[128,1024]{1,0:T(8,128)(2,1)S(1)}, u32[]{:S(2)}, u32[]{:S(2)}) collective-permute-start(bf16[128,1024]{1,0:T(8,128)(2,1)} %collective-permute-done.2), channel_id=1, source_target_pairs={{0,64},{32,480},{64,128},{96,32},{128,192},{160,96},{192,256},{224... | collective-permute-start | bytes 786440 | tf_op jit(solution)/shard_map/ppermute | solution.py:230
  56.1 10.3 %collective-permute-start.8 = (bf16[768,1024]{1,0:T(8,128)(2,1)S(1)}, bf16[768,1024]{1,0:T(8,128)(2,1)S(1)}, u32[]{:S(2)}, u32[]{:S(2)}) collective-permute-start(bf16[768,1024]{1,0:T(8,128)(2,1)S(1)} %constant_dynamic-update-slice_fusion.refs_4_), channel_id=1, source_target_pairs={{0,32},{32,0},{64,96},{96,64},{128,160},{160,128},{192,224},{224,1... | collective-permute-start | bytes 4718600 | tf_op jit(solution)/shard_map/ppermute | solution.py:230
  62.2 3.4 %collective-permute-start.9 = (bf16[128,1024]{1,0:T(8,128)(2,1)S(1)}, bf16[128,1024]{1,0:T(8,128)(2,1)S(1)}, u32[]{:S(2)}, u32[]{:S(2)}) collective-permute-start(bf16[128,1024]{1,0:T(8,128)(2,1)S(1)} %collective-permute-done.3.refs_3_.refs_6_), channel_id=1, source_target_pairs={{0,32},{32,0},{64,96},{96,64},{128,160},{160,128},{192,224},{224,1... | collective-permute-start | bytes 786440 | tf_op jit(solution)/shard_map/ppermute | solution.py:230
  66.4 20.1 %copy-start.1 = (f32[512]{0:T(512)S(1)}, f32[512]{0:T(512)}, u32[]{:S(2)}) copy-start(f32[512]{0:T(512)} %param.9) | copy-start | bytes 6148
  86.5 16.2 %copy-start = (f32[2048]{0:T(1024)S(1)}, f32[2048]{0:T(1024)}, u32[]{:S(2)}) copy-start(f32[2048]{0:T(1024)} %param.10) | copy-start | bytes 24580

commit v10 on v9

--- a/solution.py
+++ b/solution.py
@@ -285,7 +285,7 @@
     )
 
     three, near_three = ring(two), ring(near_two)
-    three, norm = lax.optimization_barrier((three, norm))
+    near_three, norm = lax.optimization_barrier((near_three, norm))
     last = ring(three)
     own = jnp.concatenate([target, near])
     joined = jnp.concatenate([one, near_one, two, near_two, three, near_three])

time: 197 us -> 197 us (level)
  no operation moved by 1% of the time
where the time goes in v10:
time: 197 us; the launch traced here: 196 us
  blocking collectives  118 us (60%)
  starting transfers between devices  52.9 us (27%)
  Pallas kernels  14.9 us (8%)
  local copies, waits for them, and re-layouts  4.95 us (3%)
  waiting for transfers between devices  3.53 us (2%)
    all_to_all x7, blocking collectives, spread(): return lax.all_to_all(x, axis, 0, 0, tiled=True)  118 us
    ppermute x10, starting transfers between devices, move(): return lax.ppermute(x, 'row', pairs)  42.4 us
    pallas_call x11, Pallas kernels, call(): pl.pallas_call(kernel, out_shape=shapes, in_specs=specs or [vmem] * len(a...  14.9 us
    all_to_all x1, starting transfers between devices, spread(): return lax.all_to_all(x, axis, 0, 0, tiled=True)  10.5 us
  transfers between devices with their start and end apart: 11, of which 4 were waited for; matrix products, arithmetic and copies ran while one was open for 2% of the time, Pallas kernels for 2%

profile of v10, /device:TPU:1, one launch (start us, length us, event | category | flops | bytes accessed | tf_op | source)
XLA Modules:
  0.0 196.0 jit_solution(6959653670712516722)
XLA Ops:
  0.6 1.9 broadcast_in_dim.2
  2.6 10.5 %all-to-all-start = ((bf16[32,16,1024]{2,1,0:T(8,128)(2,1)}), bf16[32,16,1024]{2,1,0:T(8,128)(2,1)S(1)}, u32[]{:S(2)}, u32[]{:S(2)}) async-start(bf16[32,16,1024]{2,1,0:T(8,128)(2,1)} %broadcast_in_dim.2), calls=%async_computation | async-start | bytes 2097152 | tf_op jit(solution)/shard_map/all_to_all | solution.py:221
  13.1 2.9 %collective-permute-start = (bf16[128,1024]{1,0:T(8,128)(2,1)S(1)}, bf16[128,1024]{1,0:T(8,128)(2,1)S(1)}, u32[]{:S(2)}, u32[]{:S(2)}) collective-permute-start(bf16[128,1024]{1,0:T(8,128)(2,1)S(1)} %copy-done.4), channel_id=1, source_target_pairs={{0,32},{32,0},{64,96},{96,64},{128,160},{160,128},{192,224},{224,1... | collective-permute-start | bytes 786440 | tf_op jit(solution)/shard_map/ppermute | solution.py:230
  15.9 10.7 %collective-permute-start.4 = (bf16[128,1024]{1,0:T(8,128)(2,1)S(1)}, bf16[128,1024]{1,0:T(8,128)(2,1)S(1)}, u32[]{:S(2)}, u32[]{:S(2)}) collective-permute-start(bf16[128,1024]{1,0:T(8,128)(2,1)S(1)} %copy-done.4), channel_id=1, source_target_pairs={{0,64},{32,480},{64,128},{96,32},{128,192},{160,96},{192,256},{224... | collective-permute-start | bytes 786440 | tf_op jit(solution)/shard_map/ppermute | solution.py:230
  26.6 2.2 %collective-permute-start.1 = (bf16[128,1024]{1,0:T(8,128)(2,1)S(1)}, bf16[128,1024]{1,0:T(8,128)(2,1)S(1)}, u32[]{:S(2)}, u32[]{:S(2)}) collective-permute-start(bf16[128,1024]{1,0:T(8,128)(2,1)S(1)} %collective-permute-done), channel_id=1, source_target_pairs={{0,64},{32,480},{64,128},{96,32},{128,192},{160,96},{192,256},{224... | collective-permute-start | bytes 786440 | tf_op jit(solution)/shard_map/ppermute | solution.py:230
  28.8 1.1 collective-permute-done.4
  29.9 5.3 %collective-permute-start.5 = (bf16[128,1024]{1,0:T(8,128)(2,1)S(1)}, bf16[128,1024]{1,0:T(8,128)(2,1)S(1)}, u32[]{:S(2)}, u32[]{:S(2)}) collective-permute-start(bf16[128,1024]{1,0:T(8,128)(2,1)S(1)} %collective-permute-done.4), channel_id=1, source_target_pairs={{0,64},{32,480},{64,128},{96,32},{128,192},{160,96},{192,256},{224... | collective-permute-start | bytes 786440 | tf_op jit(solution)/shard_map/ppermute | solution.py:230
  35.9 2.1 %collective-permute-start.2 = (bf16[128,1024]{1,0:T(8,128)(2,1)S(1)}, bf16[128,1024]{1,0:T(8,128)(2,1)}, u32[]{:S(2)}, u32[]{:S(2)}) collective-permute-start(bf16[128,1024]{1,0:T(8,128)(2,1)S(1)} %collective-permute-done.1), channel_id=1, source_target_pairs={{0,64},{32,480},{64,128},{96,32},{128,192},{160,96},{192,256},{224... | collective-permute-start | bytes 786440 | tf_op jit(solution)/shard_map/ppermute | solution.py:230
  38.5 5.3 %collective-permute-start.6 = (bf16[128,1024]{1,0:T(8,128)(2,1)S(1)}, bf16[128,1024]{1,0:T(8,128)(2,1)}, u32[]{:S(2)}, u32[]{:S(2)}) collective-permute-start(bf16[128,1024]{1,0:T(8,128)(2,1)S(1)} %collective-permute-done.5), channel_id=1, source_target_pairs={{0,64},{32,480},{64,128},{96,32},{128,192},{160,96},{192,256},{224... | collective-permute-start | bytes 786440 | tf_op jit(solution)/shard_map/ppermute | solution.py:230
  43.9 2.7 %collective-permute-start.3 = (bf16[128,1024]{1,0:T(8,128)(2,1)}, bf16[128,1024]{1,0:T(8,128)(2,1)}, u32[]{:S(2)}, u32[]{:S(2)}) collective-permute-start(bf16[128,1024]{1,0:T(8,128)(2,1)} %collective-permute-done.2), channel_id=1, source_target_pairs={{0,64},{32,480},{64,128},{96,32},{128,192},{160,96},{192,256},{224... | collective-permute-start | bytes 786440 | tf_op jit(solution)/shard_map/ppermute | solution.py:230
  47.1 5.2 %collective-permute-start.7 = (bf16[128,1024]{1,0:T(8,128)(2,1)}, bf16[128,1024]{1,0:T(8,128)(2,1)S(1)}, u32[]{:S(2)}, u32[]{:S(2)}) collective-permute-start(bf16[128,1024]{1,0:T(8,128)(2,1)} %collective-permute-done.6), channel_id=1, source_target_pairs={{0,64},{32,480},{64,128},{96,32},{128,192},{160,96},{192,256},{224... | collective-permute-start | bytes 786440 | tf_op jit(solution)/shard_map/ppermute | solution.py:230
  52.4 1.0 constant_dynamic-update-slice_fusion.2
  54.3 1.1 shard_map.94
  55.4 1.0 constant_dynamic-update-slice_fusion.refs_4_
  56.4 1.3 shard_map.95.refs_4_.refs_0_.refs_8_
  57.8 4.1 %collective-permute-start.8 = (bf16[768,1024]{1,0:T(8,128)(2,1)S(1)}, bf16[768,1024]{1,0:T(8,128)(2,1)S(1)}, u32[]{:S(2)}, u32[]{:S(2)}) collective-permute-start(bf16[768,1024]{1,0:T(8,128)(2,1)S(1)} %constant_dynamic-update-slice_fusion.refs_4_), channel_id=1, source_target_pairs={{0,32},{32,0},{64,96},{96,64},{128,160},{160,128},{192,224},{224,1... | collective-permute-start | bytes 4718600 | tf_op jit(solution)/shard_map/ppermute | solution.py:230
  61.9 1.9 collective-permute-start.9
  63.8 1.5 collective-permute-done.9.refs_4_.refs_7_
  66.0 2.0 %shard_map.97 = (f32[512,768]{1,0:T(8,128)S(1)}, f32[32,4,128]{2,1,0:T(4,128)S(1)}) custom-call(bf16[512,1024]{1,0:T(8,128)(2,1)S(1)} %bitcast.12, f32[512,128]{1,0:T(8,128)S(1)} %get-tuple-element.18.refs_1_, f32[64,128]{1,0:T(8,128)S(1)} %get-tuple-element.19.refs_2_, bf16[768,1024]{1,0:T(8,128)(2,1)S(1)} %collective-permute-done.8.refs_3_.refs_5_, ...), custom_call_target="tpu_custom_call" | custom-call | tf_op jit(solution)/shard_map/pallas_call | solution.py:206
  68.0 18.1 %all_to_all.40.parts_ref = f32[32,4,128]{2,1,0:T(4,128)S(1)} all-to-all(f32[32,4,128]{2,1,0:T(4,128)S(1)} %get-tuple-element.24), channel_id=1, replica_groups=mesh['row'=16,'col'=32] {'col'}, dimensions={0} | all-to-all | bytes 131072 | tf_op jit(solution)/shard_map/all_to_all | solution.py:221
  86.1 1.0 shard_map.98
  87.1 15.2 %all_to_all.41.parts_ref = f32[16,16,128]{2,1,0:T(8,128)S(1)} all-to-all(f32[16,16,128]{2,1,0:T(8,128)S(1)} %shard_map.98), channel_id=1, replica_groups=mesh['row'=16,'col'=32] {'row'}, dimensions={0} | all-to-all | bytes 262144 | tf_op jit(solution)/shard_map/all_to_all | solution.py:221
  102.3 1.0 shard_map.99
  103.3 12.3 %all_to_all.42.parts_ref = f32[32,4,128]{2,1,0:T(4,128)S(1)} all-to-all(f32[32,4,128]{2,1,0:T(4,128)S(1)} %shard_map.99), channel_id=1, replica_groups=mesh['row'=16,'col'=32] {'col'}, dimensions={0} | all-to-all | bytes 131072 | tf_op jit(solution)/shard_map/all_to_all | solution.py:221
  115.6 1.0 shard_map.100
  116.6 12.5 %all_to_all.43.parts_ref = f32[16,16,128]{2,1,0:T(8,128)S(1)} all-to-all(f32[16,16,128]{2,1,0:T(8,128)S(1)} %shard_map.100), channel_id=1, replica_groups=mesh['row'=16,'col'=32] {'row'}, dimensions={0} | all-to-all | bytes 262144 | tf_op jit(solution)/shard_map/all_to_all | solution.py:221
  129.2 1.0 shard_map.101
  130.1 12.3 %all_to_all.44.parts_ref = f32[32,4,128]{2,1,0:T(4,128)S(1)} all-to-all(f32[32,4,128]{2,1,0:T(4,128)S(1)} %shard_map.101), channel_id=1, replica_groups=mesh['row'=16,'col'=32] {'col'}, dimensions={0} | all-to-all | bytes 131072 | tf_op jit(solution)/shard_map/all_to_all | solution.py:221
  142.4 1.0 shard_map.102
  143.4 12.5 %all_to_all.45.refs_0_ = f32[16,16,128]{2,1,0:T(8,128)S(1)} all-to-all(f32[16,16,128]{2,1,0:T(8,128)S(1)} %get-tuple-element.26), channel_id=1, replica_groups=mesh['row'=16,'col'=32] {'row'}, dimensions={0} | all-to-all | bytes 262144 | tf_op jit(solution)/shard_map/all_to_all | solution.py:221
  156.0 4.1 %shard_map.103 = (f32[4,128]{1,0:T(4,128)}, f32[16,128]{1,0:T(8,128)}, bf16[32,136,128]{2,1,0:T(8,128)(2,1)S(1)}) custom-call(f32[16,16,128]{2,1,0:T(8,128)S(1)} %all_to_all.45.refs_0_, f32[16,128]{1,0:T(8,128)S(1)} %bitcast.15, f32[4,128]{1,0:T(4,128)S(1)} %get-tuple-element.27.refs_2_, bf16[256,1024]{1,0:T(8,128)(2,1)S(1)} %constant_dynamic-update-slice_fusion.6.refs_3_, ...), custom_call_target="tpu_custom_call" | custom-call | tf_op jit(solution)/shard_map/pallas_call | solution.py:206
  160.1 35.2 %all_to_all.46.sums_ref = bf16[32,136,128]{2,1,0:T(8,128)(2,1)S(1)} all-to-all(bf16[32,136,128]{2,1,0:T(8,128)(2,1)S(1)} %get-tuple-element.30), channel_id=1, replica_groups=mesh['row'=16,'col'=32] {'col'}, dimensions={0} | all-to-all | bytes 2228224 | tf_op jit(solution)/shard_map/all_to_all | solution.py:221
  (27 shorter events, 3.5 us)
Async XLA Ops:
  0.6 12.4 %copy-start.4 = (bf16[128,1024]{1,0:T(8,128)(2,1)S(1)}, bf16[128,1024]{1,0:T(8,128)(2,1)}, u32[]{:S(2)}) copy-start(bf16[128,1024]{1,0:T(8,128)(2,1)} %param.8) | copy-start | bytes 786436
  2.6 51.8 %all-to-all-start = ((bf16[32,16,1024]{2,1,0:T(8,128)(2,1)}), bf16[32,16,1024]{2,1,0:T(8,128)(2,1)S(1)}, u32[]{:S(2)}, u32[]{:S(2)}) async-start(bf16[32,16,1024]{2,1,0:T(8,128)(2,1)} %broadcast_in_dim.2), calls=%async_computation | async-start | bytes 2097152 | tf_op jit(solution)/shard_map/all_to_all | solution.py:221
  13.1 13.6 %collective-permute-start = (bf16[128,1024]{1,0:T(8,128)(2,1)S(1)}, bf16[128,1024]{1,0:T(8,128)(2,1)S(1)}, u32[]{:S(2)}, u32[]{:S(2)}) collective-permute-start(bf16[128,1024]{1,0:T(8,128)(2,1)S(1)} %copy-done.4), channel_id=1, source_target_pairs={{0,32},{32,0},{64,96},{96,64},{128,160},{160,128},{192,224},{224,1... | collective-permute-start | bytes 786440 | tf_op jit(solution)/shard_map/ppermute | solution.py:230
  15.9 14.0 %collective-permute-start.4 = (bf16[128,1024]{1,0:T(8,128)(2,1)S(1)}, bf16[128,1024]{1,0:T(8,128)(2,1)S(1)}, u32[]{:S(2)}, u32[]{:S(2)}) collective-permute-start(bf16[128,1024]{1,0:T(8,128)(2,1)S(1)} %copy-done.4), channel_id=1, source_target_pairs={{0,64},{32,480},{64,128},{96,32},{128,192},{160,96},{192,256},{224... | collective-permute-start | bytes 786440 | tf_op jit(solution)/shard_map/ppermute | solution.py:230
  26.6 9.3 %collective-permute-start.1 = (bf16[128,1024]{1,0:T(8,128)(2,1)S(1)}, bf16[128,1024]{1,0:T(8,128)(2,1)S(1)}, u32[]{:S(2)}, u32[]{:S(2)}) collective-permute-start(bf16[128,1024]{1,0:T(8,128)(2,1)S(1)} %collective-permute-done), channel_id=1, source_target_pairs={{0,64},{32,480},{64,128},{96,32},{128,192},{160,96},{192,256},{224... | collective-permute-start | bytes 786440 | tf_op jit(solution)/shard_map/ppermute | solution.py:230
  29.9 8.6 %collective-permute-start.5 = (bf16[128,1024]{1,0:T(8,128)(2,1)S(1)}, bf16[128,1024]{1,0:T(8,128)(2,1)S(1)}, u32[]{:S(2)}, u32[]{:S(2)}) collective-permute-start(bf16[128,1024]{1,0:T(8,128)(2,1)S(1)} %collective-permute-done.4), channel_id=1, source_target_pairs={{0,64},{32,480},{64,128},{96,32},{128,192},{160,96},{192,256},{224... | collective-permute-start | bytes 786440 | tf_op jit(solution)/shard_map/ppermute | solution.py:230
  35.9 18.4 %copy-start.2 = (s32[1,1,32]{2,1,0:T(1,128)S(1)}, s32[1,1,32]{2,1,0:T(1,128)}, u32[]{:S(2)}) copy-start(s32[1,1,32]{2,1,0:T(1,128)} %param.11) | copy-start | bytes 388
  35.9 18.4 %copy-start.3 = (s32[1,1,32]{2,1,0:T(1,128)S(1)}, s32[1,1,32]{2,1,0:T(1,128)}, u32[]{:S(2)}) copy-start(s32[1,1,32]{2,1,0:T(1,128)} %param.12) | copy-start | bytes 388
  35.9 8.0 %collective-permute-start.2 = (bf16[128,1024]{1,0:T(8,128)(2,1)S(1)}, bf16[128,1024]{1,0:T(8,128)(2,1)}, u32[]{:S(2)}, u32[]{:S(2)}) collective-permute-start(bf16[128,1024]{1,0:T(8,128)(2,1)S(1)} %collective-permute-done.1), channel_id=1, source_target_pairs={{0,64},{32,480},{64,128},{96,32},{128,192},{160,96},{192,256},{224... | collective-permute-start | bytes 786440 | tf_op jit(solution)/shard_map/ppermute | solution.py:230
  38.5 8.6 %collective-permute-start.6 = (bf16[128,1024]{1,0:T(8,128)(2,1)S(1)}, bf16[128,1024]{1,0:T(8,128)(2,1)}, u32[]{:S(2)}, u32[]{:S(2)}) collective-permute-start(bf16[128,1024]{1,0:T(8,128)(2,1)S(1)} %collective-permute-done.5), channel_id=1, source_target_pairs={{0,64},{32,480},{64,128},{96,32},{128,192},{160,96},{192,256},{224... | collective-permute-start | bytes 786440 | tf_op jit(solution)/shard_map/ppermute | solution.py:230
  43.9 11.5 %collective-permute-start.3 = (bf16[128,1024]{1,0:T(8,128)(2,1)}, bf16[128,1024]{1,0:T(8,128)(2,1)}, u32[]{:S(2)}, u32[]{:S(2)}) collective-permute-start(bf16[128,1024]{1,0:T(8,128)(2,1)} %collective-permute-done.2), channel_id=1, source_target_pairs={{0,64},{32,480},{64,128},{96,32},{128,192},{160,96},{192,256},{224... | collective-permute-start | bytes 786440 | tf_op jit(solution)/shard_map/ppermute | solution.py:230
  47.1 10.6 %collective-permute-start.7 = (bf16[128,1024]{1,0:T(8,128)(2,1)}, bf16[128,1024]{1,0:T(8,128)(2,1)S(1)}, u32[]{:S(2)}, u32[]{:S(2)}) collective-permute-start(bf16[128,1024]{1,0:T(8,128)(2,1)} %collective-permute-done.6), channel_id=1, source_target_pairs={{0,64},{32,480},{64,128},{96,32},{128,192},{160,96},{192,256},{224... | collective-permute-start | bytes 786440 | tf_op jit(solution)/shard_map/ppermute | solution.py:230
  57.8 8.2 %collective-permute-start.8 = (bf16[768,1024]{1,0:T(8,128)(2,1)S(1)}, bf16[768,1024]{1,0:T(8,128)(2,1)S(1)}, u32[]{:S(2)}, u32[]{:S(2)}) collective-permute-start(bf16[768,1024]{1,0:T(8,128)(2,1)S(1)} %constant_dynamic-update-slice_fusion.refs_4_), channel_id=1, source_target_pairs={{0,32},{32,0},{64,96},{96,64},{128,160},{160,128},{192,224},{224,1... | collective-permute-start | bytes 4718600 | tf_op jit(solution)/shard_map/ppermute | solution.py:230
  61.9 3.4 %collective-permute-start.9 = (bf16[128,1024]{1,0:T(8,128)(2,1)S(1)}, bf16[128,1024]{1,0:T(8,128)(2,1)S(1)}, u32[]{:S(2)}, u32[]{:S(2)}) collective-permute-start(bf16[128,1024]{1,0:T(8,128)(2,1)S(1)} %collective-permute-done.7.refs_3_.refs_6_), channel_id=1, source_target_pairs={{0,32},{32,0},{64,96},{96,64},{128,160},{160,128},{192,224},{224,1... | collective-permute-start | bytes 786440 | tf_op jit(solution)/shard_map/ppermute | solution.py:230
  66.0 20.1 %copy-start.1 = (f32[512]{0:T(512)S(1)}, f32[512]{0:T(512)}, u32[]{:S(2)}) copy-start(f32[512]{0:T(512)} %param.9) | copy-start | bytes 6148
  86.1 16.2 %copy-start = (f32[2048]{0:T(1024)S(1)}, f32[2048]{0:T(1024)}, u32[]{:S(2)}) copy-start(f32[2048]{0:T(1024)} %param.10) | copy-start | bytes 24580
